TPU v7x, 32 devices: a whole 2x2x4 slice. The times are simulated.
32 devices in a mesh: seq: 8 (over z, y), own: 4 (over x, core).
Axes of the slice: x: 2, y: 2, z: 4, core: 2. Of those that a mesh axis runs over, the one named last changes fastest.
Arguments:
- tokens: bfloat16 [4, 8192, 768], P('own', 'seq')
- cotangent: bfloat16 [4, 8192, 768], P('own', 'seq'), may hold values from -6 to 6
- lengths: int32 [4, 10], P('own'), may hold values from 512 to 2048, as said below
- offsets: int32 [4, 10], P('own'), may hold values from 0 to 1536, as said below
- valid_count: int32 [4, 10], P('own'), may hold values from 257 to 2048, as said below
- weights: float32 [768, 96, 96], P(('seq', 'own'))
- stat_left: float32 [768, 96, 96], P(('seq', 'own')), as said below
- stat_right: float32 [768, 96, 96], P(('seq', 'own')), as said below
- root_left: float32 [768, 96, 96], P(('seq', 'own')), as said below
- root_right: float32 [768, 96, 96], P(('seq', 'own')), as said below
- projection: float32 [2048, 256], P('own'), may hold values from -0.125 to 0.125
- projection_left: float32 [8, 256, 256], P('own'), as said below
- projection_right: float32 [8, 256, 256], P('own'), as said below
- projection_root_left: float32 [8, 256, 256], P('own'), as said below
- projection_root_right: float32 [8, 256, 256], P('own'), as said below
- norm_params: float32 [4, 768], replicated
- norm_stat: float32 [4, 768], replicated, as said below
Outputs:
- output: bfloat16 [4, 8192, 768], P('own', 'seq')
- grad_input: float32 [4, 8192, 768], P('own', 'seq')
- weight_grad: float32 [768, 96, 96], P(('seq', 'own'))
- stat_left_new: float32 [768, 96, 96], P(('seq', 'own'))
- stat_right_new: float32 [768, 96, 96], P(('seq', 'own'))
- weights_new: float32 [768, 96, 96], P(('seq', 'own'))
- projection_grad: float32 [2048, 256], P('own')
- projection_left_new: float32 [8, 256, 256], P('own')
- projection_right_new: float32 [8, 256, 256], P('own')
- projection_new: float32 [2048, 256], P('own')
- norm_grad: float32 [4, 768], replicated
- norm_stat_new: float32 [4, 768], replicated
- norm_new: float32 [4, 768], replicated
- residual_rms: float32 [2], replicated
Inputs may be any that keep to these rules, and one draw needn't show every extreme that they name: `lengths`: each pack holds exactly 2 items of 2048 tokens and 8 of 512, in a drawn order, filling the pack. `offsets`: offset plus length is at most 2048; items of 2048 tokens have offset 0; in each pack some item of 512 tokens ends at position 2048. `valid_count`: an item's valid count is more than half of its length and at most its length; in each pack some item of 2048 tokens is wholly valid, and some item of 512 tokens has 257 valid tokens. `stat_left`: Symmetric. `stat_right`: Symmetric. `root_left`: Symmetric. `root_right`: Symmetric. `projection_left`: Symmetric. `projection_right`: Symmetric. `projection_root_left`: Symmetric. `projection_root_right`: Symmetric. `norm_stat`: Positive.
All inputs are finite; a program needn't handle non-finite values.
Results may differ from a plain program's by a relative error of at most 0.015.
The roundings to bfloat16 on the way count: a program that leaves them out, or rounds other values in their place, can miss the bound.
Values may be sent and summed in bfloat16 or wider, within the bound.
A program may use at most 448 MiB of HBM per device.

v0:
```python
import math

import jax
import jax.numpy as jnp
from jax import lax
from jax.sharding import PartitionSpec as P

HEADS = 12
FF = 3072
SHORT = 512


eps_norm = 1e-05
decay = 0.5
rate_matrix = 0.2
rate_norm = 0.2
highest = lax.Precision.HIGHEST


def prefix(shard, axis, combine, identity, reverse):
    peers, index = (lax.axis_size(axis), lax.axis_index(axis))
    everything = jax.tree.map(lambda part: lax.all_gather(part, axis), shard)
    start = jax.tree.map(
        lambda part, zero: jnp.broadcast_to(jnp.asarray(zero, part.dtype), part.shape),
        shard,
        identity,
    )

    def hop(k, before):
        at = peers - 1 - k if reverse else k
        reached = at > index if reverse else at < index
        new = combine(before, jax.tree.map(lambda part: part[at], everything))
        return jax.tree.map(lambda a, b: jnp.where(reached, a, b), new, before)

    return lax.fori_loop(0, peers, hop, start)


def entering(shard, axis, join, neutral, backward):
    count = lax.axis_size(axis)
    place = lax.axis_index(axis)
    ahead = count - 1 - place if backward else place
    gathered = jax.tree.map(
        lambda a, kind: lax.all_gather(a.astype(kind), axis), shard, (jnp.bfloat16, jnp.bfloat16)
    )
    state = jax.tree.map(lambda a, e: jnp.zeros_like(a) + jnp.asarray(e, a.dtype), shard, neutral)

    def one(hop, state):
        source = count - 1 - hop if backward else hop
        return join(
            state,
            jax.tree.map(
                lambda a, own: lax.dynamic_index_in_dim(a, source, 0, False).astype(own.dtype),
                gathered,
                shard,
            ),
        )

    return lax.fori_loop(0, ahead, one, state)


def to_matrix(tiles, rows, cols):
    size = tiles.shape[-1]
    return (
        tiles.reshape(rows // size, cols // size, size, size)
        .transpose(0, 2, 1, 3)
        .reshape(rows, cols)
    )


def to_tiles(matrix, size):
    rows, cols = matrix.shape
    return (
        matrix.reshape(rows // size, size, cols // size, size)
        .transpose(0, 2, 1, 3)
        .reshape(-1, size, size)
    )


def segment_combine(earlier, later):
    flag_early, value_early = earlier
    flag_late, value_late = later
    return (
        jnp.maximum(flag_early, flag_late),
        jnp.where(flag_late > 0, value_late, value_early + value_late),
    )


def layer_norm(values, gain, shift):
    mean = jnp.mean(values, axis=-1, keepdims=True)
    centered = values - mean
    inverse = lax.rsqrt(jnp.mean(centered * centered, axis=-1, keepdims=True) + eps_norm)
    normed = centered * inverse
    return (normed * gain + shift, normed, inverse)


def norm_back(grad_out, normed, inverse, gain):
    scaled = grad_out * gain
    return inverse * (
        scaled
        - jnp.mean(scaled, axis=-1, keepdims=True)
        - normed * jnp.mean(scaled * normed, axis=-1, keepdims=True)
    )


def gelu_slope(values):
    cumulative = 0.5 * (1.0 + jax.scipy.special.erf(values * (1.0 / math.sqrt(2.0))))
    density = jnp.exp(-0.5 * values * values) * (1.0 / math.sqrt(2.0 * math.pi))
    return cumulative + values * density


def shampoo(grad, left, right, root_left, root_right, weight):
    new_left = decay * left + (1.0 - decay) * jnp.einsum(
        "tij,tkj->tik", grad, grad, precision=highest
    )
    new_right = decay * right + (1.0 - decay) * jnp.einsum(
        "tji,tjk->tik", grad, grad, precision=highest
    )
    inner = jnp.einsum("tij,tjk->tik", grad, root_right, precision=highest)
    step = jnp.einsum("tij,tjk->tik", root_left, inner, precision=highest)
    return (new_left, new_right, weight - rate_matrix * step)


def contract_rows(left, right):
    return lax.dot_general(
        left, right, (((0,), (0,)), ((), ())), preferred_element_type=jnp.float32
    )


def contract_cols(left, right):
    return lax.dot_general(
        left, right, (((1,), (1,)), ((), ())), preferred_element_type=jnp.float32
    )


def per_device(
    tokens,
    cotangent,
    lengths,
    offsets,
    valid_count,
    weights,
    stat_left,
    stat_right,
    root_left,
    root_right,
    projection,
    projection_left,
    projection_right,
    projection_root_left,
    projection_root_right,
    norm_params,
    norm_stat,
):
    size = weights.shape[-1]
    width = tokens.shape[-1]
    rows_here = tokens.shape[1]
    heads = HEADS
    head = width // heads
    scale = head ** (-0.5)
    kp = projection.shape[1]
    blocks = rows_here // SHORT
    devices = lax.axis_size("seq") * lax.axis_size("own")
    per_dev = weights.shape[0]
    att_dev = 4 * (width // size) ** 2 // devices
    gathered = lax.all_gather(weights.astype(jnp.bfloat16), ("seq", "own"), axis=0, tiled=True)
    grid = gathered.reshape(devices, per_dev, size, size)
    attention = grid[:, :att_dev].reshape(-1, size, size)
    forward_tiles = grid[:, att_dev:].reshape(-1, size, size)
    count_sq = (width // size) ** 2
    count_ff = width // size * (FF // size)
    w_qkv = jnp.concatenate(
        [
            to_matrix(attention[0:count_sq], width, width),
            to_matrix(attention[count_sq : 2 * count_sq], width, width),
            to_matrix(attention[2 * count_sq : 3 * count_sq], width, width),
        ],
        axis=1,
    )
    w_out = to_matrix(attention[3 * count_sq :], width, width)
    w_up = to_matrix(forward_tiles[0:count_ff], width, FF)
    w_down = to_matrix(forward_tiles[count_ff:], FF, width)
    proj_all = lax.all_gather(projection.astype(jnp.bfloat16), "own", axis=0, tiled=True)
    lens = lengths[0]
    offs = offsets[0]
    counts = valid_count[0]
    item_count = lens.shape[0]
    starts = jnp.cumsum(lens) - lens
    row_start = lax.axis_index("seq") * rows_here
    rows = row_start + jnp.arange(rows_here, dtype=jnp.int32)
    item_of = jnp.sum((starts[None, :] <= rows[:, None]).astype(jnp.int32), axis=1) - 1
    item_hot = (item_of[:, None] == jnp.arange(item_count, dtype=jnp.int32)[None, :]).astype(
        jnp.int32
    )
    place = rows - jnp.sum(item_hot * starts[None, :], axis=1)
    keep = place < jnp.sum(item_hot * counts[None, :], axis=1)
    keep_float = keep.astype(jnp.float32)
    column_start = (jnp.sum(item_hot * offs[None, :], axis=1) + place).reshape(blocks, SHORT)[:, 0]
    item_first = item_of[0]
    item_last = item_of[rows_here - 1]
    last_slot = item_last - item_first
    block_slot = item_of.reshape(blocks, SHORT)[:, 0] - item_first
    slot_index = jnp.arange(blocks, dtype=jnp.int32)
    block_hot = (block_slot[:, None] == slot_index[None, :]).astype(jnp.float32)
    start_flag = (starts[item_last] >= row_start).astype(jnp.float32)
    end_flag = (starts[item_first] + lens[item_first] <= row_start + rows_here).astype(jnp.float32)
    from_left = (starts[item_first] < row_start).astype(jnp.float32)
    from_right = (starts[item_last] + lens[item_last] > row_start + rows_here).astype(jnp.float32)
    first_hot = (slot_index == 0).astype(jnp.float32) * from_left
    last_hot = (slot_index == last_slot).astype(jnp.float32) * from_right
    keep_blocks = keep.reshape(blocks, SHORT)
    inputs = tokens[0]
    qkv = jnp.dot(inputs, w_qkv, preferred_element_type=jnp.float32).astype(jnp.bfloat16)
    query = qkv[:, :width].reshape(blocks, SHORT, heads, head)
    keyval = qkv[:, width:].reshape(blocks, SHORT, 2 * width)
    e_rows = jax.vmap(lambda begin: lax.dynamic_slice_in_dim(proj_all, begin, SHORT, 0))(
        column_start
    )
    e_rows = jnp.where(keep_blocks[:, :, None], e_rows, jnp.zeros((), jnp.bfloat16))
    block_partial = jnp.einsum("bsk,bsc->bkc", e_rows, keyval, preferred_element_type=jnp.float32)
    partial_value = jnp.einsum("bn,bkc->nkc", block_hot, block_partial, precision=highest)
    zero_block = jnp.zeros((kp, 2 * width), jnp.float32)
    tail = lax.dynamic_index_in_dim(partial_value, last_slot, 0, keepdims=False)
    left_flag, left_sum = prefix(
        (start_flag, tail), "seq", segment_combine, (jnp.float32(0.0), zero_block), False
    )
    right_flag, right_sum = prefix(
        (end_flag, partial_value[0]), "seq", segment_combine, (jnp.float32(0.0), zero_block), True
    )
    summary = (
        partial_value
        + first_hot[:, None, None] * left_sum[None]
        + last_hot[:, None, None] * right_sum[None]
    ).astype(jnp.bfloat16)
    block_summary = jnp.einsum(
        "bn,nkc->bkc", block_hot, summary.astype(jnp.float32), precision=highest
    ).astype(jnp.bfloat16)
    keys = block_summary[:, :, :width].reshape(blocks, kp, heads, head)
    values = block_summary[:, :, width:].reshape(blocks, kp, heads, head)
    scores = jnp.einsum("bshd,bjhd->bshj", query, keys, preferred_element_type=jnp.float32) * scale
    top = jnp.max(scores, axis=-1, keepdims=True)
    lse = top + jnp.log(jnp.sum(jnp.exp(scores - top), axis=-1, keepdims=True))
    prob_low = jnp.exp(scores - lse).astype(jnp.bfloat16)
    attended = jnp.einsum("bshj,bjhd->bshd", prob_low, values, preferred_element_type=jnp.float32)
    mixed = attended.reshape(rows_here, width).astype(jnp.bfloat16)
    branch = jnp.dot(mixed, w_out, preferred_element_type=jnp.float32)
    first_sum = inputs.astype(jnp.float32) + branch
    first_norm, normed_one, inverse_one = layer_norm(first_sum, norm_params[0], norm_params[1])
    first_low = first_norm.astype(jnp.bfloat16)
    up_value = jnp.dot(first_low, w_up, preferred_element_type=jnp.float32)
    hidden = jax.nn.gelu(up_value, approximate=False).astype(jnp.bfloat16)
    second_sum = first_norm + jnp.dot(hidden, w_down, preferred_element_type=jnp.float32)
    result, normed_two, inverse_two = layer_norm(second_sum, norm_params[2], norm_params[3])
    row_sums = jnp.stack(
        [
            jnp.sum(keep_float[:, None] * first_sum * first_sum),
            jnp.sum(keep_float[:, None] * branch * branch),
            jnp.sum(keep_float),
        ]
    )
    row_totals = lax.psum(row_sums, ("seq", "own"))
    grad_out = cotangent[0].astype(jnp.float32)
    grad_gain_two = jnp.sum(grad_out * normed_two, axis=0)
    grad_shift_two = jnp.sum(grad_out, axis=0)
    grad_second = norm_back(grad_out, normed_two, inverse_two, norm_params[2])
    grad_down_in = grad_second.astype(jnp.bfloat16)
    grad_w_down = contract_rows(hidden, grad_down_in)
    grad_hidden = contract_cols(grad_down_in, w_down)
    grad_up = (grad_hidden * gelu_slope(up_value)).astype(jnp.bfloat16)
    grad_w_up = contract_rows(first_low, grad_up)
    grad_first_norm = grad_second + contract_cols(grad_up, w_up)
    ffn_grad = jnp.concatenate([to_tiles(grad_w_up, size), to_tiles(grad_w_down, size)], axis=0)
    grad_gain_one = jnp.sum(grad_first_norm * normed_one, axis=0)
    grad_shift_one = jnp.sum(grad_first_norm, axis=0)
    grad_first = norm_back(grad_first_norm, normed_one, inverse_one, norm_params[0])
    grad_branch = grad_first.astype(jnp.bfloat16)
    grad_w_out = contract_rows(mixed, grad_branch)
    grad_mixed = (
        contract_cols(grad_branch, w_out).astype(jnp.bfloat16).reshape(blocks, SHORT, heads, head)
    )
    prob = jnp.exp(
        jnp.einsum("bshd,bjhd->bshj", query, keys, preferred_element_type=jnp.float32) * scale - lse
    )
    prob_again = prob.astype(jnp.bfloat16)
    grad_prob = jnp.einsum(
        "bshd,bjhd->bshj", grad_mixed, values, preferred_element_type=jnp.float32
    )
    grad_values = jnp.einsum(
        "bshj,bshd->bjhd", prob_again, grad_mixed, preferred_element_type=jnp.float32
    )
    grad_scores = (prob * (grad_prob - jnp.sum(prob * grad_prob, axis=-1, keepdims=True))).astype(
        jnp.bfloat16
    )
    grad_query = (
        jnp.einsum("bshj,bjhd->bshd", grad_scores, keys, preferred_element_type=jnp.float32) * scale
    )
    grad_keys = (
        jnp.einsum("bshj,bshd->bjhd", grad_scores, query, preferred_element_type=jnp.float32)
        * scale
    )
    grad_blocks = jnp.concatenate(
        [grad_keys.reshape(blocks, kp, width), grad_values.reshape(blocks, kp, width)], axis=2
    )
    grad_parts = jnp.einsum("bn,bkc->nkc", block_hot, grad_blocks, precision=highest)
    grad_tail = lax.dynamic_index_in_dim(grad_parts, last_slot, 0, keepdims=False)
    grad_flag_left, grad_from_left = entering(
        (start_flag, grad_tail), "seq", segment_combine, (jnp.float32(0.0), zero_block), False
    )
    grad_flag_right, grad_from_right = entering(
        (end_flag, grad_parts[0]), "seq", segment_combine, (jnp.float32(0.0), zero_block), True
    )
    grad_summary = (
        grad_parts
        + first_hot[:, None, None] * grad_from_left[None]
        + last_hot[:, None, None] * grad_from_right[None]
    ).astype(jnp.bfloat16)
    grad_block_summary = jnp.einsum(
        "bn,nkc->bkc", block_hot, grad_summary.astype(jnp.float32), precision=highest
    ).astype(jnp.bfloat16)
    grad_keyval = (
        jnp.einsum("bsk,bkc->bsc", e_rows, grad_block_summary, preferred_element_type=jnp.float32)
        .astype(jnp.bfloat16)
        .reshape(rows_here, 2 * width)
    )
    grad_e = jnp.einsum(
        "bsc,bkc->bsk", keyval, grad_block_summary, preferred_element_type=jnp.float32
    ) * keep_blocks[:, :, None].astype(jnp.float32)
    grad_proj = jnp.zeros((proj_all.shape[0], kp), jnp.float32)
    for index in range(blocks):
        current = lax.dynamic_slice_in_dim(grad_proj, column_start[index], SHORT, 0)
        grad_proj = lax.dynamic_update_slice_in_dim(
            grad_proj, current + grad_e[index], column_start[index], 0
        )
    grad_qkv = jnp.concatenate(
        [grad_query.reshape(rows_here, width).astype(jnp.bfloat16), grad_keyval], axis=1
    )
    grad_w_qkv = contract_rows(inputs, grad_qkv)
    grad_input = grad_first + contract_cols(grad_qkv, w_qkv)
    att_grad = jnp.concatenate(
        [
            to_tiles(grad_w_qkv[:, :width], size),
            to_tiles(grad_w_qkv[:, width : 2 * width], size),
            to_tiles(grad_w_qkv[:, 2 * width :], size),
            to_tiles(grad_w_out, size),
        ],
        axis=0,
    )
    stacked = jnp.concatenate(
        [
            att_grad.reshape(devices, att_dev, size, size),
            ffn_grad.reshape(devices, per_dev - att_dev, size, size),
        ],
        axis=1,
    ).reshape(-1, size, size)
    owned = lax.psum_scatter(stacked, ("seq", "own"), scatter_dimension=0, tiled=True)
    norm_terms = jnp.stack([grad_gain_one, grad_shift_one, grad_gain_two, grad_shift_two])
    proj_total, norm_grad = lax.psum((grad_proj, norm_terms), ("seq", "own"))
    residual_rms = jnp.sqrt(row_totals[:2] / (row_totals[2] * width))
    left_new, right_new, weights_new = shampoo(
        owned, stat_left, stat_right, root_left, root_right, weights
    )
    part_rows = projection.shape[0]
    proj_grad = lax.dynamic_slice_in_dim(
        proj_total, lax.axis_index("own") * part_rows, part_rows, 0
    )
    proj_left_new, proj_right_new, proj_blocks = shampoo(
        proj_grad.reshape(-1, kp, kp),
        projection_left,
        projection_right,
        projection_root_left,
        projection_root_right,
        projection.reshape(-1, kp, kp),
    )
    stat_new = decay * norm_stat + (1.0 - decay) * norm_grad * norm_grad
    norm_new = norm_params - rate_norm * norm_grad * lax.rsqrt(stat_new)
    return (
        result.astype(jnp.bfloat16)[None],
        grad_input[None],
        owned,
        left_new,
        right_new,
        weights_new,
        proj_grad,
        proj_left_new,
        proj_right_new,
        proj_blocks.reshape(part_rows, kp),
        norm_grad,
        stat_new,
        norm_new,
        residual_rms,
    )


def solution(mesh):
    in_specs = (
        P("own", "seq", None),
        P("own", "seq", None),
        P("own", None),
        P("own", None),
        P("own", None),
        P(("seq", "own"), None, None),
        P(("seq", "own"), None, None),
        P(("seq", "own"), None, None),
        P(("seq", "own"), None, None),
        P(("seq", "own"), None, None),
        P("own", None),
        P("own", None, None),
        P("own", None, None),
        P("own", None, None),
        P("own", None, None),
        P(),
        P(),
    )
    out_specs = (
        P("own", "seq", None),
        P("own", "seq", None),
        P(("seq", "own"), None, None),
        P(("seq", "own"), None, None),
        P(("seq", "own"), None, None),
        P(("seq", "own"), None, None),
        P("own", None),
        P("own", None, None),
        P("own", None, None),
        P("own", None),
        P(),
        P(),
        P(),
        P(),
    )
    return jax.shard_map(
        per_device, mesh=mesh, in_specs=in_specs, out_specs=out_specs, check_vma=False
    )
```

profile of v0, /device:TPU:9, one launch (start us, length us, event | category | flops | bytes accessed | tf_op | source)
XLA Modules:
  0.0 1549.5 jit_solution(16576937047804058836)
XLA Ops:
  15.6 12.8 all-gather.7.cloned.1.call-done
  30.6 124.2 %all-gather.9.cloned.1.call-done = bf16[768,96,96]{2,1,0:T(8,128)(2,1)} async-done(((bf16[24,96,96]{2,1,0:T(8,128)(2,1)}), bf16[768,96,96]{2,1,0:T(8,128)(2,1)}) %all-gather.9.cloned.1.call-update) | async-done | bytes 14155792 | tf_op jit(solution)/shard_map/all_gather | solution.py:165
  191.4 19.7 %fusion.37 = f32[2,256,1536]{2,0,1:T(2,128)S(1)} fusion(f32[2,256,1536]{2,1,0:T(8,128)S(1)} %fusion.79, s32[2]{0:T(128)S(1)} %fusion.84), kind=kOutput, calls=%fused_computation.82 | convolution fusion | flops 18874372 | bytes 6291464 | tf_op jit(solution)/shard_map/bn,bkc->nkc/dot_general | solution.py:220
  225.9 16.0 %all-reduce.6 = (f32[8]{0:T(128)S(1)}, f32[8]{0:T(128)S(1)}) all-reduce(f32[8]{0:T(128)S(1)} %dynamic-update-slice.3, f32[8]{0:T(128)S(1)} %dynamic-update-slice.2), channel_id=1, replica_groups=mesh['seq'=8,'own'=4] {'seq'}, use_global_device_ids=true, to_apply=%add.2 | all-reduce | flops 16 | bytes 128
  267.6 12.1 reshape.325
  312.7 75.2 %all-gather.13.cloned.1.call-done = f32[8,256,1536]{2,1,0:T(8,128)} async-done(((f32[1,256,1536]{2,1,0:T(8,128)}), f32[8,256,1536]{2,1,0:T(8,128)}) %all-gather.13.cloned.1.call-update) | async-done | bytes 12582928 | tf_op jit(solution)/shard_map/all_gather | solution.py:22
  387.9 37.0 %while.66 = (s32[]{:T(128)}, f32[256,1536]{1,0:T(8,128)}, s32[]{:T(128)}, f32[8]{0:T(128)S(1)}, f32[8,256,1536]{2,1,0:T(8,128)}, /*index=5*/f32[1]{0:T(128)}) while((s32[]{:T(128)}, f32[256,1536]{1,0:T(8,128)}, s32[]{:T(128)}, f32[8]{0:T(128)S(1)}, f32[8,256,1536]{2,1,0:T(8,128)}, /*index=5*/f32[1]{0:T(128)}) %tuple.193), condition=%wide.region_8.9_spmd.clone.clone, body=%wide.region_7.8_spmd.clone.sunk.clone | while | flops 1572873 | bytes 4718761 | solution.py:35
  424.9 139.4 %all-gather.11.cloned.1.call-done = f32[8,256,1536]{2,1,0:T(8,128)} async-done(((f32[1,256,1536]{2,1,0:T(8,128)}), f32[8,256,1536]{2,1,0:T(8,128)}) %all-gather.11.cloned.1.call-update) | async-done | bytes 12582928 | tf_op jit(solution)/shard_map/all_gather | solution.py:22
  564.3 27.6 %while.65 = (s32[]{:T(128)}, f32[256,1536]{1,0:T(8,128)S(1)}, s32[]{:T(128)}, f32[8]{0:T(128)S(1)}, f32[8,256,1536]{2,1,0:T(8,128)}, /*index=5*/f32[1]{0:T(128)}) while((s32[]{:T(128)}, f32[256,1536]{1,0:T(8,128)S(1)}, s32[]{:T(128)}, f32[8]{0:T(128)S(1)}, f32[8,256,1536]{2,1,0:T(8,128)}, /*index=5*/f32[1]{0:T(128)}) %tuple.196), condition=%wide.region_6.7_spmd.clone.clone, body=%wide.region_5.6_spmd.clone.sunk.clone | while | flops 1572869 | bytes 4718715 | solution.py:35
  618.6 35.9 %fusion.4 = (bf16[1024,3072]{1,0:T(8,128)(2,1)}, f32[1024,3072]{1,0:T(8,128)}) fusion(bf16[768,3072]{1,0:T(8,128)(2,1)S(1)} %bitcast.340, f32[1024,768]{0,1:T(8,128)S(1)} %get-tuple-element.622, f32[768]{0:T(1024)S(1)} %copy-done.69, f32[768]{0:T(1024)S(1)} %get-tuple-element.556, f32[1024]{0:T(1024)S(1)} %add_rsqrt_fusion.1, ...), kind=kOutput, calls=%fused_computation.14 | convolution fusion | flops 5040242688 | bytes 26753024 | tf_op jit(solution)/shard_map/dot_general | solution.py:249
  668.0 11.7 fusion.10
  740.7 11.4 fusion.39
  764.1 17.2 %all-reduce.7 = (bf16[8]{0:T(256)(128)(2,1)}, bf16[8]{0:T(256)(128)(2,1)}) all-reduce(bf16[8]{0:T(256)(128)(2,1)} %dynamic-update-slice.5, bf16[8]{0:T(256)(128)(2,1)} %dynamic-update-slice.4), channel_id=1, replica_groups=mesh['seq'=8,'own'=4] {'seq'}, use_global_device_ids=true, to_apply=%add.4 | all-reduce | flops 16 | bytes 64
  807.2 13.7 reshape.342
  820.9 11.5 copy.240
  843.0 13.2 reshape.340
  856.2 16.4 %copy.239 = f32[8,96,32,96]{3,1,2,0:T(8,128)} copy(f32[8,96,32,96]{3,2,1,0:T(8,128)} %reshape.340) | data formatting | bytes 18874368 | tf_op jit(solution)/shard_map/reshape | solution.py:73
  878.3 14.5 pad_maximum_fusion.1
  893.0 14.8 while.63
  907.8 45.7 %all-gather.15.cloned.1.call-done = bf16[8,256,1536]{2,1,0:T(8,128)(2,1)} async-done(((bf16[1,256,1536]{2,1,0:T(8,128)(2,1)}), bf16[8,256,1536]{2,1,0:T(8,128)(2,1)}) %all-gather.15.cloned.1.call-update) | async-done | bytes 6291472 | tf_op jit(solution)/shard_map/all_gather | solution.py:43
  1026.0 28.4 %pad_maximum_fusion = f32[32,24,96,96]{3,2,1,0:T(8,128)} fusion(f32[32,16,96,96]{3,2,1,0:T(8,128)} %bitcast.314, f32[32,8,96,96]{3,2,1,0:T(8,128)} %bitcast.315), kind=kLoop, calls=%fused_computation.8 | loop fusion | flops 7077888 | bytes 56623104 | tf_op jit(solution)/shard_map/concatenate | solution.py:347
  1062.3 60.8 %all-reduce.5 = (f32[4,768]{1,0:T(4,128)S(1)}, f32[3]{0:T(128)S(1)}) all-reduce(f32[4,768]{1,0:T(4,128)S(1)} %pad_maximum_fusion.10, f32[3]{0:T(128)S(1)} %pad_maximum_fusion.11), channel_id=1, replica_groups=mesh['seq'=8,'own'=4] {'seq','own'}, use_global_device_ids=true, to_apply=%region_30.31 | all-reduce | flops 3075 | bytes 24600 | tf_op jit(solution)/shard_map/psum | solution.py:356
  1140.1 30.1 %all-reduce.10.cloned.1.call-done = f32[2048,256]{1,0:T(8,128)} async-done(((f32[2048,256]{1,0:T(8,128)}), f32[2048,256]{1,0:T(8,128)}) %all-reduce.10.cloned.1.call-update) | async-done | bytes 2097168 | tf_op jit(solution)/shard_map/psum | solution.py:356
  1176.7 348.8 %reduce-scatter.2.cloned.1.call-done = f32[24,96,96]{2,1,0:T(8,128)} async-done(((f32[768,96,96]{2,1,0:T(8,128)}), f32[24,96,96]{2,1,0:T(8,128)}) %reduce-scatter.2.cloned.1.call-update) | async-done | bytes 884752 | tf_op jit(solution)/shard_map/reduce_scatter | solution.py:354
  (424 shorter events, 456.3 us)
Async XLA Ops:
  7.2 1518.4 %copy-start = (f32[24,96,96]{2,1,0:T(8,128)S(1)}, f32[24,96,96]{2,1,0:T(8,128)}, u32[]{:S(2)}) copy-start(f32[24,96,96]{2,1,0:T(8,128)} %param.34) | copy-start | bytes 2654212
  7.2 21.2 %all-gather.7.cloned.1.call-start = ((), (), s32[]{:S(2)}) async-start(), calls=%async_computation.1 | async-start | bytes 1310720 | tf_op jit(solution)/shard_map/all_gather | solution.py:182
  9.1 145.7 %all-gather.9.cloned.1.call-start = ((), (), s32[]{:S(2)}) async-start(), calls=%async_computation.2 | async-start | bytes 19464192 | tf_op jit(solution)/shard_map/all_gather | solution.py:165
  11.4 376.5 %all-gather.13.cloned.1.call-start = ((), (), s32[]{:S(2)}) async-start(), calls=%async_computation.4 | async-start | bytes 14155776 | tf_op jit(solution)/shard_map/all_gather | solution.py:22
  12.3 142.5 %copy-start.68 = (s32[2,512]{1,0:T(2,128)}, s32[2,512]{1,0:T(2,128)S(1)}, u32[]{:S(2)}) copy-start(s32[2,512]{1,0:T(2,128)S(1)} %fusion.93) | copy-start | bytes 12292
  15.0 175.8 %copy-start.80 = (s32[2]{0:T(128)}, s32[2]{0:T(128)S(1)}, u32[]{:S(2)}) copy-start(s32[2]{0:T(128)S(1)} %fusion.84) | copy-start | bytes 28
  15.6 174.1 %copy-start.52 = (pred[2,512]{1,0:T(4,128)(4,1)}, pred[2,512]{1,0:T(4,128)(4,1)S(1)}, u32[]{:S(2)}) copy-start(pred[2,512]{1,0:T(4,128)(4,1)S(1)} %get-tuple-element.620) | copy-start | bytes 3076
  30.6 124.3 %copy-start.26 = (bf16[2,512,256]{2,1,0:T(8,128)(2,1)}, bf16[2,512,256]{2,1,0:T(8,128)(2,1)S(1)}, u32[]{:S(2)}) copy-start(bf16[2,512,256]{2,1,0:T(8,128)(2,1)S(1)} %get-tuple-element.379) | copy-start | bytes 1572868
  215.1 349.1 %all-gather.11.cloned.1.call-start = ((), (), s32[]{:S(2)}) async-start(), calls=%async_computation.3 | async-start | bytes 14155776 | tf_op jit(solution)/shard_map/all_gather | solution.py:22
  216.5 676.3 %all-gather.17.cloned.1.call-start = ((), (), s32[]{:S(2)}) async-start(), calls=%async_computation.6 | async-start | bytes 7077888 | tf_op jit(solution)/shard_map/all_gather | solution.py:43
  249.1 342.9 %copy-start.88 = (f32[2]{0:T(128)}, f32[2]{0:T(128)S(1)}, u32[]{:S(2)}) copy-start(f32[2]{0:T(128)S(1)} %get-tuple-element.657) | copy-start | bytes 28
  249.1 342.9 %copy-start.90 = (f32[2]{0:T(128)}, f32[2]{0:T(128)S(1)}, u32[]{:S(2)}) copy-start(f32[2]{0:T(128)S(1)} %get-tuple-element.658) | copy-start | bytes 28
  250.3 363.6 %copy-start.73 = (f32[1024]{0:T(1024)}, f32[1024]{0:T(1024)S(1)}, u32[]{:S(2)}) copy-start(f32[1024]{0:T(1024)S(1)} %get-tuple-element.618) | copy-start | bytes 12292
  613.9 40.6 %slice-start.2 = ((s8[4718592]{0:T(1024)(128)(4,1)}), s8[4194304]{0:T(1024)(128)(4,1)S(1)}, s32[]{:S(2)}) async-start(s8[4718592]{0:T(1024)(128)(4,1)} %bitcast.341), calls=%async_computation.11 | async-start | bytes 8388608
  616.7 73.1 %copy-start.11 = (f32[1024,768]{0,1:T(8,128)}, f32[1024,768]{0,1:T(8,128)S(1)}, u32[]{:S(2)}) copy-start(f32[1024,768]{0,1:T(8,128)S(1)} %get-tuple-element.622) | copy-start | bytes 9437188
  756.7 196.9 %all-gather.15.cloned.1.call-start = ((), (), s32[]{:S(2)}) async-start(), calls=%async_computation.5 | async-start | bytes 7077888 | tf_op jit(solution)/shard_map/all_gather | solution.py:43
  759.1 411.0 %all-reduce.10.cloned.1.call-start = ((), (), s32[]{:S(2)}) async-start(), calls=%async_computation.8 | async-start | bytes 4194304 | tf_op jit(solution)/shard_map/psum | solution.py:356
  893.0 61.9 %copy-start.95 = (bf16[8]{0:T(256)(128)(2,1)S(1)}, bf16[8]{0:T(256)(128)(2,1)}, u32[]{:S(2)}) copy-start(bf16[8]{0:T(256)(128)(2,1)} %get-tuple-element.960) | copy-start | bytes 52
  1015.4 510.2 %reduce-scatter.2.cloned.1.call-start = ((), (), s32[]{:S(2)}) async-start(), calls=%async_computation.7 | async-start | bytes 38928384 | tf_op jit(solution)/shard_map/reduce_scatter | solution.py:354
  1054.5 70.4 %copy-start.55 = (f32[4,768]{1,0:T(4,128)S(1)}, f32[4,768]{1,0:T(4,128)}, u32[]{:S(2)}) copy-start(f32[4,768]{1,0:T(4,128)} %param.40) | copy-start | bytes 36868
  1054.5 70.4 %copy-start.66 = (f32[4,768]{1,0:T(4,128)S(1)}, f32[4,768]{1,0:T(4,128)}, u32[]{:S(2)}) copy-start(f32[4,768]{1,0:T(4,128)} %param.41) | copy-start | bytes 36868
  1054.5 71.0 %copy-start.57 = (f32[1024]{0:T(1024)S(1)}, f32[1024]{0:T(1024)}, u32[]{:S(2)}) copy-start(f32[1024]{0:T(1024)} %copy-done.56) | copy-start | bytes 12292
  1054.5 71.0 %copy-start.59 = (f32[1024]{0:T(1024)S(1)}, f32[1024]{0:T(1024)}, u32[]{:S(2)}) copy-start(f32[1024]{0:T(1024)} %copy-done.58) | copy-start | bytes 12292
  1057.6 67.9 %copy-start.38 = (bf16[1024,768]{1,0:T(8,128)(2,1)S(1)}, bf16[1024,768]{1,0:T(8,128)(2,1)}, u32[]{:S(2)}) copy-start(bf16[1024,768]{1,0:T(8,128)(2,1)} %copy.234) | copy-start | bytes 4718596
  (85 other events, 628.3 us)
Sparse Core Ops, SparseCore 0:
  10.2 18.2 all-gather.6
  31.9 122.9 all-gather.8
  215.3 172.6 all-gather.12
  390.0 174.2 all-gather.10
  756.8 97.1 all-gather.16
  856.6 96.8 all-gather.14
  1015.5 154.6 all-reduce.9
  1177.2 348.3 reduce-scatter.1
where the time goes:
time: 1560 us; the launch traced here: 1550 us
  waiting for transfers between devices  776 us (50%)
  local copies, waits for them, and re-layouts  280 us (18%)
  matrix products  213 us (14%)
  other arithmetic  141 us (9%)
  blocking collectives  94 us (6%)
  between operations  29.1 us (2%)
  loops' own time  15.9 us (1%)
    reduce_scatter x1, waiting for transfers between devices, per_device(): lax.psum_scatter(stacked, ('seq', 'own'), scatter_dimension=0, tiled=True)  349 us
    all_gather x2, waiting for transfers between devices, prefix(): everything = jax.tree.map(lambda part: lax.all_gather(part, axis), shard)  215 us
    all_gather x1, waiting for transfers between devices, per_device(): lax.all_gather(weights.astype(jnp.bfloat16), ('seq', 'own'), axis=0, tile...  124 us
    reshape x10, local copies, waits for them, and re-layouts, to_tiles(): matrix.reshape(rows // size, size, cols // size, size).transpose(0, 2, 1, 3)  77.3 us
    psum x1, blocking collectives, per_device(): proj_total, norm_grad = lax.psum((grad_proj, norm_terms), ('seq', 'own'))  60.8 us
    unnamed x221, local copies, waits for them, and re-layouts  46.1 us
    all_gather x2, waiting for transfers between devices, entering(): lax.all_gather(a.astype(kind), axis)  45.7 us
    select_n x16, other arithmetic, hop(): return jax.tree.map(lambda a, b: jnp.where(reached, a, b), new, before)  44.2 us
  transfers between devices with their start and end apart: 8, of which 7 were waited for; matrix products, arithmetic and copies ran while one was open for 20% of the time, Pallas kernels for 0%

commit v1 on v0

v1 whole, which is shorter than its diff:
```python
import functools
import math

import jax
import jax.numpy as jnp
from jax import lax
from jax.experimental import pallas as pl
from jax.experimental.pallas import tpu as pltpu
from jax.sharding import PartitionSpec as P

HEADS = 12
FF = 3072
SHORT = 512
BF = jnp.bfloat16
F32 = jnp.float32

eps_norm = 1e-05
decay = 0.5
rate_matrix = 0.2
rate_norm = 0.2
highest = lax.Precision.HIGHEST
VMEM_LIMIT = 60 * 1024 * 1024


def dot(a, b):
    return lax.dot_general(a, b, (((1,), (0,)), ((), ())), preferred_element_type=F32)


def dot_t(a, b):
    return lax.dot_general(a, b, (((1,), (1,)), ((), ())), preferred_element_type=F32)


def dot_l(a, b):
    return lax.dot_general(a, b, (((0,), (0,)), ((), ())), preferred_element_type=F32)


def vspec(shape, index_map, once=False):
    if once:
        return pl.BlockSpec(shape, index_map, pipeline_mode=pl.Buffered(1))
    return pl.BlockSpec(shape, index_map)


def params():
    return pltpu.CompilerParams(
        dimension_semantics=("arbitrary",), vmem_limit_bytes=VMEM_LIMIT
    )


def cost(flops, nbytes, trans=0):
    return pl.CostEstimate(flops=int(flops), bytes_accessed=int(nbytes), transcendentals=int(trans))


def project_body(width, with_query, x_ref, w_ref, e_ref, *outs):
    x = x_ref[...]
    if with_query:
        q_ref, kv_ref, p_ref = outs
        q_ref[...] = dot(x, w_ref[pl.ds(0, width), :]).astype(BF)
    else:
        (p_ref,) = outs
    e = e_ref[0]
    for part in range(2):
        kv = dot(x, w_ref[pl.ds((1 + part) * width, width), :]).astype(BF)
        if with_query:
            kv_ref[:, pl.ds(part * width, width)] = kv
        p_ref[0, :, pl.ds(part * width, width)] = dot(e, kv)


def project(x, w_att, e_t, with_query):
    rows, width = x.shape
    blocks, kp, short = e_t.shape
    out_shape = [jax.ShapeDtypeStruct((blocks, kp, 2 * width), F32)]
    out_specs = [vspec((1, kp, 2 * width), lambda i: (i, 0, 0))]
    if with_query:
        out_shape = [
            jax.ShapeDtypeStruct((rows, width), BF),
            jax.ShapeDtypeStruct((rows, 2 * width), BF),
        ] + out_shape
        out_specs = [
            vspec((short, width), lambda i: (i, 0)),
            vspec((short, 2 * width), lambda i: (i, 0)),
        ] + out_specs
    return pl.pallas_call(
        functools.partial(project_body, width, with_query),
        grid=(blocks,),
        in_specs=[
            vspec((short, width), lambda i: (i, 0)),
            vspec((3 * width, width), lambda i: (0, 0), True),
            vspec((1, kp, short), lambda i: (i, 0, 0)),
        ],
        out_specs=out_specs,
        out_shape=out_shape,
        compiler_params=params(),
        cost_estimate=cost(2 * rows * width * width * 3, 12e6),
        name="project" if with_query else "project_peer",
    )(x, w_att, e_t)


def head_pair(ref_slice, low_lane):
    zero = jnp.zeros_like(ref_slice)
    return jnp.concatenate(
        [jnp.where(low_lane, ref_slice, zero), jnp.where(low_lane, zero, ref_slice)], axis=0
    )


def softmax_pair(scores, kp):
    parts = []
    for half in range(2):
        s = scores[:, half * kp : (half + 1) * kp]
        top = jnp.max(s, axis=-1, keepdims=True)
        e = jnp.exp(s - top)
        parts.append(e * (1.0 / jnp.sum(e, axis=-1, keepdims=True)))
    return parts


def attend_body(width, head, kp, n_ref, q_ref, s_ref, w_ref, x_ref, mix_ref, sum_ref, stat_ref):
    pairs = width // (2 * head)
    step = pl.program_id(0)
    scale = head ** (-0.5)
    low_lane = lax.broadcasted_iota(jnp.int32, (kp, 2 * head), 1) < head
    for j in range(pairs):
        cols = pl.ds(j * 2 * head, 2 * head)
        keys = head_pair(s_ref[0, :, cols], low_lane)
        values = head_pair(s_ref[0, :, pl.ds(width + j * 2 * head, 2 * head)], low_lane)
        scores = dot_t(q_ref[:, cols], keys) * scale
        prob = jnp.concatenate(softmax_pair(scores, kp), axis=1).astype(BF)
        mix_ref[:, cols] = dot(prob, values).astype(BF)
    branch = dot(mix_ref[...], w_ref[...])
    first = x_ref[...].astype(F32) + branch
    sum_ref[...] = first
    rows = q_ref.shape[0]
    keep = (lax.broadcasted_iota(jnp.int32, (rows, 1), 0) < n_ref[step]).astype(F32)
    sums = jnp.concatenate(
        [
            jnp.sum(keep * first * first, axis=0, keepdims=True),
            jnp.sum(keep * branch * branch, axis=0, keepdims=True),
        ],
        axis=0,
    )

    @pl.when(step == 0)
    def _():
        stat_ref[...] = sums

    @pl.when(step > 0)
    def _():
        stat_ref[...] += sums


def attend(n_valid, q, summary, w_att, x, head):
    rows, width = q.shape
    blocks, kp, _ = summary.shape
    short = rows // blocks
    return pl.pallas_call(
        functools.partial(attend_body, width, head, kp),
        grid_spec=pltpu.PrefetchScalarGridSpec(
            num_scalar_prefetch=1,
            grid=(blocks,),
            in_specs=[
                vspec((short, width), lambda i, n: (i, 0)),
                vspec((1, kp, 2 * width), lambda i, n: (i, 0, 0)),
                vspec((width, width), lambda i, n: (3, 0), True),
                vspec((short, width), lambda i, n: (i, 0)),
            ],
            out_specs=[
                vspec((short, width), lambda i, n: (i, 0)),
                vspec((short, width), lambda i, n: (i, 0)),
                vspec((2, width), lambda i, n: (0, 0)),
            ],
        ),
        out_shape=[
            jax.ShapeDtypeStruct((rows, width), BF),
            jax.ShapeDtypeStruct((rows, width), F32),
            jax.ShapeDtypeStruct((2, width), F32),
        ],
        compiler_params=params(),
        cost_estimate=cost(2 * rows * width * (width + 4 * kp), 10e6, rows * kp * 12),
        name="attend",
    )(n_valid, q, summary, w_att, x)


def normalize(values):
    mean = jnp.mean(values, axis=-1, keepdims=True)
    centered = values - mean
    inverse = lax.rsqrt(jnp.mean(centered * centered, axis=-1, keepdims=True) + eps_norm)
    return centered * inverse, inverse


def norm_back(grad_out, normed, inverse, gain):
    scaled = grad_out * gain
    return inverse * (
        scaled
        - jnp.mean(scaled, axis=-1, keepdims=True)
        - normed * jnp.mean(scaled * normed, axis=-1, keepdims=True)
    )


def feed_body(
    chunks,
    first_ref,
    w1_ref,
    w2_ref,
    wo_ref,
    cot_ref,
    np_ref,
    out_ref,
    hid_ref,
    up_ref,
    down_ref,
    flow_ref,
    dfirst_ref,
    dbranch_ref,
    dmix_ref,
    ng_ref,
    slope_ref,
):
    step = pl.program_id(0)
    rows, width = first_ref.shape
    normed_one, inverse_one = normalize(first_ref[...])
    first_norm = normed_one * np_ref[0:1, :] + np_ref[1:2, :]
    first_low = first_norm.astype(BF)
    flow_ref[...] = first_low
    second = first_norm
    for c in range(chunks):
        cols = pl.ds(c * width, width)
        u = dot(first_low, w1_ref[:, c].reshape(width, width))
        cumulative = 0.5 * (1.0 + lax.erf(u * (1.0 / math.sqrt(2.0))))
        density = jnp.exp(-0.5 * u * u) * (1.0 / math.sqrt(2.0 * math.pi))
        slope_ref[:, cols] = cumulative + u * density
        hidden = (u * cumulative).astype(BF)
        hid_ref[:, cols] = hidden
        second = second + dot(hidden, w2_ref[pl.ds(c * width, width), :])
    normed_two, inverse_two = normalize(second)
    out_ref[...] = (normed_two * np_ref[2:3, :] + np_ref[3:4, :]).astype(BF)
    grad_out = cot_ref[...].astype(F32)
    gain_two = jnp.sum(grad_out * normed_two, axis=0, keepdims=True)
    shift_two = jnp.sum(grad_out, axis=0, keepdims=True)
    grad_second = norm_back(grad_out, normed_two, inverse_two, np_ref[2:3, :])
    down = grad_second.astype(BF)
    down_ref[...] = down
    grad_first_norm = grad_second
    for c in range(chunks):
        cols = pl.ds(c * width, width)
        grad_hidden = dot_t(down, w2_ref[pl.ds(c * width, width), :])
        up = (grad_hidden * slope_ref[:, cols]).astype(BF)
        up_ref[:, cols] = up
        grad_first_norm = grad_first_norm + dot_t(up, w1_ref[:, c].reshape(width, width))
    gain_one = jnp.sum(grad_first_norm * normed_one, axis=0, keepdims=True)
    shift_one = jnp.sum(grad_first_norm, axis=0, keepdims=True)
    grad_first = norm_back(grad_first_norm, normed_one, inverse_one, np_ref[0:1, :])
    dfirst_ref[...] = grad_first
    grad_branch = grad_first.astype(BF)
    dbranch_ref[...] = grad_branch
    dmix_ref[...] = dot_t(grad_branch, wo_ref[...]).astype(BF)
    sums = jnp.concatenate([gain_one, shift_one, gain_two, shift_two], axis=0)

    @pl.when(step == 0)
    def _():
        ng_ref[...] = sums

    @pl.when(step > 0)
    def _():
        ng_ref[...] += sums


def feed(first_sum, w_up, w_down, w_att, cotangent, norm_params, tile):
    rows, width = first_sum.shape
    chunks = w_up.shape[1]
    ff = chunks * width
    row = lambda i: (i, 0)
    return pl.pallas_call(
        functools.partial(feed_body, chunks),
        grid=(rows // tile,),
        in_specs=[
            vspec((tile, width), row),
            vspec(w_up.shape, lambda i: (0, 0, 0, 0), True),
            vspec((ff, width), lambda i: (0, 0), True),
            vspec((width, width), lambda i: (3, 0), True),
            vspec((tile, width), row),
            vspec(norm_params.shape, lambda i: (0, 0)),
        ],
        out_specs=[
            vspec((tile, width), row),
            vspec((tile, ff), row),
            vspec((tile, ff), row),
            vspec((tile, width), row),
            vspec((tile, width), row),
            vspec((tile, width), row),
            vspec((tile, width), row),
            vspec((tile, width), row),
            vspec((4, width), lambda i: (0, 0)),
        ],
        out_shape=[
            jax.ShapeDtypeStruct((rows, width), BF),
            jax.ShapeDtypeStruct((rows, ff), BF),
            jax.ShapeDtypeStruct((rows, ff), BF),
            jax.ShapeDtypeStruct((rows, width), BF),
            jax.ShapeDtypeStruct((rows, width), BF),
            jax.ShapeDtypeStruct((rows, width), F32),
            jax.ShapeDtypeStruct((rows, width), BF),
            jax.ShapeDtypeStruct((rows, width), BF),
            jax.ShapeDtypeStruct((4, width), F32),
        ],
        scratch_shapes=[pltpu.VMEM((tile, ff), F32)],
        compiler_params=params(),
        cost_estimate=cost(2 * rows * width * ff * 4, 30e6, rows * ff * 2),
        name="feed",
    )(first_sum, w_up, w_down, w_att, cotangent, norm_params)


def attend_back_body(width, head, kp, q_ref, s_ref, g_ref, dq_ref, ds_ref):
    pairs = width // (2 * head)
    scale = head ** (-0.5)
    low_lane = lax.broadcasted_iota(jnp.int32, (kp, 2 * head), 1) < head
    for j in range(pairs):
        cols = pl.ds(j * 2 * head, 2 * head)
        vcols = pl.ds(width + j * 2 * head, 2 * head)
        keys = head_pair(s_ref[0, :, cols], low_lane)
        values = head_pair(s_ref[0, :, vcols], low_lane)
        q = q_ref[:, cols]
        g = g_ref[:, cols]
        prob = softmax_pair(dot_t(q, keys) * scale, kp)
        grad_prob = dot_t(g, values)
        low_parts = []
        for half in range(2):
            p = prob[half]
            d = grad_prob[:, half * kp : (half + 1) * kp]
            low_parts.append((p * (d - jnp.sum(p * d, axis=-1, keepdims=True))).astype(BF))
        grad_scores = jnp.concatenate(low_parts, axis=1)
        prob_low = jnp.concatenate(prob, axis=1).astype(BF)
        dq_ref[:, cols] = (dot(grad_scores, keys) * scale).astype(BF)
        dk = dot_l(grad_scores, q) * scale
        dv = dot_l(prob_low, g)
        ds_ref[0, :, cols] = jnp.where(low_lane, dk[:kp], dk[kp:])
        ds_ref[0, :, vcols] = jnp.where(low_lane, dv[:kp], dv[kp:])


def attend_back(q, summary, grad_mix, head):
    rows, width = q.shape
    blocks, kp, _ = summary.shape
    short = rows // blocks
    return pl.pallas_call(
        functools.partial(attend_back_body, width, head, kp),
        grid=(blocks,),
        in_specs=[
            vspec((short, width), lambda i: (i, 0)),
            vspec((1, kp, 2 * width), lambda i: (i, 0, 0)),
            vspec((short, width), lambda i: (i, 0)),
        ],
        out_specs=[
            vspec((short, width), lambda i: (i, 0)),
            vspec((1, kp, 2 * width), lambda i: (i, 0, 0)),
        ],
        out_shape=[
            jax.ShapeDtypeStruct((rows, width), BF),
            jax.ShapeDtypeStruct((blocks, kp, 2 * width), F32),
        ],
        compiler_params=params(),
        cost_estimate=cost(2 * rows * width * 8 * kp, 10e6, rows * kp * 12),
        name="attend_back",
    )(q, summary, grad_mix)


def outer_body(split, l_ref, r_ref, o_ref):
    value = dot_l(l_ref[...], r_ref[...])
    o_ref[...] = value.reshape(o_ref.shape).astype(o_ref.dtype)


def outer_up(first_low, grad_up, size, dtype):
    rows, width = first_low.shape
    chunks = grad_up.shape[1] // width
    groups = width // size
    return pl.pallas_call(
        functools.partial(outer_body, True),
        grid=(chunks,),
        in_specs=[
            vspec((rows, width), lambda i: (0, 0), True),
            vspec((rows, width), lambda i: (0, i)),
        ],
        out_specs=vspec((groups, 1, size, width), lambda i: (0, i, 0, 0)),
        out_shape=jax.ShapeDtypeStruct((groups, chunks, size, width), dtype),
        compiler_params=params(),
        cost_estimate=cost(2 * rows * width * width * chunks, 20e6),
        name="outer_up",
    )(first_low, grad_up)


def outer_rows(left, right, dtype, name):
    rows, width = right.shape
    chunks = left.shape[1] // width
    return pl.pallas_call(
        functools.partial(outer_body, False),
        grid=(chunks,),
        in_specs=[
            vspec((rows, width), lambda i: (0, i)),
            vspec((rows, width), lambda i: (0, 0), True),
        ],
        out_specs=vspec((width, width), lambda i: (i, 0)),
        out_shape=jax.ShapeDtypeStruct((chunks * width, width), dtype),
        compiler_params=params(),
        cost_estimate=cost(2 * rows * width * width * chunks, 20e6),
        name=name,
    )(left, right)


def back_body(width, e_ref, kv_ref, s_ref, dq_ref, w_ref, df_ref, dkv_ref, ge_ref, gi_ref):
    summary = s_ref[0]
    dkv = dot(e_ref[0], summary).astype(BF)
    dkv_ref[...] = dkv
    ge_ref[0] = dot_t(kv_ref[...], summary)
    gi_ref[...] = (
        df_ref[...]
        + dot_t(dq_ref[...], w_ref[pl.ds(0, width), :])
        + dot_t(dkv[:, :width], w_ref[pl.ds(width, width), :])
        + dot_t(dkv[:, width:], w_ref[pl.ds(2 * width, width), :])
    )


def back(e_rows, kv, grad_summary, dq, w_att, grad_first):
    rows, width = dq.shape
    blocks, short, kp = e_rows.shape
    row = lambda i: (i, 0)
    lead = lambda i: (i, 0, 0)
    return pl.pallas_call(
        functools.partial(back_body, width),
        grid=(blocks,),
        in_specs=[
            vspec((1, short, kp), lead),
            vspec((short, 2 * width), row),
            vspec((1, kp, 2 * width), lead),
            vspec((short, width), row),
            vspec((3 * width, width), lambda i: (0, 0), True),
            vspec((short, width), row),
        ],
        out_specs=[
            vspec((short, 2 * width), row),
            vspec((1, short, kp), lead),
            vspec((short, width), row),
        ],
        out_shape=[
            jax.ShapeDtypeStruct((rows, 2 * width), BF),
            jax.ShapeDtypeStruct((blocks, short, kp), F32),
            jax.ShapeDtypeStruct((rows, width), F32),
        ],
        compiler_params=params(),
        cost_estimate=cost(2 * rows * width * (3 * width + 4 * kp), 20e6),
        name="back",
    )(e_rows, kv, grad_summary, dq, w_att, grad_first)


MESH_ID = pl.DeviceIdType.MESH


def reduce_body(depth, half, n_src, extra_keep, *refs):
    sources = refs[:n_src]
    outs = refs[n_src : n_src + 5]
    (own, got_c, sum_c, got_a, got_b, sum_a, sum_b, got_a2, got_b2, sum_z, got_z) = refs[
        n_src + 5 : n_src + 16
    ]
    (e_own, e_got, e_sum, e_got1, e_sum1, e_got2, e_sum2, e_gotz, e_all, e_rows) = refs[
        n_src + 16 : n_src + 26
    ]
    send, recv, local = refs[n_src + 26 :]
    seq, mine = lax.axis_index("seq"), lax.axis_index("own")
    z, y, x, c = seq // 2, seq % 2, mine // 2, mine % 2
    core = (seq, 2 * x + (1 - c))
    along_x = (seq, 2 * (1 - x) + c)
    along_y = (2 * z + (1 - y), mine)
    along_z = [(2 * lax.rem(z + d, depth) + y, mine) for d in range(1, depth)]
    barrier = pltpu.get_barrier_semaphore()
    partners = [core, along_x, along_y] + along_z
    for partner in partners:
        pl.semaphore_signal(barrier, inc=1, device_id=partner, device_id_type=MESH_ID)
    pl.semaphore_wait(barrier, len(partners))

    sent = []

    def push(src, dst, partner):
        at = len(sent)
        copy = pltpu.make_async_remote_copy(
            src_ref=src,
            dst_ref=dst,
            send_sem=send.at[at],
            recv_sem=recv.at[at],
            device_id=partner,
            device_id_type=MESH_ID,
        )
        copy.start()
        sent.append(copy)
        return copy

    pieces = 3
    up, down, extra = sources[0], sources[1], sources[6]
    half_z = depth // 2
    loads, firsts = [], []

    def load(src, dst):
        copy = pltpu.make_async_copy(src, dst, local.at[len(loads)])
        copy.start()
        loads.append(copy)
        return copy

    e_first = [push(extra.at[:, :, 1 - c], e_got, core)]
    e_load = [load(extra.at[:, :, c], e_own)]
    piece_first, piece_load = [], []
    for p in range(2):
        piece_first.append(
            [
                push(up.at[:, :, 1 - c, p], got_c.at[p, pl.ds(0, half_z)], core),
                push(down.at[:, :, 1 - c, p], got_c.at[p, pl.ds(half_z, half_z)], core),
            ]
        )
        piece_load.append(
            [
                load(up.at[:, :, c, p], own.at[p, pl.ds(0, half_z)]),
                load(down.at[:, :, c, p], own.at[p, pl.ds(half_z, half_z)]),
            ]
        )
    piece_first.append(
        [push(sources[2 + m].at[:, 1 - c], got_c.at[2, m], core) for m in range(depth)]
    )
    piece_load.append([load(sources[2 + m].at[:, c], own.at[2, m]) for m in range(depth)])

    state = {}

    def wait_recv(copies):
        for copy in copies:
            copy.wait_recv()

    def add(a, b):
        return (a.astype(F32) + b.astype(F32)).astype(BF)

    def piece_c(p):
        for copy in piece_load[p]:
            copy.wait()
        wait_recv(piece_first[p])

        def body(i, carry):
            zz, yx = i // 4, i % 4
            sum_c[p, zz, yx // 2, yx % 2] = add(own[p, zz, yx], got_c[p, zz, yx])
            return carry

        lax.fori_loop(0, depth * 4, body, 0)
        state["1", p] = [
            push(sum_c.at[p, :, :, 1 - x, pl.ds(0, half), :], got_a.at[p], along_x),
            push(sum_c.at[p, :, 1 - y, :, pl.ds(half, half), :], got_b.at[p], along_y),
        ]

    def piece_1(p):
        wait_recv(state["1", p])

        def body(i, carry):
            zz, w = i // 2, i % 2
            sum_a[p, zz, w] = add(sum_c[p, zz, w, x, pl.ds(0, half), :], got_a[p, zz, w])
            sum_b[p, zz, w] = add(sum_c[p, zz, y, w, pl.ds(half, half), :], got_b[p, zz, w])
            return carry

        lax.fori_loop(0, depth * 2, body, 0)
        state["2", p] = [
            push(sum_a.at[p, :, 1 - y], got_a2.at[p], along_y),
            push(sum_b.at[p, :, 1 - x], got_b2.at[p], along_x),
        ]

    def piece_2(p):
        wait_recv(state["2", p])

        def body(zz, carry):
            sum_z[p, zz, pl.ds(0, half), :] = add(sum_a[p, zz, y], got_a2[p, zz])
            sum_z[p, zz, pl.ds(half, half), :] = add(sum_b[p, zz, x], got_b2[p, zz])
            return carry

        lax.fori_loop(0, depth, body, 0)
        state["z", p] = [
            push(sum_z.at[p, lax.rem(z + d, depth)], got_z.at[p, d - 1], along_z[d - 1])
            for d in range(1, depth)
        ]

    def piece_z(p):
        wait_recv(state["z", p])
        total = sum_z[p, z].astype(F32)
        for d in range(depth - 1):
            total = total + got_z[p, d].astype(F32)
        outs[p][...] = total

    def extra_c():
        e_load[0].wait()
        wait_recv(e_first)

        def body(i, carry):
            zz, yx = i // 4, i % 4
            e_sum[zz, yx // 2, yx % 2] = e_own[zz, yx] + e_got[zz, yx]
            return carry

        lax.fori_loop(0, depth * 4, body, 0)
        state["e1"] = [push(e_sum.at[:, :, 1 - x], e_got1, along_x)]

    def extra_1():
        wait_recv(state["e1"])

        def body(i, carry):
            zz, yy = i // 2, i % 2
            e_sum1[zz, yy] = e_sum[zz, yy, x] + e_got1[zz, yy]
            return carry

        lax.fori_loop(0, depth * 2, body, 0)
        state["e2"] = [push(e_sum1.at[:, 1 - y], e_got2, along_y)]

    def extra_2():
        wait_recv(state["e2"])

        def body(zz, carry):
            e_sum2[zz] = e_sum1[zz, y] + e_got2[zz]
            return carry

        lax.fori_loop(0, depth, body, 0)
        state["ez"] = [
            push(e_sum2.at[lax.rem(z + d, depth)], e_gotz.at[d - 1], along_z[d - 1])
            for d in range(1, depth)
        ]

    def extra_z():
        wait_recv(state["ez"])
        total = e_sum2[z]
        for d in range(depth - 1):
            total = total + e_gotz[d]
        e_all[z, y] = total
        state["gz"] = [push(e_all.at[z, y], e_all.at[z, y], there) for there in along_z]

    def extra_gather_y():
        wait_recv(state["gz"])
        state["gy"] = [push(e_all.at[:, y], e_all.at[:, y], along_y)]

    def extra_gather_x():
        wait_recv(state["gy"])
        e_rows[x, c] = e_all[:, :, pl.ds(extra_keep, e_rows.shape[4]), :]
        state["gx"] = [push(e_rows.at[x, c], e_rows.at[x, c], along_x)]

    def extra_gather_c():
        wait_recv(state["gx"])
        state["gc"] = [push(e_rows.at[:, c], e_rows.at[:, c], core)]

    extra_c()
    piece_c(0)
    extra_1()
    piece_c(1)
    extra_2()
    piece_1(0)
    piece_c(2)
    extra_z()
    piece_2(0)
    piece_1(1)
    extra_gather_y()
    piece_1(2)
    piece_2(1)
    extra_gather_x()
    piece_z(0)
    piece_2(2)
    extra_gather_c()
    piece_z(1)
    piece_z(2)
    outs[3][...] = e_all[:, :, pl.ds(0, extra_keep), :]
    wait_recv(state["gc"])
    outs[4][...] = e_rows[...]
    for copy in sent:
        copy.wait_send()


def reduce_all(g_att, g_up, g_down, extra, peers):
    depth = peers // 2
    size, width = g_up.shape[2], g_up.shape[3]
    half = size // 2
    e_rows_all, kp = extra.shape[1], extra.shape[2]
    keep = e_rows_all - 8
    sources = (
        [
            g_up.reshape(depth // 2, 4, 2, 2, size, width),
            g_down.reshape(depth // 2, 4, 2, 2, size, width),
        ]
        + [g.reshape(4, 2, size, width) for g in g_att]
        + [extra.reshape(depth, 4, 2, e_rows_all, kp)]
    )
    n_src = len(sources)
    messages = 1 + 4 + depth + 3 * (4 + depth - 1) + 2 + 2 * (depth - 1) + 3
    loads = 1 + 4 + depth
    any_spec = pl.BlockSpec(memory_space=pl.ANY)
    vmem = pl.BlockSpec(memory_space=pltpu.VMEM)
    scratch = [
        pltpu.VMEM((3, depth, 4, size, width), BF),
        pltpu.VMEM((3, depth, 4, size, width), BF),
        pltpu.VMEM((3, depth, 2, 2, size, width), BF),
        pltpu.VMEM((3, depth, 2, half, width), BF),
        pltpu.VMEM((3, depth, 2, half, width), BF),
        pltpu.VMEM((3, depth, 2, half, width), BF),
        pltpu.VMEM((3, depth, 2, half, width), BF),
        pltpu.VMEM((3, depth, half, width), BF),
        pltpu.VMEM((3, depth, half, width), BF),
        pltpu.VMEM((3, depth, size, width), BF),
        pltpu.VMEM((3, depth - 1, size, width), BF),
        pltpu.VMEM((depth, 4, e_rows_all, kp), F32),
        pltpu.VMEM((depth, 4, e_rows_all, kp), F32),
        pltpu.VMEM((depth, 2, 2, e_rows_all, kp), F32),
        pltpu.VMEM((depth, 2, e_rows_all, kp), F32),
        pltpu.VMEM((depth, 2, e_rows_all, kp), F32),
        pltpu.VMEM((depth, e_rows_all, kp), F32),
        pltpu.VMEM((depth, e_rows_all, kp), F32),
        pltpu.VMEM((depth - 1, e_rows_all, kp), F32),
        pltpu.VMEM((depth, 2, e_rows_all, kp), F32),
        pltpu.VMEM((2, 2, depth, 2, 8, kp), F32),
        pltpu.SemaphoreType.DMA((messages,)),
        pltpu.SemaphoreType.DMA((messages,)),
        pltpu.SemaphoreType.DMA((loads,)),
    ]
    return pl.pallas_call(
        functools.partial(reduce_body, depth, half, n_src, keep),
        in_specs=[any_spec] * n_src,
        out_specs=[vmem] * 5,
        out_shape=[jax.ShapeDtypeStruct((size, width), F32)] * 3
        + [
            jax.ShapeDtypeStruct((depth, 2, keep, kp), F32),
            jax.ShapeDtypeStruct((2, 2, depth, 2, 8, kp), F32),
        ],
        scratch_shapes=scratch,
        compiler_params=pltpu.CompilerParams(
            collective_id=1, has_side_effects=True, vmem_limit_bytes=VMEM_LIMIT
        ),
        name="reduce_all",
    )(*sources)


def shampoo(grad, left, right, root_left, root_right, weight):
    new_left = decay * left + (1.0 - decay) * jnp.einsum(
        "tij,tkj->tik", grad, grad, precision=highest
    )
    new_right = decay * right + (1.0 - decay) * jnp.einsum(
        "tji,tjk->tik", grad, grad, precision=highest
    )
    inner = jnp.einsum("tij,tjk->tik", grad, root_right, precision=highest)
    step = jnp.einsum("tij,tjk->tik", root_left, inner, precision=highest)
    return (new_left, new_right, weight - rate_matrix * step)


def to_matrix(tiles, rows, cols):
    size = tiles.shape[-1]
    return (
        tiles.reshape(rows // size, cols // size, size, size)
        .transpose(0, 2, 1, 3)
        .reshape(rows, cols)
    )


def to_bands(tiles, cols):
    count, size, _ = tiles.shape
    return to_matrix(tiles, count * size * size // cols, cols)


def from_bands(bands, size):
    rows, cols = bands.shape
    return (
        bands.reshape(rows // size, size, cols // size, size)
        .transpose(0, 2, 1, 3)
        .reshape(-1, size, size)
    )


def gather_weights(weights, att_dev, width, both):
    size = weights.shape[-1]
    low = weights.astype(BF)
    groups, chunks = width // size, FF // width
    if banded(weights.shape[0], att_dev, width, size):
        att = lax.all_gather(to_bands(low[:att_dev], width), both, axis=0, tiled=True)
        ffn = lax.all_gather(to_bands(low[att_dev:], width), both, axis=0, tiled=True)
        half = ffn.shape[0] // 2
        return att, ffn[:half].reshape(groups, chunks, size, width), ffn[half:]
    per_dev = weights.shape[0]
    grid = lax.all_gather(low, both, axis=0, tiled=True).reshape(-1, per_dev, size, size)
    att = to_bands(grid[:, :att_dev].reshape(-1, size, size), width)
    tiles = grid[:, att_dev:].reshape(-1, size, size)
    half = tiles.shape[0] // 2
    w_up = to_matrix(tiles[:half], width, FF).reshape(groups, size, chunks, width)
    return att, w_up.transpose(0, 2, 1, 3), to_matrix(tiles[half:], FF, width)


def banded(per_dev, att_dev, width, size):
    wide = width // size
    return att_dev % wide == 0 and (per_dev - att_dev) % wide == 0


def scatter_weight_grads(g_att, g_up, g_down, per_dev, att_dev, both):
    size, width = g_up.shape[2], g_up.shape[3]
    if banded(per_dev, att_dev, width, size):
        ffn = jnp.concatenate([g_up.reshape(-1, width), g_down], axis=0)
        ffn = lax.psum_scatter(ffn, both, scatter_dimension=0, tiled=True)
        att = lax.psum_scatter(g_att, both, scatter_dimension=0, tiled=True)
        return jnp.concatenate([from_bands(att, size), from_bands(ffn, size)], axis=0)
    up = g_up.transpose(0, 2, 1, 3).reshape(width, -1)
    att = from_bands(g_att, size)
    ffn = jnp.concatenate([from_bands(up, size), from_bands(g_down, size)], axis=0)
    stacked = jnp.concatenate(
        [
            att.reshape(-1, att_dev, size, size),
            ffn.reshape(-1, per_dev - att_dev, size, size),
        ],
        axis=1,
    ).reshape(-1, size, size)
    return lax.psum_scatter(stacked, both, scatter_dimension=0, tiled=True)


def per_device(
    tokens,
    cotangent,
    lengths,
    offsets,
    valid_count,
    weights,
    stat_left,
    stat_right,
    root_left,
    root_right,
    projection,
    projection_left,
    projection_right,
    projection_root_left,
    projection_root_right,
    norm_params,
    norm_stat,
):
    both = ("seq", "own")
    size = weights.shape[-1]
    width = tokens.shape[-1]
    rows_here = tokens.shape[1]
    head = width // HEADS
    kp = projection.shape[1]
    blocks = rows_here // SHORT
    peers = lax.axis_size("seq")
    devices = peers * lax.axis_size("own")
    per_dev = weights.shape[0]
    att_dev = 4 * (width // size) ** 2 // devices
    x = tokens[0]
    seq = lax.axis_index("seq")
    side = seq % 2

    swap = [(i, i ^ 1) for i in range(peers)]
    peer_x = lax.ppermute(x, "seq", swap)
    proj_all = lax.all_gather(projection.astype(BF), "own", axis=0, tiled=True)
    w_att, w_up, w_down = gather_weights(weights, att_dev, width, both)

    lens, offs, counts = lengths[0], offsets[0], valid_count[0]
    ends = jnp.cumsum(lens)
    starts = ends - lens
    unit_rows = 2 * rows_here
    unit_start = (seq - side) * rows_here
    unit_end = unit_start + unit_rows
    block_row = unit_start + SHORT * jnp.arange(2 * blocks, dtype=jnp.int32)
    hot = ((starts[None, :] <= block_row[:, None]) & (block_row[:, None] < ends[None, :])).astype(
        jnp.int32
    )
    b_start = jnp.sum(hot * starts[None, :], axis=1)
    b_end = jnp.sum(hot * ends[None, :], axis=1)
    place = block_row - b_start
    column = jnp.sum(hot * offs[None, :], axis=1) + place
    n_valid = jnp.clip(jnp.sum(hot * counts[None, :], axis=1) - place, 0, SHORT)
    is_head = b_start == b_start[0]
    is_tail = b_start == b_start[-1]
    own_at = side * blocks
    peer_at = (1 - side) * blocks
    take = lambda v, at: lax.dynamic_slice_in_dim(v, at, blocks, 0)

    def proj_rows(at):
        col, n = take(column, at), take(n_valid, at)
        rows = jnp.stack(
            [lax.dynamic_slice_in_dim(proj_all, col[b], SHORT, 0) for b in range(blocks)]
        )
        keep = lax.broadcasted_iota(jnp.int32, (blocks, SHORT, 1), 1) < n[:, None, None]
        return jnp.where(keep, rows, jnp.zeros((), BF))

    e_own = proj_rows(own_at)
    e_own_t = e_own.transpose(0, 2, 1)
    e_peer_t = proj_rows(peer_at).transpose(0, 2, 1)
    n_own = take(n_valid, own_at)

    query, keyval, part_own = project(x, w_att, e_own_t, True)
    (part_peer,) = project(peer_x, w_att, e_peer_t, False)
    coef = lambda flag, at: take(flag, at).astype(F32)

    def unit_sum(flag):
        mine = coef(flag, own_at)
        theirs = coef(flag, peer_at)
        total = mine[0] * part_own[0]
        for b in range(1, blocks):
            total = total + mine[b] * part_own[b]
        for b in range(blocks):
            total = total + theirs[b] * part_peer[b]
        return total

    head_sum, tail_sum = unit_sum(is_head), unit_sum(is_tail)
    from_left = lax.ppermute(tail_sum, "seq", [(i, i + 2) for i in range(peers - 2)])
    from_right = lax.ppermute(head_sum, "seq", [(i + 2, i) for i in range(peers - 2)])
    head_cross = (b_start[0] < unit_start).astype(F32)
    tail_cross = (b_end[-1] > unit_end).astype(F32)
    own_head, own_tail = coef(is_head, own_at), coef(is_tail, own_at)
    summary = jnp.stack(
        [
            jnp.where(
                own_head[b] > 0,
                head_sum + head_cross * from_left,
                jnp.where(own_tail[b] > 0, tail_sum + tail_cross * from_right, part_own[b]),
            ).astype(BF)
            for b in range(blocks)
        ]
    )
    mixed, first_sum, row_sums = attend(n_own, query, summary, w_att, x, head)
    (
        result,
        hidden,
        grad_up,
        grad_down,
        first_low,
        grad_first,
        grad_branch,
        grad_mix,
        norm_terms,
    ) = feed(first_sum, w_up, w_down, w_att, cotangent[0], norm_params, 256)
    grad_query, grad_parts = attend_back(query, summary, grad_mix, head)

    row_start = seq * rows_here
    row_end = row_start + rows_here
    o_start, o_end = take(b_start, own_at), take(b_end, own_at)
    same = (o_start[0] == o_start[-1]).astype(F32)
    g_head = grad_parts[0]
    g_tail = grad_parts[-1]
    for b in range(1, blocks):
        g_head = g_head + (o_start[b] == o_start[0]).astype(F32) * grad_parts[b]
    for b in range(blocks - 1):
        g_tail = g_tail + (o_start[b] == o_start[-1]).astype(F32) * grad_parts[b]
    low_head, low_tail = g_head.astype(BF), g_tail.astype(BF)
    left_sum = jnp.zeros_like(g_head)
    right_sum = jnp.zeros_like(g_head)
    for far in (1, 2):
        tail_far = lax.ppermute(low_tail, "seq", [(i, i + far) for i in range(peers - far)])
        head_far = lax.ppermute(low_head, "seq", [(i + far, i) for i in range(peers - far)])
        reach = (far - 1) * rows_here
        left_sum = left_sum + (o_start[0] < row_start - reach).astype(F32) * tail_far.astype(F32)
        right_sum = right_sum + (o_end[-1] > row_end + reach).astype(F32) * head_far.astype(F32)
    at_head = (o_start == o_start[0]).astype(F32)
    grad_summary = jnp.stack(
        [
            jnp.where(
                at_head[b] > 0, g_head + left_sum + same * right_sum, g_tail + right_sum
            ).astype(BF)
            for b in range(blocks)
        ]
    )
    own_size = lax.axis_size("own")
    fused = own_size == 4 and peers == 8 and banded(per_dev, att_dev, width, size)
    gtype = BF if fused else F32
    g_up = outer_up(first_low, grad_up, size, gtype)
    g_down = outer_rows(hidden, grad_down, gtype, "outer_down")
    g_out = outer_rows(mixed, grad_branch, gtype, "outer_out")
    g_query = outer_rows(x, grad_query, gtype, "outer_query")
    grad_keyval, grad_e, grad_input = back(e_own, keyval, grad_summary, grad_query, w_att, grad_first)
    g_key = outer_rows(x, grad_keyval[:, :width], gtype, "outer_key")
    g_value = outer_rows(x, grad_keyval[:, width:], gtype, "outer_value")
    g_att = [g_query, g_key, g_value, g_out]

    part_rows = projection.shape[0]
    grad_proj = jnp.zeros((proj_all.shape[0], kp), F32)
    keep_e = lax.broadcasted_iota(jnp.int32, (blocks, SHORT, 1), 1) < n_own[:, None, None]
    grad_e = jnp.where(keep_e, grad_e, 0.0)
    own_col = take(column, own_at)
    for b in range(blocks):
        current = lax.dynamic_slice_in_dim(grad_proj, own_col[b], SHORT, 0)
        grad_proj = lax.dynamic_update_slice_in_dim(grad_proj, current + grad_e[b], own_col[b], 0)
    valid_here = jnp.sum(n_own).astype(F32)
    extra = jnp.concatenate(
        [
            norm_terms.reshape(-1, kp),
            row_sums.reshape(-1, kp),
            jnp.full((1, kp), 1.0 / kp, F32) * valid_here,
        ],
        axis=0,
    )
    n_norm = 4 * width // kp
    n_row = 2 * width // kp
    if fused:
        extra = jnp.pad(extra, ((0, devices - extra.shape[0]), (0, 0)))[:, None, :]
        extra = jnp.pad(extra, ((0, 0), (0, 7), (0, 0)))
        shares = grad_proj.reshape(own_size, peers, part_rows // peers, kp).swapaxes(0, 1)
        shares = shares.reshape(devices, part_rows // peers, kp)
        ffn_a, ffn_b, att, proj_parts, rows = reduce_all(
            g_att, g_up, g_down, jnp.concatenate([shares, extra], axis=1), peers
        )
        owned = jnp.concatenate(
            [from_bands(att, size), from_bands(ffn_a, size), from_bands(ffn_b, size)], axis=0
        )
        proj_grad = proj_parts.reshape(part_rows, kp)
        totals = rows[..., 0, :].transpose(2, 3, 0, 1, 4).reshape(devices, kp)
    else:
        owned = scatter_weight_grads(
            jnp.concatenate(g_att, axis=0), g_up, g_down, per_dev, att_dev, both
        )
        packed = jnp.concatenate([grad_proj, extra], axis=0)
        packed = lax.psum(jnp.pad(packed, ((0, -packed.shape[0] % 16), (0, 0))), both)
        proj_grad = lax.dynamic_slice_in_dim(
            packed, lax.axis_index("own") * part_rows, part_rows, 0
        )
        totals = packed[grad_proj.shape[0] :]
    norm_grad = totals[:n_norm].reshape(4, width)
    row_total = totals[n_norm : n_norm + n_row].reshape(2, width).sum(axis=1)
    valid_total = totals[n_norm + n_row].sum()
    residual_rms = jnp.sqrt(row_total / (valid_total * width))
    left_new, right_new, weights_new = shampoo(
        owned, stat_left, stat_right, root_left, root_right, weights
    )
    proj_left_new, proj_right_new, proj_blocks = shampoo(
        proj_grad.reshape(-1, kp, kp),
        projection_left,
        projection_right,
        projection_root_left,
        projection_root_right,
        projection.reshape(-1, kp, kp),
    )
    stat_new = decay * norm_stat + (1.0 - decay) * norm_grad * norm_grad
    norm_new = norm_params - rate_norm * norm_grad * lax.rsqrt(stat_new)
    return (
        result[None],
        grad_input[None],
        owned,
        left_new,
        right_new,
        weights_new,
        proj_grad,
        proj_left_new,
        proj_right_new,
        proj_blocks.reshape(part_rows, kp),
        norm_grad,
        stat_new,
        norm_new,
        residual_rms,
    )


def solution(mesh):
    pack = P("own", "seq", None)
    table = P("own", None)
    tile = P(("seq", "own"), None, None)
    proj = P("own", None, None)
    return jax.shard_map(
        per_device,
        mesh=mesh,
        in_specs=(pack, pack, table, table, table)
        + (tile,) * 5
        + (table, proj, proj, proj, proj, P(), P()),
        out_specs=(pack, pack) + (tile,) * 4 + (table, proj, proj, table, P(), P(), P(), P()),
        check_vma=False,
    )
```

time: 1560 us -> 508 us (0.33)
  waiting for transfers between devices: 776 us -> 117 us
  local copies, waits for them, and re-layouts: 280 us -> 42 us
  Pallas kernels: 0 us -> 228 us
  matrix products: 213 us -> 18.9 us
  other arithmetic: 141 us -> 38.3 us
  blocking collectives: 94 us -> 0 us
  starting transfers between devices: 0.33 us -> 21.5 us
  loops' own time: 15.9 us -> 0 us
    reduce_scatter x1 -> x0, waiting for transfers between devices: 349 us -> none  [per_device(): lax.psum_scatter(stacked, ('seq', 'own'), scatter_dimension=0, tiled=True)]
    all_gather x6 -> x3, waiting for transfers between devices: 397 us -> 64.2 us  [the longest x1 64 us: gather_weights(): lax.all_gather(to_bands(low[:att_dev], width), both, axis=0, tiled=True)]
    pallas_call x0 -> x13, Pallas kernels: none -> 228 us  [the longest x1 101 us: reduce_all(): pl.pallas_call(functools.partial(reduce_body, depth, half, n_src, keep),...]
    dot_general x25 -> x0, matrix products: 192 us -> none  [the longest x1 35.9 us: per_device(): up_value = jnp.dot(first_low, w_up, preferred_element_type=jnp.float32)]
    reshape x14 -> x12, local copies, waits for them, and re-layouts: 92.6 us -> 4.22 us  [the longest x6 1.78 us: from_bands(): bands.reshape(rows // size, size, cols // size, size).transpose(0, 2, 1, 3)]
    psum x1 -> x0, blocking collectives: 60.8 us -> none  [per_device(): proj_total, norm_grad = lax.psum((grad_proj, norm_terms), ('seq', 'own'))]
    select_n x24 -> x2, other arithmetic: 58.6 us -> 2.42 us  [the longest x1 1.42 us: per_device(): grad_e = jnp.where(keep_e, grad_e, 0.0)]
    ppermute x0 -> x7, waiting for transfers between devices: none -> 52.9 us  [the longest x1 47.2 us: per_device(): lax.ppermute(tail_sum, 'seq', [(i, i + 2) for i in range(peers - 2)])]
  transfers between devices with their start and end apart: 8 -> 10, of which waited for: 7 -> 5; matrix products, arithmetic and copies ran while one was open for 20% -> 7% of each run, Pallas kernels for 0% -> 11%
where the time goes in v1:
time: 508 us; the launch traced here: 500 us
  Pallas kernels  228 us (45%)
  waiting for transfers between devices  117 us (23%)
  local copies, waits for them, and re-layouts  42 us (8%)
  other arithmetic  38.3 us (8%)
  between operations  34.2 us (7%)
  starting transfers between devices  21.5 us (4%)
  matrix products  18.9 us (4%)
    pallas_call x1, Pallas kernels, reduce_all(): pl.pallas_call(functools.partial(reduce_body, depth, half, n_src, keep),...  101 us
    all_gather x1, waiting for transfers between devices, gather_weights(): lax.all_gather(to_bands(low[:att_dev], width), both, axis=0, tiled=True)  64 us
    ppermute x1, waiting for transfers between devices, per_device(): lax.ppermute(tail_sum, 'seq', [(i, i + 2) for i in range(peers - 2)])  47.2 us
    pallas_call x1, Pallas kernels, feed(): pl.pallas_call(functools.partial(feed_body, chunks), grid=(rows // tile,)...  34.7 us
    pallas_call x5, Pallas kernels, outer_rows(): pl.pallas_call(functools.partial(outer_body, False), grid=(chunks,), in_s...  26.9 us
    pallas_call x2, Pallas kernels, project(): pl.pallas_call(functools.partial(project_body, width, with_query), grid=(...  17 us
    pallas_call x1, Pallas kernels, attend_back(): pl.pallas_call(functools.partial(attend_back_body, width, head, kp), grid...  15.6 us
    pallas_call x1, Pallas kernels, attend(): pl.pallas_call(functools.partial(attend_body, width, head, kp), grid_spec...  12.7 us
  transfers between devices with their start and end apart: 10, of which 5 were waited for; matrix products, arithmetic and copies ran while one was open for 7% of the time, Pallas kernels for 11%

profile of v1, /device:TPU:9, one launch (start us, length us, event | category | flops | bytes accessed | tf_op | source)
XLA Modules:
  0.0 499.9 jit_solution(9263941219631760502)
XLA Ops:
  32.3 64.0 %all-gather.4.cloned.1.call-done.w_ref.wo_ref = bf16[3072,768]{1,0:T(8,128)(2,1)} async-done(((bf16[96,768]{1,0:T(8,128)(2,1)}), bf16[3072,768]{1,0:T(8,128)(2,1)}) %all-gather.4.cloned.1.call-update) | async-done | bytes 4718608 | tf_op jit(solution)/shard_map/all_gather | solution.py:769
  96.3 9.3 %project.1 = (bf16[1024,768]{1,0:T(8,128)(2,1)}, bf16[1024,1536]{1,0:T(8,128)(2,1)}, f32[2,256,1536]{2,1,0:T(8,128)}) custom-call(bf16[1024,768]{1,0:T(8,128)(2,1)} %bitcast.5.x_ref.l_ref, bf16[3072,768]{1,0:T(8,128)(2,1)} %all-gather.4.cloned.1.call-done.w_ref.wo_ref, bf16[2,256,512]{2,1,0:T(8,128)(2,1)} %copy.57.e_ref), custom_call_target="tpu_custom_call" | custom-call | flops 3623878656 | bytes 12000000 | tf_op jit(solution)/shard_map/project/pallas_call | solution.py:82
  105.6 7.7 %project_peer.1 = f32[2,256,1536]{2,1,0:T(8,128)} custom-call(bf16[1024,768]{1,0:T(8,128)(2,1)} %collective-permute-done.x_ref, bf16[3072,768]{1,0:T(8,128)(2,1)} %all-gather.4.cloned.1.call-done.w_ref.wo_ref, bf16[2,256,512]{2,1,0:T(8,128)(2,1)} %copy.58.e_ref), custom_call_target="tpu_custom_call" | custom-call | flops 3623878656 | bytes 12000000 | tf_op jit(solution)/shard_map/project_peer/pallas_call | solution.py:82
  113.3 9.8 %bitcast_add_fusion.1 = (f32[256,1536]{1,0:T(8,128)S(1)}, f32[256,1536]{1,0:T(8,128)}) fusion(f32[2,256,1536]{2,1,0:T(8,128)} %project_peer.1, f32[2,256,1536]{2,1,0:T(8,128)} %get-tuple-element.40, f32[]{:T(128)} %bitcast.33, f32[]{:T(128)} %bitcast.31, f32[]{:T(128)} %bitcast.30, f32[]{:T(128)} %bitcast.29, f32[]{:T(128)} %bitcast.26, f32[]{:T(128)} %bitcast.19, ...), kind=kLoop, calls=%fused_computation.7 | loop fusion | flops 5505024 | bytes 9437216 | tf_op jit(solution)/shard_map/add | solution.py:891
  125.4 4.0 collective-permute-start.2
  147.5 47.2 %collective-permute-done.1 = f32[256,1536]{1,0:T(8,128)} collective-permute-done((f32[256,1536]{1,0:T(8,128)S(1)}, f32[256,1536]{1,0:T(8,128)}, u32[]{:S(2)}, u32[]{:S(2)}) %collective-permute-start.1) | collective-permute-done | bytes 1572896 | tf_op jit(solution)/shard_map/ppermute | solution.py:895
  195.6 4.6 fusion.18
  201.5 12.7 %attend.1 = (bf16[1024,768]{1,0:T(8,128)(2,1)}, f32[1024,768]{1,0:T(8,128)}, f32[2,768]{1,0:T(2,128)}) custom-call(s32[2]{0:T(128)} %copy-done.21, bf16[1024,768]{1,0:T(8,128)(2,1)} %get-tuple-element.39.q_ref, bf16[2,256,1536]{2,1,0:T(8,128)(2,1)} %pad_maximum_fusion.1.s_ref, bf16[3072,768]{1,0:T(8,128)(2,1)} %all-gather.4.cloned.1.call-done.w_ref.wo_ref, ...), custom_call_target="tpu_custom_call" | custom-call | flops 2818572288 | bytes 10000000 | tf_op jit(solution)/shard_map/attend/pallas_call | solution.py:153
  214.9 8.0 %fusion.29 = (bf16[3072,768]{1,0:T(8,128)(2,1)}, bf16[3072,768]{1,0:T(8,128)(2,1)}) fusion(bf16[6144,768]{1,0:T(8,128)(2,1)} %all-gather.8.cloned.1.call-done), kind=kLoop, calls=%fused_computation.95 | loop fusion | bytes 18874368 | tf_op jit(solution)/shard_map/slice | solution.py:772
  223.0 34.7 %feed.1 = (bf16[1024,768]{1,0:T(8,128)(2,1)}, bf16[1024,3072]{1,0:T(8,128)(2,1)}, bf16[1024,3072]{1,0:T(8,128)(2,1)}, bf16[1024,768]{1,0:T(8,128)(2,1)}, bf16[10...) custom-call(f32[1024,768]{1,0:T(8,128)} %get-tuple-element.41.first_, ...), custom_call_target="tpu_custom_call" | custom-call | flops 19327352832 | bytes 30000000 | tf_op jit(solution)/shard_map/feed/pallas_call | solution.py:270
  257.7 15.6 %attend_back.1 = (bf16[1024,768]{1,0:T(8,128)(2,1)}, f32[2,256,1536]{2,1,0:T(8,128)}) custom-call(bf16[1024,768]{1,0:T(8,128)(2,1)} %get-tuple-element.39.q_ref, bf16[2,256,1536]{2,1,0:T(8,128)(2,1)} %pad_maximum_fusion.1.s_ref, bf16[1024,768]{1,0:T(8,128)(2,1)} %get-tuple-element.44.g_ref), custom_call_target="tpu_custom_call" | custom-call | flops 3221225472 | bytes 10000000 | tf_op jit(solution)/shard_map/attend_back/pallas_call | solution.py:341
  278.7 4.9 collective-permute-start.4
  283.6 3.7 collective-permute-start.5
  289.4 4.3 outer_query.1
  293.7 4.3 outer_out.1
  298.0 9.4 %outer_down.1 = bf16[3072,768]{1,0:T(8,128)(2,1)} custom-call(bf16[1024,3072]{1,0:T(8,128)(2,1)} %get-tuple-element.51.l_ref, bf16[1024,768]{1,0:T(8,128)(2,1)} %get-tuple-element.52.r_ref), custom_call_target="tpu_custom_call" | custom-call | flops 4831838208 | bytes 20000000 | tf_op jit(solution)/shard_map/outer_down/pallas_call | solution.py:390
  307.4 9.2 %outer_up.1 = bf16[8,4,96,768]{3,2,1,0:T(8,128)(2,1)} custom-call(bf16[1024,768]{1,0:T(8,128)(2,1)} %get-tuple-element.49.l_ref, bf16[1024,3072]{1,0:T(8,128)(2,1)} %get-tuple-element.50.r_ref), custom_call_target="tpu_custom_call" | custom-call | flops 4831838208 | bytes 20000000 | tf_op jit(solution)/shard_map/outer_up/pallas_call | solution.py:372
  316.7 4.7 collective-permute-done.6
  321.4 3.8 fusion.16
  326.6 11.0 %back.1 = (bf16[1024,1536]{1,0:T(8,128)(2,1)}, f32[2,512,256]{2,1,0:T(8,128)}, f32[1024,768]{1,0:T(8,128)}) custom-call(bf16[2,512,256]{2,1,0:T(8,128)(2,1)} %maximum_select_fusion.e_ref, bf16[1024,1536]{1,0:T(8,128)(2,1)} %get-tuple-element.43.kv_ref, bf16[2,256,1536]{2,1,0:T(8,128)(2,1)} %pad_maximum_fusion.2.s_ref, ...), custom_call_target="tpu_custom_call" | custom-call | flops 5234491392 | bytes 20000000 | tf_op jit(solution)/shard_map/back/pallas_call | solution.py:423
  352.9 4.3 outer_key.1
  357.2 4.5 outer_value.1
  363.3 100.9 %reduce_all.1 = (f32[96,768]{1,0:T(8,128)}, f32[96,768]{1,0:T(8,128)}, f32[96,768]{1,0:T(8,128)}, f32[4,2,64,256]{3,2,1,0:T(8,128)}, f32[2,2,4,2,8,256]{5,4,3,2,1,0:T(8,128)}) custom-call(bf16[2,4,2,2,96,768]{5,4,3,2,1,0:T(8,128)(2,1)} %bitcast.215, bf16[2,4,2,2,96,768]{5,4,3,2,1,0:T(8,128)(2,1)} %bitcast.214, bf16[4,2,96,768]{3,2,1,0:T(8,128)(2,1)} %bitcast.223, ...), custom_call_target="tpu_custom_call" | custom-call | tf_op jit(solution)/shard_map/reduce_all/pallas_call | solution.py:712
  476.5 4.9 fusion.10
  (154 shorter events, 78.2 us)
Async XLA Ops:
  7.2 461.1 %copy-start = (f32[24,96,96]{2,1,0:T(8,128)S(1)}, f32[24,96,96]{2,1,0:T(8,128)}, u32[]{:S(2)}) copy-start(f32[24,96,96]{2,1,0:T(8,128)} %param.26) | copy-start | bytes 2654212
  7.2 21.2 %all-gather.6.cloned.1.call-start = ((), (), s32[]{:S(2)}) async-start(), calls=%async_computation.1 | async-start | bytes 1310720 | tf_op jit(solution)/shard_map/all_gather | solution.py:843
  9.1 87.1 %all-gather.4.cloned.1.call-start = ((), (), s32[]{:S(2)}) async-start(), calls=%async_computation | async-start | bytes 4866048 | tf_op jit(solution)/shard_map/all_gather | solution.py:769
  10.6 3.5 copy-start.24
  10.6 3.7 copy-start.22
  10.7 3.7 copy-start.23
  11.5 203.4 %all-gather.8.cloned.1.call-start = ((), (), s32[]{:S(2)}) async-start(), calls=%async_computation.2 | async-start | bytes 9732096 | tf_op jit(solution)/shard_map/all_gather | solution.py:770
  12.8 92.7 %collective-permute-start = (bf16[1024,768]{1,0:T(8,128)(2,1)}, bf16[1024,768]{1,0:T(8,128)(2,1)}, u32[]{:S(2)}, u32[]{:S(2)}) collective-permute-start(bf16[1024,768]{1,0:T(8,128)(2,1)} %bitcast.5.x_ref.l_ref), channel_id=1, source_target_pairs={{0,4},{4,0},{8,12},{12,8},{16,20},{20,16},{24,28},{28,24},{1,5},{5... | collective-permute-start | bytes 4718600 | tf_op jit(solution)/shard_map/ppermute | solution.py:842
  123.0 71.7 %collective-permute-start.1 = (f32[256,1536]{1,0:T(8,128)S(1)}, f32[256,1536]{1,0:T(8,128)}, u32[]{:S(2)}, u32[]{:S(2)}) collective-permute-start(f32[256,1536]{1,0:T(8,128)S(1)} %get-tuple-element.121), channel_id=1, source_target_pairs={{0,8},{4,12},{8,16},{12,20},{16,24},{20,28},{1,9},{5,13},{9,17},{1... | collective-permute-start | bytes 4718600 | tf_op jit(solution)/shard_map/ppermute | solution.py:895
  125.4 70.2 %collective-permute-start.2 = (f32[256,1536]{1,0:T(8,128)}, f32[256,1536]{1,0:T(8,128)}, u32[]{:S(2)}, u32[]{:S(2)}) collective-permute-start(f32[256,1536]{1,0:T(8,128)} %get-tuple-element.122), channel_id=1, source_target_pairs={{8,0},{12,4},{16,8},{20,12},{24,16},{28,20},{9,1},{13,5},{17,9},{2... | collective-permute-start | bytes 4718600 | tf_op jit(solution)/shard_map/ppermute | solution.py:896
  273.3 15.9 %copy-start.18 = (f32[4,768]{1,0:T(4,128)S(1)}, f32[4,768]{1,0:T(4,128)}, u32[]{:S(2)}) copy-start(f32[4,768]{1,0:T(4,128)} %get-tuple-element.57) | copy-start | bytes 36868
  275.5 41.1 %collective-permute-start.3 = (bf16[256,1536]{1,0:T(8,128)(2,1)S(1)}, bf16[256,1536]{1,0:T(8,128)(2,1)}, u32[]{:S(2)}, u32[]{:S(2)}) collective-permute-start(bf16[256,1536]{1,0:T(8,128)(2,1)S(1)} %get-tuple-element.125), channel_id=1, source_target_pairs={{0,4},{4,8},{8,12},{12,16},{16,20},{20,24},{24,28},{1,5},{5,9},{9,... | collective-permute-start | bytes 2359304 | tf_op jit(solution)/shard_map/ppermute | solution.py:938
  278.7 38.0 %collective-permute-start.4 = (bf16[256,1536]{1,0:T(8,128)(2,1)S(1)}, bf16[256,1536]{1,0:T(8,128)(2,1)}, u32[]{:S(2)}, u32[]{:S(2)}) collective-permute-start(bf16[256,1536]{1,0:T(8,128)(2,1)S(1)} %get-tuple-element.125), channel_id=1, source_target_pairs={{0,8},{4,12},{8,16},{12,20},{16,24},{20,28},{1,9},{5,13},{9,17},{1... | collective-permute-start | bytes 2359304 | tf_op jit(solution)/shard_map/ppermute | solution.py:938
  283.6 33.1 %collective-permute-start.5 = (bf16[256,1536]{1,0:T(8,128)(2,1)S(1)}, bf16[256,1536]{1,0:T(8,128)(2,1)}, u32[]{:S(2)}, u32[]{:S(2)}) collective-permute-start(bf16[256,1536]{1,0:T(8,128)(2,1)S(1)} %get-tuple-element.126), channel_id=1, source_target_pairs={{4,0},{8,4},{12,8},{16,12},{20,16},{24,20},{28,24},{5,1},{9,5},{13... | collective-permute-start | bytes 2359304 | tf_op jit(solution)/shard_map/ppermute | solution.py:939
  287.3 34.1 %collective-permute-start.6 = (bf16[256,1536]{1,0:T(8,128)(2,1)S(1)}, bf16[256,1536]{1,0:T(8,128)(2,1)}, u32[]{:S(2)}, u32[]{:S(2)}) collective-permute-start(bf16[256,1536]{1,0:T(8,128)(2,1)S(1)} %get-tuple-element.126), channel_id=1, source_target_pairs={{8,0},{12,4},{16,8},{20,12},{24,16},{28,20},{9,1},{13,5},{17,9},{2... | collective-permute-start | bytes 2359304 | tf_op jit(solution)/shard_map/ppermute | solution.py:939
  357.2 4.5 copy-start.3
  464.3 3.3 copy-start.15
  468.2 13.1 %copy-start.1 = (f32[24,96,96]{2,1,0:T(8,128)}, f32[24,96,96]{2,1,0:T(8,128)S(1)}, u32[]{:S(2)}) copy-start(f32[24,96,96]{2,1,0:T(8,128)S(1)} %pad_maximum_fusion.3) | copy-start | bytes 2654212
  476.5 4.9 copy-start.9
  481.4 3.1 copy-start.2
  481.4 3.1 copy-start.10
  487.4 3.3 copy-start.7
  487.4 3.3 copy-start.13
  488.9 4.1 copy-start.17
  (12 other events, 26.6 us)
Sparse Core Ops, SparseCore 0:
  10.1 18.2 all-gather.5
  31.9 64.3 all-gather.3
  99.7 101.1 all-gather.7

commit v2 on v1

--- a/solution.py
+++ b/solution.py
@@ -215,6 +215,8 @@
 ):
     step = pl.program_id(0)
     rows, width = first_ref.shape
+    deep = w2_ref.shape[0] // chunks
+    down_rows = lambda c: w2_ref[pl.ds(c * deep, deep)].reshape(width, width)
     normed_one, inverse_one = normalize(first_ref[...])
     first_norm = normed_one * np_ref[0:1, :] + np_ref[1:2, :]
     first_low = first_norm.astype(BF)
@@ -228,7 +230,7 @@
         slope_ref[:, cols] = cumulative + u * density
         hidden = (u * cumulative).astype(BF)
         hid_ref[:, cols] = hidden
-        second = second + dot(hidden, w2_ref[pl.ds(c * width, width), :])
+        second = second + dot(hidden, down_rows(c))
     normed_two, inverse_two = normalize(second)
     out_ref[...] = (normed_two * np_ref[2:3, :] + np_ref[3:4, :]).astype(BF)
     grad_out = cot_ref[...].astype(F32)
@@ -240,7 +242,7 @@
     grad_first_norm = grad_second
     for c in range(chunks):
         cols = pl.ds(c * width, width)
-        grad_hidden = dot_t(down, w2_ref[pl.ds(c * width, width), :])
+        grad_hidden = dot_t(down, down_rows(c))
         up = (grad_hidden * slope_ref[:, cols]).astype(BF)
         up_ref[:, cols] = up
         grad_first_norm = grad_first_norm + dot_t(up, w1_ref[:, c].reshape(width, width))
@@ -262,9 +264,10 @@
         ng_ref[...] += sums
 
 
-def feed(first_sum, w_up, w_down, w_att, cotangent, norm_params, tile):
+def feed(first_sum, w_ffn, w_att, cotangent, norm_params, tile):
     rows, width = first_sum.shape
-    chunks = w_up.shape[1]
+    groups, chunks, size, _ = w_ffn.shape
+    groups = groups // 2
     ff = chunks * width
     row = lambda i: (i, 0)
     return pl.pallas_call(
@@ -272,8 +275,8 @@
         grid=(rows // tile,),
         in_specs=[
             vspec((tile, width), row),
-            vspec(w_up.shape, lambda i: (0, 0, 0, 0), True),
-            vspec((ff, width), lambda i: (0, 0), True),
+            vspec((groups, chunks, size, width), lambda i: (0, 0, 0, 0), True),
+            vspec((groups, chunks, size, width), lambda i: (1, 0, 0, 0), True),
             vspec((width, width), lambda i: (3, 0), True),
             vspec((tile, width), row),
             vspec(norm_params.shape, lambda i: (0, 0)),
@@ -304,7 +307,7 @@
         compiler_params=params(),
         cost_estimate=cost(2 * rows * width * ff * 4, 30e6, rows * ff * 2),
         name="feed",
-    )(first_sum, w_up, w_down, w_att, cotangent, norm_params)
+    )(first_sum, w_ffn, w_ffn, w_att, cotangent, norm_params)
 
 
 def attend_back_body(width, head, kp, q_ref, s_ref, g_ref, dq_ref, ds_ref):
@@ -726,6 +729,112 @@
     )(*sources)
 
 
+def gather_body(depth, half, band_ref, proj_ref, out_ref, pout_ref, send, recv, local):
+    seq, mine = lax.axis_index("seq"), lax.axis_index("own")
+    z, y, x, c = seq // 2, seq % 2, mine // 2, mine % 2
+    core = (seq, 2 * x + (1 - c))
+    along_x = (seq, 2 * (1 - x) + c)
+    along_y = (2 * z + (1 - y), mine)
+    order = [1, 3, 2]
+    along_z = [(2 * lax.rem(z + d, depth) + y, mine) for d in order]
+    barrier = pltpu.get_barrier_semaphore()
+    partners = [core, along_x, along_y] + along_z
+    for partner in partners:
+        pl.semaphore_signal(barrier, inc=1, device_id=partner, device_id_type=MESH_ID)
+    pl.semaphore_wait(barrier, len(partners))
+
+    sent = []
+
+    def push(src, dst, partner):
+        at = len(sent)
+        copy = pltpu.make_async_remote_copy(
+            src_ref=src,
+            dst_ref=dst,
+            send_sem=send.at[at],
+            recv_sem=recv.at[at],
+            device_id=partner,
+            device_id_type=MESH_ID,
+        )
+        copy.start()
+        sent.append(copy)
+        return copy
+
+    keep = pltpu.make_async_copy(band_ref, out_ref.at[z, y, x, c], local.at[0])
+    keep.start()
+    keep_p = pltpu.make_async_copy(proj_ref, pout_ref.at[x, c], local.at[1])
+    keep_p.start()
+    mine_at = out_ref.at[z, y, x, c]
+    from_z = [push(band_ref, mine_at, there) for there in along_z]
+    from_x = [push(band_ref, mine_at, along_x)]
+    from_y = [push(band_ref, mine_at, along_y)]
+    proj_x = push(proj_ref, pout_ref.at[x, c], along_x)
+    last = [push(band_ref, mine_at, core), push(proj_ref, pout_ref.at[x, c], core)]
+    planes = [z]
+    for k in range(depth - 1):
+        from_z[k].wait_recv()
+        plane = lax.rem(z + depth - order[k], depth)
+        planes.append(plane)
+        slab = out_ref.at[plane, y, x, c]
+        from_x.append(push(slab, slab, along_x))
+        from_y.append(push(slab, slab, along_y))
+        last.append(push(slab, slab, core))
+    low, high = pl.ds(0, half), pl.ds(half, half)
+    cross = []
+    for k in range(depth):
+        plane = planes[k]
+        from_x[k].wait_recv()
+        slab = out_ref.at[plane, y, 1 - x, c]
+        part = out_ref.at[plane, y, 1 - x, c, low, :]
+        cross_y = push(part, part, along_y)
+        last.append(push(slab, slab, core))
+        from_y[k].wait_recv()
+        slab = out_ref.at[plane, 1 - y, x, c]
+        part = out_ref.at[plane, 1 - y, x, c, high, :]
+        cross.append((cross_y, push(part, part, along_x)))
+        last.append(push(slab, slab, core))
+        if k == 0:
+            proj_x.wait_recv()
+            slab = pout_ref.at[1 - x, c]
+            last.append(push(slab, slab, core))
+    for k in range(depth):
+        for copy in cross[k]:
+            copy.wait_recv()
+        slab = out_ref.at[planes[k], 1 - y, 1 - x, c]
+        last.append(push(slab, slab, core))
+    for copy in last:
+        copy.wait_recv()
+    keep.wait()
+    keep_p.wait()
+    for copy in sent:
+        copy.wait_send()
+
+
+def gather_bands(band, proj, peers):
+    depth = peers // 2
+    size, width = band.shape
+    messages = (depth - 1) + 3 + 2 + 3 * (depth - 1) + 4 * depth + 1 + depth
+    vmem = pl.BlockSpec(memory_space=pltpu.VMEM)
+    return pl.pallas_call(
+        functools.partial(gather_body, depth, size // 2),
+        in_specs=[vmem] * 2,
+        out_specs=[vmem] * 2,
+        out_shape=[
+            jax.ShapeDtypeStruct((depth, 2, 2, 2, size, width), BF),
+            jax.ShapeDtypeStruct((2, 2) + proj.shape, BF),
+        ],
+        scratch_shapes=[
+            pltpu.SemaphoreType.DMA((messages,)),
+            pltpu.SemaphoreType.DMA((messages,)),
+            pltpu.SemaphoreType.DMA((2,)),
+        ],
+        compiler_params=pltpu.CompilerParams(
+            collective_id=2, has_side_effects=True, vmem_limit_bytes=VMEM_LIMIT
+        ),
+        cost_estimate=cost(1e9, 90e6),
+        name="gather_bands",
+    )(band, proj)
+
+
 def shampoo(grad, left, right, root_left, root_right, weight):
     new_left = decay * left + (1.0 - decay) * jnp.einsum(
         "tij,tkj->tik", grad, grad, precision=highest
@@ -761,22 +870,29 @@
     )
 
 
-def gather_weights(weights, att_dev, width, both):
+def gather_weights(weights, projection, att_dev, width, both, fused, peers):
     size = weights.shape[-1]
     low = weights.astype(BF)
     groups, chunks = width // size, FF // width
     if banded(weights.shape[0], att_dev, width, size):
-        att = lax.all_gather(to_bands(low[:att_dev], width), both, axis=0, tiled=True)
         ffn = lax.all_gather(to_bands(low[att_dev:], width), both, axis=0, tiled=True)
-        half = ffn.shape[0] // 2
-        return att, ffn[:half].reshape(groups, chunks, size, width), ffn[half:]
+        band = to_bands(low[:att_dev], width)
+        if fused:
+            att, proj = gather_bands(band, projection.astype(BF), peers)
+            att, proj = att.reshape(-1, width), proj.reshape(-1, projection.shape[1])
+        else:
+            att = lax.all_gather(band, both, axis=0, tiled=True)
+            proj = lax.all_gather(projection.astype(BF), "own", axis=0, tiled=True)
+        return att, ffn.reshape(2 * groups, chunks, size, width), proj
     per_dev = weights.shape[0]
+    proj = lax.all_gather(projection.astype(BF), "own", axis=0, tiled=True)
     grid = lax.all_gather(low, both, axis=0, tiled=True).reshape(-1, per_dev, size, size)
     att = to_bands(grid[:, :att_dev].reshape(-1, size, size), width)
     tiles = grid[:, att_dev:].reshape(-1, size, size)
     half = tiles.shape[0] // 2
     w_up = to_matrix(tiles[:half], width, FF).reshape(groups, size, chunks, width)
-    return att, w_up.transpose(0, 2, 1, 3), to_matrix(tiles[half:], FF, width)
+    w_down = to_matrix(tiles[half:], FF, width).reshape(groups, chunks, size, width)
+    return att, jnp.concatenate([w_up.transpose(0, 2, 1, 3), w_down], axis=0), proj
 
 
 def banded(per_dev, att_dev, width, size):
@@ -840,8 +956,11 @@
 
     swap = [(i, i ^ 1) for i in range(peers)]
     peer_x = lax.ppermute(x, "seq", swap)
-    proj_all = lax.all_gather(projection.astype(BF), "own", axis=0, tiled=True)
-    w_att, w_up, w_down = gather_weights(weights, att_dev, width, both)
+    own_size = lax.axis_size("own")
+    fused = own_size == 4 and peers == 8 and banded(per_dev, att_dev, width, size)
+    w_att, w_ffn, proj_all = gather_weights(
+        weights, projection, att_dev, width, both, fused, peers
+    )
 
     lens, offs, counts = lengths[0], offsets[0], valid_count[0]
     ends = jnp.cumsum(lens)
@@ -918,7 +1037,7 @@
         grad_branch,
         grad_mix,
         norm_terms,
-    ) = feed(first_sum, w_up, w_down, w_att, cotangent[0], norm_params, 256)
+    ) = feed(first_sum, w_ffn, w_att, cotangent[0], norm_params, 256)
     grad_query, grad_parts = attend_back(query, summary, grad_mix, head)
 
     row_start = seq * rows_here
@@ -949,8 +1068,6 @@
             for b in range(blocks)
         ]
     )
-    own_size = lax.axis_size("own")
-    fused = own_size == 4 and peers == 8 and banded(per_dev, att_dev, width, size)
     gtype = BF if fused else F32
     g_up = outer_up(first_low, grad_up, size, gtype)
     g_down = outer_rows(hidden, grad_down, gtype, "outer_down")

time: 508 us -> 454 us (0.89)
  waiting for transfers between devices: 117 us -> 19.5 us
  Pallas kernels: 228 us -> 282 us
  local copies, waits for them, and re-layouts: 42 us -> 34.4 us
    all_gather x2 -> x0, waiting for transfers between devices: 64.2 us -> none  [the longest x1 64 us: gather_weights(): lax.all_gather(to_bands(low[:att_dev], width), both, axis=0, tiled=True)]
    pallas_call x0 -> x1, Pallas kernels: none -> 53.7 us  [gather_bands(): pl.pallas_call(functools.partial(gather_body, depth, size // 2), in_specs...]
    ppermute x1, waiting for transfers between devices: 47.2 us -> 13.1 us  [per_device(): lax.ppermute(tail_sum, 'seq', [(i, i + 2) for i in range(peers - 2)])]
    slice x1 -> x0, local copies, waits for them, and re-layouts: 8.05 us -> none  [gather_weights(): return (att, ffn[:half].reshape(groups, chunks, size, width), ffn[half:])]
  transfers between devices with their start and end apart: 10 -> 8, of which waited for: 5 -> 3; matrix products, arithmetic and copies ran while one was open for 7% -> 8% of each run, Pallas kernels for 11% -> 25%
where the time goes in v2:
time: 454 us; the launch traced here: 446 us
  Pallas kernels  282 us (62%)
  other arithmetic  37 us (8%)
  between operations  34.5 us (8%)
  local copies, waits for them, and re-layouts  34.4 us (8%)
  starting transfers between devices  20.5 us (5%)
  waiting for transfers between devices  19.5 us (4%)
  matrix products  18.9 us (4%)
    pallas_call x1, Pallas kernels, reduce_all(): pl.pallas_call(functools.partial(reduce_body, depth, half, n_src, keep),...  101 us
    pallas_call x1, Pallas kernels, gather_bands(): pl.pallas_call(functools.partial(gather_body, depth, size // 2), in_specs...  53.7 us
    pallas_call x1, Pallas kernels, feed(): pl.pallas_call(functools.partial(feed_body, chunks), grid=(rows // tile,)...  34.7 us
    pallas_call x5, Pallas kernels, outer_rows(): pl.pallas_call(functools.partial(outer_body, False), grid=(chunks,), in_s...  26.8 us
    pallas_call x2, Pallas kernels, project(): pl.pallas_call(functools.partial(project_body, width, with_query), grid=(...  17 us
    pallas_call x1, Pallas kernels, attend_back(): pl.pallas_call(functools.partial(attend_back_body, width, head, kp), grid...  15.6 us
    ppermute x1, waiting for transfers between devices, per_device(): lax.ppermute(tail_sum, 'seq', [(i, i + 2) for i in range(peers - 2)])  13.1 us
    pallas_call x1, Pallas kernels, attend(): pl.pallas_call(functools.partial(attend_body, width, head, kp), grid_spec...  12.2 us
  transfers between devices with their start and end apart: 8, of which 3 were waited for; matrix products, arithmetic and copies ran while one was open for 8% of the time, Pallas kernels for 25%

profile of v2, /device:TPU:9, one launch (start us, length us, event | category | flops | bytes accessed | tf_op | source)
XLA Modules:
  0.0 446.4 jit_solution(17215888740412098959)
XLA Ops:
  23.1 53.7 %gather_bands.1 = (bf16[4,2,2,2,96,768]{5,4,3,2,1,0:T(8,128)(2,1)}, bf16[2,2,512,256]{3,2,1,0:T(8,128)(2,1)}) custom-call(bf16[96,768]{1,0:T(8,128)(2,1)} %reshape.190.band_ref, bf16[512,256]{1,0:T(8,128)(2,1)} %convert_element_type.87.proj_ref), custom_call_target="tpu_custom_call" | custom-call | flops 1000000000 | bytes 90000000 | tf_op jit(solution)/shard_map/gather_bands/pallas_call | solution.py:817
  85.1 9.3 %project.1 = (bf16[1024,768]{1,0:T(8,128)(2,1)}, bf16[1024,1536]{1,0:T(8,128)(2,1)}, f32[2,256,1536]{2,1,0:T(8,128)}) custom-call(bf16[1024,768]{1,0:T(8,128)(2,1)} %bitcast.237, bf16[3072,768]{1,0:T(8,128)(2,1)} %bitcast.243, bf16[2,256,512]{2,1,0:T(8,128)(2,1)} %copy.57.e_ref), custom_call_target="tpu_custom_call" | custom-call | flops 3623878656 | bytes 12000000 | tf_op jit(solution)/shard_map/project/pallas_call | solution.py:82
  94.4 7.7 %project_peer.1 = f32[2,256,1536]{2,1,0:T(8,128)} custom-call(bf16[1024,768]{1,0:T(8,128)(2,1)} %collective-permute-done.x_ref, bf16[3072,768]{1,0:T(8,128)(2,1)} %bitcast.244, bf16[2,256,512]{2,1,0:T(8,128)(2,1)} %copy.58.e_ref), custom_call_target="tpu_custom_call" | custom-call | flops 3623878656 | bytes 12000000 | tf_op jit(solution)/shard_map/project_peer/pallas_call | solution.py:82
  102.1 9.8 %bitcast_add_fusion.1 = (f32[256,1536]{1,0:T(8,128)S(1)}, f32[256,1536]{1,0:T(8,128)}) fusion(f32[2,256,1536]{2,1,0:T(8,128)} %project_peer.1, f32[2,256,1536]{2,1,0:T(8,128)} %get-tuple-element.44, f32[]{:T(128)} %bitcast.35, f32[]{:T(128)} %bitcast.33, f32[]{:T(128)} %bitcast.32, f32[]{:T(128)} %bitcast.31, f32[]{:T(128)} %bitcast.28, f32[]{:T(128)} %bitcast.21, ...), kind=kLoop, calls=%fused_computation.7 | loop fusion | flops 5505024 | bytes 9437216 | tf_op jit(solution)/shard_map/add | solution.py:1010
  115.1 3.7 collective-permute-start.2
  136.8 13.1 %collective-permute-done.1 = f32[256,1536]{1,0:T(8,128)} collective-permute-done((f32[256,1536]{1,0:T(8,128)S(1)}, f32[256,1536]{1,0:T(8,128)}, u32[]{:S(2)}, u32[]{:S(2)}) %collective-permute-start.1) | collective-permute-done | bytes 1572896 | tf_op jit(solution)/shard_map/ppermute | solution.py:1014
  153.0 4.4 fusion.18
  158.8 12.2 %attend.1 = (bf16[1024,768]{1,0:T(8,128)(2,1)}, f32[1024,768]{1,0:T(8,128)}, f32[2,768]{1,0:T(2,128)}) custom-call(s32[2]{0:T(128)} %copy-done.22, bf16[1024,768]{1,0:T(8,128)(2,1)} %get-tuple-element.43.q_ref, bf16[2,256,1536]{2,1,0:T(8,128)(2,1)} %pad_maximum_fusion.1.s_ref, bf16[3072,768]{1,0:T(8,128)(2,1)} %bitcast.245, bf16[1024,768]{1,0:T(8,128)(2,1)} %bitcast.238), custom_call_target="tpu_custom_call" | custom-call | flops 2818572288 | bytes 10000000 | tf_op jit(solution)/shard_map/attend/pallas_call | solution.py:153
  171.7 34.7 %feed.1 = (bf16[1024,768]{1,0:T(8,128)(2,1)}, bf16[1024,3072]{1,0:T(8,128)(2,1)}, bf16[1024,3072]{1,0:T(8,128)(2,1)}, bf16[1024,768]{1,0:T(8,128)(2,1)}, bf16[10...) custom-call(f32[1024,768]{1,0:T(8,128)} %get-tuple-element.45.first_, ...), custom_call_target="tpu_custom_call" | custom-call | flops 19327352832 | bytes 30000000 | tf_op jit(solution)/shard_map/feed/pallas_call | solution.py:273
  206.4 15.6 %attend_back.1 = (bf16[1024,768]{1,0:T(8,128)(2,1)}, f32[2,256,1536]{2,1,0:T(8,128)}) custom-call(bf16[1024,768]{1,0:T(8,128)(2,1)} %get-tuple-element.43.q_ref, bf16[2,256,1536]{2,1,0:T(8,128)(2,1)} %pad_maximum_fusion.1.s_ref, bf16[1024,768]{1,0:T(8,128)(2,1)} %get-tuple-element.48.g_ref), custom_call_target="tpu_custom_call" | custom-call | flops 3221225472 | bytes 10000000 | tf_op jit(solution)/shard_map/attend_back/pallas_call | solution.py:344
  227.4 3.3 collective-permute-start.4
  230.7 3.9 collective-permute-start.5
  236.8 4.3 outer_query.1
  241.1 4.3 outer_out.1
  245.4 9.4 %outer_down.1 = bf16[3072,768]{1,0:T(8,128)(2,1)} custom-call(bf16[1024,3072]{1,0:T(8,128)(2,1)} %get-tuple-element.55.l_ref, bf16[1024,768]{1,0:T(8,128)(2,1)} %get-tuple-element.56.r_ref), custom_call_target="tpu_custom_call" | custom-call | flops 4831838208 | bytes 20000000 | tf_op jit(solution)/shard_map/outer_down/pallas_call | solution.py:393
  254.8 9.2 %outer_up.1 = bf16[8,4,96,768]{3,2,1,0:T(8,128)(2,1)} custom-call(bf16[1024,768]{1,0:T(8,128)(2,1)} %get-tuple-element.53.l_ref, bf16[1024,3072]{1,0:T(8,128)(2,1)} %get-tuple-element.54.r_ref), custom_call_target="tpu_custom_call" | custom-call | flops 4831838208 | bytes 20000000 | tf_op jit(solution)/shard_map/outer_up/pallas_call | solution.py:375
  267.2 3.8 fusion.16
  272.4 11.0 %back.1 = (bf16[1024,1536]{1,0:T(8,128)(2,1)}, f32[2,512,256]{2,1,0:T(8,128)}, f32[1024,768]{1,0:T(8,128)}) custom-call(bf16[2,512,256]{2,1,0:T(8,128)(2,1)} %maximum_select_fusion.e_ref, bf16[1024,1536]{1,0:T(8,128)(2,1)} %get-tuple-element.47.kv_ref, bf16[2,256,1536]{2,1,0:T(8,128)(2,1)} %pad_maximum_fusion.2.s_ref, ...), custom_call_target="tpu_custom_call" | custom-call | flops 5234491392 | bytes 20000000 | tf_op jit(solution)/shard_map/back/pallas_call | solution.py:426
  290.7 3.4 dynamic_update_slice.7
  298.7 4.3 outer_key.1
  303.0 4.5 %outer_value.1 = bf16[768,768]{1,0:T(8,128)(2,1)} custom-call(bf16[1024,768]{1,0:T(8,128)(2,1)} %bitcast.241, bf16[1024,768]{1,0:T(8,128)(2,1)} %get-tuple-element.125.r_ref), custom_call_target="tpu_custom_call" | custom-call | flops 1207959552 | bytes 20000000 | tf_op jit(solution)/shard_map/outer_value/pallas_call | solution.py:393
  309.1 101.3 %reduce_all.1 = (f32[96,768]{1,0:T(8,128)}, f32[96,768]{1,0:T(8,128)}, f32[96,768]{1,0:T(8,128)}, f32[4,2,64,256]{3,2,1,0:T(8,128)}, f32[2,2,4,2,8,256]{5,4,3,2,1,0:T(8,128)}) custom-call(bf16[2,4,2,2,96,768]{5,4,3,2,1,0:T(8,128)(2,1)} %bitcast.216, bf16[2,4,2,2,96,768]{5,4,3,2,1,0:T(8,128)(2,1)} %bitcast.215, bf16[4,2,96,768]{3,2,1,0:T(8,128)(2,1)} %bitcast.222, ...), custom_call_target="tpu_custom_call" | custom-call | tf_op jit(solution)/shard_map/reduce_all/pallas_call | solution.py:715
  416.6 3.5 fusion.8
  422.7 4.9 %fusion.10 = f32[24,96,96]{2,1,0:T(8,128)} fusion(f32[24,96,96]{2,1,0:T(8,128)} %param.23, f32[24,96,96]{2,1,0:T(8,128)S(1)} %pad_maximum_fusion.3), kind=kOutput, calls=%fused_computation.35 | convolution fusion | flops 255246336 | bytes 2654208 | tf_op jit(solution)/shard_map/tij,tkj->tik/dot_general | solution.py:839
  (150 shorter events, 76.7 us)
Async XLA Ops:
  7.2 407.2 %copy-start = (f32[24,96,96]{2,1,0:T(8,128)S(1)}, f32[24,96,96]{2,1,0:T(8,128)}, u32[]{:S(2)}) copy-start(f32[24,96,96]{2,1,0:T(8,128)} %param.26) | copy-start | bytes 2654212
  7.2 164.5 %all-gather.2.cloned.1.call-start = ((), (), s32[]{:S(2)}) async-start(), calls=%async_computation | async-start | bytes 9732096 | tf_op jit(solution)/shard_map/all_gather | solution.py:878
  8.7 2.8 copy-start.23
  8.7 2.8 copy-start.24
  8.8 11.0 %copy-start.7 = (f32[512,256]{1,0:T(8,128)S(1)}, f32[512,256]{1,0:T(8,128)}, u32[]{:S(2)}) copy-start(f32[512,256]{1,0:T(8,128)} %param.27) | copy-start | bytes 1572868
  10.0 84.4 %collective-permute-start = (bf16[1024,768]{1,0:T(8,128)(2,1)}, bf16[1024,768]{1,0:T(8,128)(2,1)}, u32[]{:S(2)}, u32[]{:S(2)}) collective-permute-start(bf16[1024,768]{1,0:T(8,128)(2,1)} %bitcast.236), channel_id=1, source_target_pairs={{0,4},{4,0},{8,12},{12,8},{16,20},{20,16},{24,28},{28,24},{1,5},{5... | collective-permute-start | bytes 4718600 | tf_op jit(solution)/shard_map/ppermute | solution.py:958
  12.4 66.1 %copy-start.22 = (s32[2]{0:T(128)}, s32[2]{0:T(128)S(1)}, u32[]{:S(2)}) copy-start(s32[2]{0:T(128)S(1)} %get-tuple-element.117.n_ref) | copy-start | bytes 28
  111.9 38.0 %collective-permute-start.1 = (f32[256,1536]{1,0:T(8,128)S(1)}, f32[256,1536]{1,0:T(8,128)}, u32[]{:S(2)}, u32[]{:S(2)}) collective-permute-start(f32[256,1536]{1,0:T(8,128)S(1)} %get-tuple-element.123), channel_id=1, source_target_pairs={{0,8},{4,12},{8,16},{12,20},{16,24},{20,28},{1,9},{5,13},{9,17},{1... | collective-permute-start | bytes 4718600 | tf_op jit(solution)/shard_map/ppermute | solution.py:1014
  115.1 37.9 %collective-permute-start.2 = (f32[256,1536]{1,0:T(8,128)}, f32[256,1536]{1,0:T(8,128)}, u32[]{:S(2)}, u32[]{:S(2)}) collective-permute-start(f32[256,1536]{1,0:T(8,128)} %get-tuple-element.124), channel_id=1, source_target_pairs={{8,0},{12,4},{16,8},{20,12},{24,16},{28,20},{9,1},{13,5},{17,9},{2... | collective-permute-start | bytes 4718600 | tf_op jit(solution)/shard_map/ppermute | solution.py:1015
  222.0 14.6 %copy-start.19 = (f32[4,768]{1,0:T(4,128)S(1)}, f32[4,768]{1,0:T(4,128)}, u32[]{:S(2)}) copy-start(f32[4,768]{1,0:T(4,128)} %get-tuple-element.61) | copy-start | bytes 36868
  224.3 39.7 %collective-permute-start.3 = (bf16[256,1536]{1,0:T(8,128)(2,1)S(1)}, bf16[256,1536]{1,0:T(8,128)(2,1)}, u32[]{:S(2)}, u32[]{:S(2)}) collective-permute-start(bf16[256,1536]{1,0:T(8,128)(2,1)S(1)} %get-tuple-element.127), channel_id=1, source_target_pairs={{0,4},{4,8},{8,12},{12,16},{16,20},{20,24},{24,28},{1,5},{5,9},{9,... | collective-permute-start | bytes 2359304 | tf_op jit(solution)/shard_map/ppermute | solution.py:1057
  227.4 36.5 %collective-permute-start.4 = (bf16[256,1536]{1,0:T(8,128)(2,1)S(1)}, bf16[256,1536]{1,0:T(8,128)(2,1)}, u32[]{:S(2)}, u32[]{:S(2)}) collective-permute-start(bf16[256,1536]{1,0:T(8,128)(2,1)S(1)} %get-tuple-element.127), channel_id=1, source_target_pairs={{0,8},{4,12},{8,16},{12,20},{16,24},{20,28},{1,9},{5,13},{9,17},{1... | collective-permute-start | bytes 2359304 | tf_op jit(solution)/shard_map/ppermute | solution.py:1057
  230.7 33.2 %collective-permute-start.5 = (bf16[256,1536]{1,0:T(8,128)(2,1)S(1)}, bf16[256,1536]{1,0:T(8,128)(2,1)}, u32[]{:S(2)}, u32[]{:S(2)}) collective-permute-start(bf16[256,1536]{1,0:T(8,128)(2,1)S(1)} %get-tuple-element.128), channel_id=1, source_target_pairs={{4,0},{8,4},{12,8},{16,12},{20,16},{24,20},{28,24},{5,1},{9,5},{13... | collective-permute-start | bytes 2359304 | tf_op jit(solution)/shard_map/ppermute | solution.py:1058
  234.7 32.5 %collective-permute-start.6 = (bf16[256,1536]{1,0:T(8,128)(2,1)S(1)}, bf16[256,1536]{1,0:T(8,128)(2,1)}, u32[]{:S(2)}, u32[]{:S(2)}) collective-permute-start(bf16[256,1536]{1,0:T(8,128)(2,1)S(1)} %get-tuple-element.128), channel_id=1, source_target_pairs={{8,0},{12,4},{16,8},{20,12},{24,16},{28,20},{9,1},{13,5},{17,9},{2... | collective-permute-start | bytes 2359304 | tf_op jit(solution)/shard_map/ppermute | solution.py:1058
  303.0 4.5 %copy-start.3 = (f32[4,8,64,256]{3,2,0,1:T(8,128)S(1)}, f32[4,8,64,256]{3,2,0,1:T(8,128)}, u32[]{:S(2)}) copy-start(f32[4,8,64,256]{3,2,0,1:T(8,128)} %copy.60) | copy-start | bytes 6291460
  410.5 3.3 copy-start.16
  414.4 13.1 %copy-start.1 = (f32[24,96,96]{2,1,0:T(8,128)}, f32[24,96,96]{2,1,0:T(8,128)S(1)}, u32[]{:S(2)}) copy-start(f32[24,96,96]{2,1,0:T(8,128)S(1)} %pad_maximum_fusion.3) | copy-start | bytes 2654212
  422.7 4.9 %copy-start.10 = (f32[24,96,96]{2,1,0:T(8,128)S(1)}, f32[24,96,96]{2,1,0:T(8,128)}, u32[]{:S(2)}) copy-start(f32[24,96,96]{2,1,0:T(8,128)} %param.24) | copy-start | bytes 2654212
  427.6 3.1 copy-start.2
  427.6 3.1 copy-start.11
  430.7 2.9 copy-start.13
  433.6 3.3 copy-start.8
  433.6 3.3 copy-start.14
  435.1 4.1 copy-start.18
  (11 other events, 23.8 us)
Sparse Core Ops, SparseCore 0:
  11.5 92.7 all-gather.1

commit v3 on v2

--- a/solution.py
+++ b/solution.py
@@ -388,28 +388,52 @@
 
 
 def outer_rows(left, right, dtype, name):
-    rows, width = right.shape
-    chunks = left.shape[1] // width
+    rows, width = right.shape[0], min(left.shape[1], right.shape[1])
+    tall, wide = left.shape[1] // width, right.shape[1] // width
+    moving = lambda n: (lambda i: (0, i)) if n > 1 else (lambda i: (0, 0))
     return pl.pallas_call(
         functools.partial(outer_body, False),
-        grid=(chunks,),
+        grid=(tall * wide,),
         in_specs=[
-            vspec((rows, width), lambda i: (0, i)),
-            vspec((rows, width), lambda i: (0, 0), True),
+            vspec((rows, width), moving(tall), tall == 1),
+            vspec((rows, width), moving(wide), wide == 1),
         ],
         out_specs=vspec((width, width), lambda i: (i, 0)),
-        out_shape=jax.ShapeDtypeStruct((chunks * width, width), dtype),
+        out_shape=jax.ShapeDtypeStruct((tall * wide * width, width), dtype),
         compiler_params=params(),
-        cost_estimate=cost(2 * rows * width * width * chunks, 20e6),
+        cost_estimate=cost(2 * rows * width * width * tall * wide, 20e6),
         name=name,
     )(left, right)
 
 
-def back_body(width, e_ref, kv_ref, s_ref, dq_ref, w_ref, df_ref, dkv_ref, ge_ref, gi_ref):
-    summary = s_ref[0]
+def back_body(
+    width, blocks, c_ref, n_ref, e_ref, kv_ref, p_ref, *refs
+):
+    far_refs = refs[:4]
+    dq_ref, w_ref, df_ref, dkv_ref, gp_ref, gi_ref = refs[4:]
+    step = pl.program_id(0)
+    short, kp = e_ref.shape[1], e_ref.shape[2]
+    total = c_ref[step, 0] * p_ref[0]
+    for other in range(1, blocks):
+        total = total + c_ref[step, other] * p_ref[other]
+    for k in range(4):
+        total = total + c_ref[step, blocks + k] * far_refs[k][...].astype(F32)
+    summary = total.astype(BF)
     dkv = dot(e_ref[0], summary).astype(BF)
     dkv_ref[...] = dkv
-    ge_ref[0] = dot_t(kv_ref[...], summary)
+    keep = lax.broadcasted_iota(jnp.int32, (short, 1), 0) < n_ref[1, step]
+    grad_e = jnp.where(keep, dot_t(kv_ref[...], summary), 0.0)
+    column = n_ref[0, step]
+    at = pl.multiple_of(jnp.minimum((column // 8) * 8, gp_ref.shape[0] - short - 8), 8)
+    moved = pltpu.roll(
+        jnp.concatenate([grad_e, jnp.zeros((8, kp), F32)], axis=0), column - at, 0
+    )
+
+    @pl.when(step == 0)
+    def _():
+        gp_ref[...] = jnp.zeros_like(gp_ref)
+
+    gp_ref[pl.ds(at, short + 8), :] += moved
     gi_ref[...] = (
         df_ref[...]
         + dot_t(dq_ref[...], w_ref[pl.ds(0, width), :])
@@ -418,36 +442,43 @@
     )
 
 
-def back(e_rows, kv, grad_summary, dq, w_att, grad_first):
+def back(coef, places, e_rows, kv, grad_parts, far_parts, dq, w_att, grad_first, positions):
     rows, width = dq.shape
     blocks, short, kp = e_rows.shape
-    row = lambda i: (i, 0)
-    lead = lambda i: (i, 0, 0)
+    row = lambda i, *_: (i, 0)
+    lead = lambda i, *_: (i, 0, 0)
+    fixed = lambda i, *_: (0, 0)
     return pl.pallas_call(
-        functools.partial(back_body, width),
-        grid=(blocks,),
-        in_specs=[
-            vspec((1, short, kp), lead),
-            vspec((short, 2 * width), row),
-            vspec((1, kp, 2 * width), lead),
-            vspec((short, width), row),
-            vspec((3 * width, width), lambda i: (0, 0), True),
-            vspec((short, width), row),
-        ],
-        out_specs=[
-            vspec((short, 2 * width), row),
-            vspec((1, short, kp), lead),
-            vspec((short, width), row),
-        ],
+        functools.partial(back_body, width, blocks),
+        grid_spec=pltpu.PrefetchScalarGridSpec(
+            num_scalar_prefetch=2,
+            grid=(blocks,),
+            in_specs=[
+                vspec((1, short, kp), lead),
+                vspec((short, 2 * width), row),
+                vspec(grad_parts.shape, lambda i, *_: (0, 0, 0), True),
+            ]
+            + [vspec((kp, 2 * width), fixed, True)] * 4
+            + [
+                vspec((short, width), row),
+                vspec((3 * width, width), fixed, True),
+                vspec((short, width), row),
+            ],
+            out_specs=[
+                vspec((short, 2 * width), row),
+                vspec((positions, kp), fixed),
+                vspec((short, width), row),
+            ],
+        ),
         out_shape=[
             jax.ShapeDtypeStruct((rows, 2 * width), BF),
-            jax.ShapeDtypeStruct((blocks, short, kp), F32),
+            jax.ShapeDtypeStruct((positions, kp), F32),
             jax.ShapeDtypeStruct((rows, width), F32),
         ],
         compiler_params=params(),
         cost_estimate=cost(2 * rows * width * (3 * width + 4 * kp), 20e6),
         name="back",
-    )(e_rows, kv, grad_summary, dq, w_att, grad_first)
+    )(coef, places, e_rows, kv, grad_parts, *far_parts, dq, w_att, grad_first)
 
 
 MESH_ID = pl.DeviceIdType.MESH
@@ -459,10 +490,11 @@
     (own, got_c, sum_c, got_a, got_b, sum_a, sum_b, got_a2, got_b2, sum_z, got_z) = refs[
         n_src + 5 : n_src + 16
     ]
+    keep_a, keep_b, keep_z = refs[n_src + 16 : n_src + 19]
     (e_own, e_got, e_sum, e_got1, e_sum1, e_got2, e_sum2, e_gotz, e_all, e_rows) = refs[
-        n_src + 16 : n_src + 26
+        n_src + 19 : n_src + 29
     ]
-    send, recv, local = refs[n_src + 26 :]
+    send, recv, local = refs[n_src + 29 :]
     seq, mine = lax.axis_index("seq"), lax.axis_index("own")
     z, y, x, c = seq // 2, seq % 2, mine // 2, mine % 2
     core = (seq, 2 * x + (1 - c))
@@ -491,10 +523,11 @@
         sent.append(copy)
         return copy
 
-    pieces = 3
-    up, down, extra = sources[0], sources[1], sources[6]
+    up, down, g_query, g_keyval, g_out, extra = sources
+    bands = [g_query, g_keyval.at[0], g_keyval.at[1], g_out]
     half_z = depth // 2
-    loads, firsts = [], []
+    cols = own.shape[-1]
+    loads = []
 
     def load(src, dst):
         copy = pltpu.make_async_copy(src, dst, local.at[len(loads)])
@@ -505,23 +538,24 @@
     e_first = [push(extra.at[:, :, 1 - c], e_got, core)]
     e_load = [load(extra.at[:, :, c], e_own)]
     piece_first, piece_load = [], []
-    for p in range(2):
-        piece_first.append(
-            [
-                push(up.at[:, :, 1 - c, p], got_c.at[p, pl.ds(0, half_z)], core),
-                push(down.at[:, :, 1 - c, p], got_c.at[p, pl.ds(half_z, half_z)], core),
+    for p in range(6):
+        at, part = p // 2, pl.ds((p % 2) * cols, cols)
+        if at < 2:
+            first = [
+                push(up.at[:, :, 1 - c, at, :, part], got_c.at[p, pl.ds(0, half_z)], core),
+                push(down.at[:, :, 1 - c, at, :, part], got_c.at[p, pl.ds(half_z, half_z)], core),
             ]
-        )
-        piece_load.append(
-            [
-                load(up.at[:, :, c, p], own.at[p, pl.ds(0, half_z)]),
-                load(down.at[:, :, c, p], own.at[p, pl.ds(half_z, half_z)]),
+            kept = [
+                load(up.at[:, :, c, at, :, part], own.at[p, pl.ds(0, half_z)]),
+                load(down.at[:, :, c, at, :, part], own.at[p, pl.ds(half_z, half_z)]),
             ]
-        )
-    piece_first.append(
-        [push(sources[2 + m].at[:, 1 - c], got_c.at[2, m], core) for m in range(depth)]
-    )
-    piece_load.append([load(sources[2 + m].at[:, c], own.at[2, m]) for m in range(depth)])
+        else:
+            first = [
+                push(bands[m].at[:, 1 - c, :, part], got_c.at[p, m], core) for m in range(depth)
+            ]
+            kept = [load(bands[m].at[:, c, :, part], own.at[p, m]) for m in range(depth)]
+        piece_first.append(first)
+        piece_load.append(kept)
 
     state = {}
 
@@ -529,8 +563,10 @@
         for copy in copies:
             copy.wait_recv()
 
+    low, high = pl.ds(0, half), pl.ds(half, half)
+
     def add(a, b):
-        return (a.astype(F32) + b.astype(F32)).astype(BF)
+        return a.astype(F32) + b.astype(F32)
 
     def piece_c(p):
         for copy in piece_load[p]:
@@ -538,40 +574,55 @@
         wait_recv(piece_first[p])
 
         def body(i, carry):
-            zz, yx = i // 4, i % 4
-            sum_c[p, zz, yx // 2, yx % 2] = add(own[p, zz, yx], got_c[p, zz, yx])
+            zz, w = i // 2, i % 2
+            to_x, to_y = 2 * w + 1 - x, 2 * (1 - y) + w
+            sum_c[p, 0, zz, w] = add(own[p, zz, to_x, low, :], got_c[p, zz, to_x, low, :]).astype(BF)
+            sum_c[p, 1, zz, w] = add(own[p, zz, to_y, high, :], got_c[p, zz, to_y, high, :]).astype(BF)
             return carry
 
-        lax.fori_loop(0, depth * 4, body, 0)
+        lax.fori_loop(0, depth * 2, body, 0)
         state["1", p] = [
-            push(sum_c.at[p, :, :, 1 - x, pl.ds(0, half), :], got_a.at[p], along_x),
-            push(sum_c.at[p, :, 1 - y, :, pl.ds(half, half), :], got_b.at[p], along_y),
+            push(sum_c.at[p, 0], got_a.at[p], along_x),
+            push(sum_c.at[p, 1], got_b.at[p], along_y),
         ]
 
     def piece_1(p):
         wait_recv(state["1", p])
 
-        def body(i, carry):
-            zz, w = i // 2, i % 2
-            sum_a[p, zz, w] = add(sum_c[p, zz, w, x, pl.ds(0, half), :], got_a[p, zz, w])
-            sum_b[p, zz, w] = add(sum_c[p, zz, y, w, pl.ds(half, half), :], got_b[p, zz, w])
+        def side_a(zz, w):
+            at = 2 * w + x
+            return add(own[p, zz, at, low, :], got_c[p, zz, at, low, :]) + got_a[p, zz, w].astype(F32)
+
+        def side_b(zz, w):
+            at = 2 * y + w
+            return add(own[p, zz, at, high, :], got_c[p, zz, at, high, :]) + got_b[p, zz, w].astype(F32)
+
+        def body(zz, carry):
+            sum_a[p, zz] = side_a(zz, 1 - y).astype(BF)
+            sum_b[p, zz] = side_b(zz, 1 - x).astype(BF)
+            keep_a[p, zz] = side_a(zz, y)
+            keep_b[p, zz] = side_b(zz, x)
             return carry
 
-        lax.fori_loop(0, depth * 2, body, 0)
+        lax.fori_loop(0, depth, body, 0)
         state["2", p] = [
-            push(sum_a.at[p, :, 1 - y], got_a2.at[p], along_y),
-            push(sum_b.at[p, :, 1 - x], got_b2.at[p], along_x),
+            push(sum_a.at[p], got_a2.at[p], along_y),
+            push(sum_b.at[p], got_b2.at[p], along_x),
         ]
 
     def piece_2(p):
         wait_recv(state["2", p])
 
         def body(zz, carry):
-            sum_z[p, zz, pl.ds(0, half), :] = add(sum_a[p, zz, y], got_a2[p, zz])
-            sum_z[p, zz, pl.ds(half, half), :] = add(sum_b[p, zz, x], got_b2[p, zz])
+            total_a = keep_a[p, zz] + got_a2[p, zz].astype(F32)
+            total_b = keep_b[p, zz] + got_b2[p, zz].astype(F32)
+            sum_z[p, zz, low, :] = total_a.astype(BF)
+            sum_z[p, zz, high, :] = total_b.astype(BF)
             return carry
 
         lax.fori_loop(0, depth, body, 0)
+        keep_z[p, low, :] = keep_a[p, z] + got_a2[p, z].astype(F32)
+        keep_z[p, high, :] = keep_b[p, z] + got_b2[p, z].astype(F32)
         state["z", p] = [
             push(sum_z.at[p, lax.rem(z + d, depth)], got_z.at[p, d - 1], along_z[d - 1])
             for d in range(1, depth)
@@ -579,10 +630,10 @@
 
     def piece_z(p):
         wait_recv(state["z", p])
-        total = sum_z[p, z].astype(F32)
+        total = keep_z[p]
         for d in range(depth - 1):
             total = total + got_z[p, d].astype(F32)
-        outs[p][...] = total
+        outs[p // 2][:, pl.ds((p % 2) * cols, cols)] = total
 
     def extra_c():
         e_load[0].wait()
@@ -641,25 +692,14 @@
         wait_recv(state["gx"])
         state["gc"] = [push(e_rows.at[:, c], e_rows.at[:, c], core)]
 
-    extra_c()
-    piece_c(0)
-    extra_1()
-    piece_c(1)
-    extra_2()
-    piece_1(0)
-    piece_c(2)
-    extra_z()
-    piece_2(0)
-    piece_1(1)
-    extra_gather_y()
-    piece_1(2)
-    piece_2(1)
-    extra_gather_x()
-    piece_z(0)
-    piece_2(2)
-    extra_gather_c()
-    piece_z(1)
-    piece_z(2)
+    stages = [piece_c, piece_1, piece_2, piece_z]
+    small = [extra_c, extra_1, extra_2, extra_z, extra_gather_y, extra_gather_x, extra_gather_c]
+    for turn in range(9):
+        if turn < len(small):
+            small[turn]()
+        for stage in range(4):
+            if 0 <= turn - stage < 6:
+                stages[stage](turn - stage)
     outs[3][...] = e_all[:, :, pl.ds(0, extra_keep), :]
     wait_recv(state["gc"])
     outs[4][...] = e_rows[...]
@@ -667,7 +707,7 @@
         copy.wait_send()
 
 
-def reduce_all(g_att, g_up, g_down, extra, peers):
+def reduce_all(g_query, g_keyval, g_out, g_up, g_down, extra, peers):
     depth = peers // 2
     size, width = g_up.shape[2], g_up.shape[3]
     half = size // 2
@@ -678,26 +718,34 @@
             g_up.reshape(depth // 2, 4, 2, 2, size, width),
             g_down.reshape(depth // 2, 4, 2, 2, size, width),
         ]
-        + [g.reshape(4, 2, size, width) for g in g_att]
+        + [
+            g_query.reshape(4, 2, size, width),
+            g_keyval.reshape(2, 4, 2, size, width),
+            g_out.reshape(4, 2, size, width),
+        ]
         + [extra.reshape(depth, 4, 2, e_rows_all, kp)]
     )
     n_src = len(sources)
-    messages = 1 + 4 + depth + 3 * (4 + depth - 1) + 2 + 2 * (depth - 1) + 3
-    loads = 1 + 4 + depth
+    cols = width // 2
+    messages = 1 + 8 + 2 * depth + 6 * (4 + depth - 1) + 2 + 2 * (depth - 1) + 3
+    loads = 1 + 8 + 2 * depth
     any_spec = pl.BlockSpec(memory_space=pl.ANY)
     vmem = pl.BlockSpec(memory_space=pltpu.VMEM)
     scratch = [
-        pltpu.VMEM((3, depth, 4, size, width), BF),
-        pltpu.VMEM((3, depth, 4, size, width), BF),
-        pltpu.VMEM((3, depth, 2, 2, size, width), BF),
-        pltpu.VMEM((3, depth, 2, half, width), BF),
-        pltpu.VMEM((3, depth, 2, half, width), BF),
-        pltpu.VMEM((3, depth, 2, half, width), BF),
-        pltpu.VMEM((3, depth, 2, half, width), BF),
-        pltpu.VMEM((3, depth, half, width), BF),
-        pltpu.VMEM((3, depth, half, width), BF),
-        pltpu.VMEM((3, depth, size, width), BF),
-        pltpu.VMEM((3, depth - 1, size, width), BF),
+        pltpu.VMEM((6, depth, 4, size, cols), BF),
+        pltpu.VMEM((6, depth, 4, size, cols), BF),
+        pltpu.VMEM((6, 2, depth, 2, half, cols), BF),
+        pltpu.VMEM((6, depth, 2, half, cols), BF),
+        pltpu.VMEM((6, depth, 2, half, cols), BF),
+        pltpu.VMEM((6, depth, half, cols), BF),
+        pltpu.VMEM((6, depth, half, cols), BF),
+        pltpu.VMEM((6, depth, half, cols), BF),
+        pltpu.VMEM((6, depth, half, cols), BF),
+        pltpu.VMEM((6, depth, size, cols), BF),
+        pltpu.VMEM((6, depth - 1, size, cols), BF),
+        pltpu.VMEM((6, depth, half, cols), F32),
+        pltpu.VMEM((6, depth, half, cols), F32),
+        pltpu.VMEM((6, size, cols), F32),
         pltpu.VMEM((depth, 4, e_rows_all, kp), F32),
         pltpu.VMEM((depth, 4, e_rows_all, kp), F32),
         pltpu.VMEM((depth, 2, 2, e_rows_all, kp), F32),
@@ -1043,7 +1091,6 @@
     row_start = seq * rows_here
     row_end = row_start + rows_here
     o_start, o_end = take(b_start, own_at), take(b_end, own_at)
-    same = (o_start[0] == o_start[-1]).astype(F32)
     g_head = grad_parts[0]
     g_tail = grad_parts[-1]
     for b in range(1, blocks):
@@ -1051,41 +1098,37 @@
     for b in range(blocks - 1):
         g_tail = g_tail + (o_start[b] == o_start[-1]).astype(F32) * grad_parts[b]
     low_head, low_tail = g_head.astype(BF), g_tail.astype(BF)
-    left_sum = jnp.zeros_like(g_head)
-    right_sum = jnp.zeros_like(g_head)
+    far_parts, far_flags = [], []
+    at_head = (o_start == o_start[0]).astype(F32)
+    at_tail = (o_start == o_start[-1]).astype(F32)
     for far in (1, 2):
-        tail_far = lax.ppermute(low_tail, "seq", [(i, i + far) for i in range(peers - far)])
-        head_far = lax.ppermute(low_head, "seq", [(i + far, i) for i in range(peers - far)])
         reach = (far - 1) * rows_here
-        left_sum = left_sum + (o_start[0] < row_start - reach).astype(F32) * tail_far.astype(F32)
-        right_sum = right_sum + (o_end[-1] > row_end + reach).astype(F32) * head_far.astype(F32)
-    at_head = (o_start == o_start[0]).astype(F32)
-    grad_summary = jnp.stack(
-        [
-            jnp.where(
-                at_head[b] > 0, g_head + left_sum + same * right_sum, g_tail + right_sum
-            ).astype(BF)
-            for b in range(blocks)
-        ]
-    )
+        far_parts.append(lax.ppermute(low_tail, "seq", [(i, i + far) for i in range(peers - far)]))
+        far_flags.append(at_head * (o_start[0] < row_start - reach).astype(F32))
+        far_parts.append(lax.ppermute(low_head, "seq", [(i + far, i) for i in range(peers - far)]))
+        far_flags.append(at_tail * (o_end[-1] > row_end + reach).astype(F32))
+    together = (o_start[:, None] == o_start[None, :]).astype(F32)
+    coef_back = jnp.concatenate([together, jnp.stack(far_flags, axis=1)], axis=1)
+    own_col = take(column, own_at)
     gtype = BF if fused else F32
     g_up = outer_up(first_low, grad_up, size, gtype)
     g_down = outer_rows(hidden, grad_down, gtype, "outer_down")
     g_out = outer_rows(mixed, grad_branch, gtype, "outer_out")
     g_query = outer_rows(x, grad_query, gtype, "outer_query")
-    grad_keyval, grad_e, grad_input = back(e_own, keyval, grad_summary, grad_query, w_att, grad_first)
-    g_key = outer_rows(x, grad_keyval[:, :width], gtype, "outer_key")
-    g_value = outer_rows(x, grad_keyval[:, width:], gtype, "outer_value")
-    g_att = [g_query, g_key, g_value, g_out]
-
+    grad_keyval, grad_proj, grad_input = back(
+        coef_back,
+        jnp.stack([own_col, n_own]),
+        e_own,
+        keyval,
+        grad_parts,
+        far_parts,
+        grad_query,
+        w_att,
+        grad_first,
+        proj_all.shape[0],
+    )
+    g_keyval = outer_rows(x, grad_keyval, gtype, "outer_keyval")
     part_rows = projection.shape[0]
-    grad_proj = jnp.zeros((proj_all.shape[0], kp), F32)
-    keep_e = lax.broadcasted_iota(jnp.int32, (blocks, SHORT, 1), 1) < n_own[:, None, None]
-    grad_e = jnp.where(keep_e, grad_e, 0.0)
-    own_col = take(column, own_at)
-    for b in range(blocks):
-        current = lax.dynamic_slice_in_dim(grad_proj, own_col[b], SHORT, 0)
-        grad_proj = lax.dynamic_update_slice_in_dim(grad_proj, current + grad_e[b], own_col[b], 0)
     valid_here = jnp.sum(n_own).astype(F32)
     extra = jnp.concatenate(
         [
@@ -1103,7 +1146,7 @@
         shares = grad_proj.reshape(own_size, peers, part_rows // peers, kp).swapaxes(0, 1)
         shares = shares.reshape(devices, part_rows // peers, kp)
         ffn_a, ffn_b, att, proj_parts, rows = reduce_all(
-            g_att, g_up, g_down, jnp.concatenate([shares, extra], axis=1), peers
+            g_query, g_keyval, g_out, g_up, g_down, jnp.concatenate([shares, extra], axis=1), peers
         )
         owned = jnp.concatenate(
             [from_bands(att, size), from_bands(ffn_a, size), from_bands(ffn_b, size)], axis=0
@@ -1112,7 +1155,7 @@
         totals = rows[..., 0, :].transpose(2, 3, 0, 1, 4).reshape(devices, kp)
     else:
         owned = scatter_weight_grads(
-            jnp.concatenate(g_att, axis=0), g_up, g_down, per_dev, att_dev, both
+            jnp.concatenate([g_query, g_keyval, g_out], axis=0), g_up, g_down, per_dev, att_dev, both
         )
         packed = jnp.concatenate([grad_proj, extra], axis=0)
         packed = lax.psum(jnp.pad(packed, ((0, -packed.shape[0] % 16), (0, 0))), both)

time: 454 us -> 437 us (0.963)
  local copies, waits for them, and re-layouts: 34.4 us -> 24.8 us
  other arithmetic: 37 us -> 31 us
    dynamic_update_slice x2 -> x0, local copies, waits for them, and re-layouts: 6.06 us -> none  [per_device(): lax.dynamic_update_slice_in_dim(grad_proj, current + grad_e[b], own_col[b...]
    pallas_call x6 -> x5, Pallas kernels: 37.8 us -> 41.1 us  [the longest x4 23.8 us: outer_rows(): pl.pallas_call(functools.partial(outer_body, False), grid=(tall * wide,),...]
  transfers between devices with their start and end apart: 8 -> 8, of which waited for: 3 -> 3; matrix products, arithmetic and copies ran while one was open for 8% -> 9% of each run, Pallas kernels for 25% -> 26%
where the time goes in v3:
time: 437 us; the launch traced here: 429 us
  Pallas kernels  281 us (64%)
  between operations  33.2 us (8%)
  other arithmetic  31 us (7%)
  local copies, waits for them, and re-layouts  24.8 us (6%)
  starting transfers between devices  20.4 us (5%)
  waiting for transfers between devices  19.2 us (4%)
  matrix products  19 us (4%)
    pallas_call x1, Pallas kernels, reduce_all(): pl.pallas_call(functools.partial(reduce_body, depth, half, n_src, keep),...  98 us
    pallas_call x1, Pallas kernels, gather_bands(): pl.pallas_call(functools.partial(gather_body, depth, size // 2), in_specs...  53.7 us
    pallas_call x1, Pallas kernels, feed(): pl.pallas_call(functools.partial(feed_body, chunks), grid=(rows // tile,)...  34.7 us
    pallas_call x4, Pallas kernels, outer_rows(): pl.pallas_call(functools.partial(outer_body, False), grid=(tall * wide,),...  23.8 us
    pallas_call x1, Pallas kernels, back(): pl.pallas_call(functools.partial(back_body, width, blocks), grid_spec=plt...  17.4 us
    pallas_call x2, Pallas kernels, project(): pl.pallas_call(functools.partial(project_body, width, with_query), grid=(...  17 us
    pallas_call x1, Pallas kernels, attend_back(): pl.pallas_call(functools.partial(attend_back_body, width, head, kp), grid...  15.6 us
    ppermute x1, waiting for transfers between devices, per_device(): lax.ppermute(tail_sum, 'seq', [(i, i + 2) for i in range(peers - 2)])  12.6 us
  transfers between devices with their start and end apart: 8, of which 3 were waited for; matrix products, arithmetic and copies ran while one was open for 9% of the time, Pallas kernels for 26%

profile of v3, /device:TPU:9, one launch (start us, length us, event | category | flops | bytes accessed | tf_op | source)
XLA Modules:
  0.0 429.1 jit_solution(5652670616070675540)
XLA Ops:
  23.1 53.7 %gather_bands.1 = (bf16[4,2,2,2,96,768]{5,4,3,2,1,0:T(8,128)(2,1)}, bf16[2,2,512,256]{3,2,1,0:T(8,128)(2,1)}) custom-call(bf16[96,768]{1,0:T(8,128)(2,1)} %reshape.185.band_ref, bf16[512,256]{1,0:T(8,128)(2,1)} %convert_element_type.70.proj_ref), custom_call_target="tpu_custom_call" | custom-call | flops 1000000000 | bytes 90000000 | tf_op jit(solution)/shard_map/gather_bands/pallas_call | solution.py:865
  85.1 9.3 %project.1 = (bf16[1024,768]{1,0:T(8,128)(2,1)}, bf16[1024,1536]{1,0:T(8,128)(2,1)}, f32[2,256,1536]{2,1,0:T(8,128)}) custom-call(bf16[1024,768]{1,0:T(8,128)(2,1)} %bitcast.225, bf16[3072,768]{1,0:T(8,128)(2,1)} %bitcast.195, bf16[2,256,512]{2,1,0:T(8,128)(2,1)} %copy.65.e_ref), custom_call_target="tpu_custom_call" | custom-call | flops 3623878656 | bytes 12000000 | tf_op jit(solution)/shard_map/project/pallas_call | solution.py:82
  94.4 7.7 %project_peer.1 = f32[2,256,1536]{2,1,0:T(8,128)} custom-call(bf16[1024,768]{1,0:T(8,128)(2,1)} %collective-permute-done.x_ref, bf16[3072,768]{1,0:T(8,128)(2,1)} %bitcast.196, bf16[2,256,512]{2,1,0:T(8,128)(2,1)} %copy.66.e_ref), custom_call_target="tpu_custom_call" | custom-call | flops 3623878656 | bytes 12000000 | tf_op jit(solution)/shard_map/project_peer/pallas_call | solution.py:82
  102.1 9.9 %bitcast_add_fusion.1 = (f32[256,1536]{1,0:T(8,128)S(1)}, f32[256,1536]{1,0:T(8,128)}) fusion(f32[2,256,1536]{2,1,0:T(8,128)} %project_peer.1, f32[2,256,1536]{2,1,0:T(8,128)} %get-tuple-element.44, f32[]{:T(128)} %bitcast.35, f32[]{:T(128)} %bitcast.33, f32[]{:T(128)} %bitcast.32, f32[]{:T(128)} %bitcast.31, f32[]{:T(128)} %bitcast.28, f32[]{:T(128)} %bitcast.21, ...), kind=kLoop, calls=%fused_computation.8 | loop fusion | flops 5505024 | bytes 9437216 | tf_op jit(solution)/shard_map/add | solution.py:1058
  115.2 3.7 collective-permute-start.2
  137.4 12.6 %collective-permute-done.1 = f32[256,1536]{1,0:T(8,128)} collective-permute-done((f32[256,1536]{1,0:T(8,128)S(1)}, f32[256,1536]{1,0:T(8,128)}, u32[]{:S(2)}, u32[]{:S(2)}) %collective-permute-start.1) | collective-permute-done | bytes 1572896 | tf_op jit(solution)/shard_map/ppermute | solution.py:1062
  153.2 4.4 %fusion.17 = (bf16[1,256,1536]{2,1,0:T(8,128)(2,1)S(1)}, bf16[1,256,1536]{2,1,0:T(8,128)(2,1)S(1)}) fusion(f32[2,256,1536]{2,1,0:T(8,128)} %get-tuple-element.44, pred[]{:T(512)S(6)} %gt.22, pred[]{:T(512)S(6)} %gt.21, f32[256,1536]{1,0:T(8,128)} %get-tuple-element.121, f32[256,1536]{1,0:T(8,128)} %collective-permute-done.1, f32[]{:T(128)S(6)} %convert_element_type.73, ...), kind=kLoop, calls=%fused_computation.41 | loop fusion | flops 3145728 | bytes 9437196 | tf_op jit(solution)/shard_map/stack | solution.py:1067
  158.9 12.2 %attend.1 = (bf16[1024,768]{1,0:T(8,128)(2,1)}, f32[1024,768]{1,0:T(8,128)}, f32[2,768]{1,0:T(2,128)}) custom-call(s32[2]{0:T(128)} %copy-done.20, bf16[1024,768]{1,0:T(8,128)(2,1)} %get-tuple-element.43.q_ref, bf16[2,256,1536]{2,1,0:T(8,128)(2,1)} %pad_maximum_fusion.1.s_ref, bf16[3072,768]{1,0:T(8,128)(2,1)} %bitcast.197, bf16[1024,768]{1,0:T(8,128)(2,1)} %bitcast.226), custom_call_target="tpu_custom_call" | custom-call | flops 2818572288 | bytes 10000000 | tf_op jit(solution)/shard_map/attend/pallas_call | solution.py:153
  171.8 34.7 %feed.1 = (bf16[1024,768]{1,0:T(8,128)(2,1)}, bf16[1024,3072]{1,0:T(8,128)(2,1)}, bf16[1024,3072]{1,0:T(8,128)(2,1)}, bf16[1024,768]{1,0:T(8,128)(2,1)}, bf16[10...) custom-call(f32[1024,768]{1,0:T(8,128)} %get-tuple-element.45.first_, ...), custom_call_target="tpu_custom_call" | custom-call | flops 19327352832 | bytes 30000000 | tf_op jit(solution)/shard_map/feed/pallas_call | solution.py:273
  206.6 15.6 %attend_back.1 = (bf16[1024,768]{1,0:T(8,128)(2,1)}, f32[2,256,1536]{2,1,0:T(8,128)}) custom-call(bf16[1024,768]{1,0:T(8,128)(2,1)} %get-tuple-element.43.q_ref, bf16[2,256,1536]{2,1,0:T(8,128)(2,1)} %pad_maximum_fusion.1.s_ref, bf16[1024,768]{1,0:T(8,128)(2,1)} %get-tuple-element.48.g_ref), custom_call_target="tpu_custom_call" | custom-call | flops 3221225472 | bytes 10000000 | tf_op jit(solution)/shard_map/attend_back/pallas_call | solution.py:344
  222.2 3.4 fusion.2
  228.7 3.3 collective-permute-start.5
  232.0 3.9 collective-permute-start.4
  238.0 4.3 %outer_query.1 = bf16[768,768]{1,0:T(8,128)(2,1)} custom-call(bf16[1024,768]{1,0:T(8,128)(2,1)} %bitcast.227, bf16[1024,768]{1,0:T(8,128)(2,1)} %get-tuple-element.50.refs_4_.r_ref), custom_call_target="tpu_custom_call" | custom-call | flops 1207959552 | bytes 20000000 | tf_op jit(solution)/shard_map/outer_query/pallas_call | solution.py:394
  242.3 4.3 %outer_out.1 = bf16[768,768]{1,0:T(8,128)(2,1)} custom-call(bf16[1024,768]{1,0:T(8,128)(2,1)} %get-tuple-element.58.l_ref, bf16[1024,768]{1,0:T(8,128)(2,1)} %get-tuple-element.59.r_ref), custom_call_target="tpu_custom_call" | custom-call | flops 1207959552 | bytes 20000000 | tf_op jit(solution)/shard_map/outer_out/pallas_call | solution.py:394
  246.7 9.4 %outer_down.1 = bf16[3072,768]{1,0:T(8,128)(2,1)} custom-call(bf16[1024,3072]{1,0:T(8,128)(2,1)} %get-tuple-element.55.l_ref, bf16[1024,768]{1,0:T(8,128)(2,1)} %get-tuple-element.56.r_ref), custom_call_target="tpu_custom_call" | custom-call | flops 4831838208 | bytes 20000000 | tf_op jit(solution)/shard_map/outer_down/pallas_call | solution.py:394
  256.0 9.2 %outer_up.1 = bf16[8,4,96,768]{3,2,1,0:T(8,128)(2,1)} custom-call(bf16[1024,768]{1,0:T(8,128)(2,1)} %get-tuple-element.53.l_ref, bf16[1024,3072]{1,0:T(8,128)(2,1)} %get-tuple-element.54.r_ref), custom_call_target="tpu_custom_call" | custom-call | flops 4831838208 | bytes 20000000 | tf_op jit(solution)/shard_map/outer_up/pallas_call | solution.py:375
  265.2 3.4 collective-permute-done.6.refs_3_
  268.6 17.4 %back.1 = (bf16[1024,1536]{1,0:T(8,128)(2,1)}, f32[2048,256]{1,0:T(8,128)}, f32[1024,768]{1,0:T(8,128)}) custom-call(f32[2,6]{1,0:T(2,128)} %concatenate.17.c_ref, s32[2,2]{1,0:T(2,128)} %pad_add_fusion.n_ref, bf16[2,512,256]{2,1,0:T(8,128)(2,1)} %maximum_select_fusion.e_ref, bf16[1024,1536]{1,0:T(8,128)(2,1)} %get-tuple-element.47.kv_ref, ...), custom_call_target="tpu_custom_call" | custom-call | flops 5234491392 | bytes 20000000 | tf_op jit(solution)/shard_map/back/pallas_call | solution.py:451
  287.8 5.8 %outer_keyval.1 = bf16[1536,768]{1,0:T(8,128)(2,1)} custom-call(bf16[1024,768]{1,0:T(8,128)(2,1)} %bitcast.228, bf16[1024,1536]{1,0:T(8,128)(2,1)} %get-tuple-element.57.r_ref), custom_call_target="tpu_custom_call" | custom-call | flops 2415919104 | bytes 20000000 | tf_op jit(solution)/shard_map/outer_keyval/pallas_call | solution.py:394
  295.2 98.0 %reduce_all.1 = (f32[96,768]{1,0:T(8,128)}, f32[96,768]{1,0:T(8,128)}, f32[96,768]{1,0:T(8,128)}, f32[4,2,64,256]{3,2,1,0:T(8,128)}, f32[2,2,4,2,8,256]{5,4,3,2,1,0:T(8,128)}) custom-call(bf16[2,4,2,2,96,768]{5,4,3,2,1,0:T(8,128)(2,1)} %bitcast.201, bf16[2,4,2,2,96,768]{5,4,3,2,1,0:T(8,128)(2,1)} %bitcast.200, bf16[4,2,96,768]{3,2,1,0:T(8,128)(2,1)} %bitcast.209, ...), custom_call_target="tpu_custom_call" | custom-call | tf_op jit(solution)/shard_map/reduce_all/pallas_call | solution.py:763
  399.2 3.5 fusion.10
  405.4 4.4 %fusion.11 = f32[24,96,96]{2,1,0:T(8,128)} fusion(f32[24,96,96]{2,1,0:T(8,128)} %param.24, f32[24,96,96]{2,1,0:T(8,128)S(1)} %pad_maximum_fusion.2), kind=kOutput, calls=%fused_computation.30 | convolution fusion | flops 255246336 | bytes 2654208 | tf_op jit(solution)/shard_map/tji,tjk->tik/dot_general | solution.py:890
  409.8 3.6 fusion.12
  (141 shorter events, 58.4 us)
Async XLA Ops:
  7.2 389.9 %copy-start = (f32[24,96,96]{2,1,0:T(8,128)S(1)}, f32[24,96,96]{2,1,0:T(8,128)}, u32[]{:S(2)}) copy-start(f32[24,96,96]{2,1,0:T(8,128)} %param.26) | copy-start | bytes 2654212
  7.2 164.6 %all-gather.2.cloned.1.call-start = ((), (), s32[]{:S(2)}) async-start(), calls=%async_computation | async-start | bytes 9732096 | tf_op jit(solution)/shard_map/all_gather | solution.py:926
  8.7 2.8 copy-start.21
  8.7 2.8 copy-start.22
  8.8 11.0 %copy-start.4 = (f32[512,256]{1,0:T(8,128)S(1)}, f32[512,256]{1,0:T(8,128)}, u32[]{:S(2)}) copy-start(f32[512,256]{1,0:T(8,128)} %param.27) | copy-start | bytes 1572868
  10.0 84.4 %collective-permute-start = (bf16[1024,768]{1,0:T(8,128)(2,1)}, bf16[1024,768]{1,0:T(8,128)(2,1)}, u32[]{:S(2)}, u32[]{:S(2)}) collective-permute-start(bf16[1024,768]{1,0:T(8,128)(2,1)} %bitcast.224), channel_id=1, source_target_pairs={{0,4},{4,0},{8,12},{12,8},{16,20},{20,16},{24,28},{28,24},{1,5},{5... | collective-permute-start | bytes 4718600 | tf_op jit(solution)/shard_map/ppermute | solution.py:1006
  12.4 123.3 %copy-start.20 = (s32[2]{0:T(128)}, s32[2]{0:T(128)S(1)}, u32[]{:S(2)}) copy-start(s32[2]{0:T(128)S(1)} %get-tuple-element.117.n_ref) | copy-start | bytes 28
  112.0 38.0 %collective-permute-start.1 = (f32[256,1536]{1,0:T(8,128)S(1)}, f32[256,1536]{1,0:T(8,128)}, u32[]{:S(2)}, u32[]{:S(2)}) collective-permute-start(f32[256,1536]{1,0:T(8,128)S(1)} %get-tuple-element.120), channel_id=1, source_target_pairs={{0,8},{4,12},{8,16},{12,20},{16,24},{20,28},{1,9},{5,13},{9,17},{1... | collective-permute-start | bytes 4718600 | tf_op jit(solution)/shard_map/ppermute | solution.py:1062
  115.2 37.9 %collective-permute-start.2 = (f32[256,1536]{1,0:T(8,128)}, f32[256,1536]{1,0:T(8,128)}, u32[]{:S(2)}, u32[]{:S(2)}) collective-permute-start(f32[256,1536]{1,0:T(8,128)} %get-tuple-element.121), channel_id=1, source_target_pairs={{8,0},{12,4},{16,8},{20,12},{24,16},{28,20},{9,1},{13,5},{17,9},{2... | collective-permute-start | bytes 4718600 | tf_op jit(solution)/shard_map/ppermute | solution.py:1063
  222.2 15.7 %copy-start.17 = (f32[4,768]{1,0:T(4,128)S(1)}, f32[4,768]{1,0:T(4,128)}, u32[]{:S(2)}) copy-start(f32[4,768]{1,0:T(4,128)} %get-tuple-element.61) | copy-start | bytes 36868
  225.6 39.6 %collective-permute-start.3 = (bf16[256,1536]{1,0:T(8,128)(2,1)}, bf16[256,1536]{1,0:T(8,128)(2,1)S(1)}, u32[]{:S(2)}, u32[]{:S(2)}) collective-permute-start(bf16[256,1536]{1,0:T(8,128)(2,1)} %get-tuple-element.123), channel_id=1, source_target_pairs={{0,4},{4,8},{8,12},{12,16},{16,20},{20,24},{24,28},{1,5},{5,9},{9,... | collective-permute-start | bytes 2359304 | tf_op jit(solution)/shard_map/ppermute | solution.py:1106
  228.7 36.5 %collective-permute-start.5 = (bf16[256,1536]{1,0:T(8,128)(2,1)}, bf16[256,1536]{1,0:T(8,128)(2,1)}, u32[]{:S(2)}, u32[]{:S(2)}) collective-permute-start(bf16[256,1536]{1,0:T(8,128)(2,1)} %get-tuple-element.123), channel_id=1, source_target_pairs={{0,8},{4,12},{8,16},{12,20},{16,24},{20,28},{1,9},{5,13},{9,17},{1... | collective-permute-start | bytes 2359304 | tf_op jit(solution)/shard_map/ppermute | solution.py:1106
  232.0 33.2 %collective-permute-start.4 = (bf16[256,1536]{1,0:T(8,128)(2,1)}, bf16[256,1536]{1,0:T(8,128)(2,1)}, u32[]{:S(2)}, u32[]{:S(2)}) collective-permute-start(bf16[256,1536]{1,0:T(8,128)(2,1)} %get-tuple-element.122), channel_id=1, source_target_pairs={{4,0},{8,4},{12,8},{16,12},{20,16},{24,20},{28,24},{5,1},{9,5},{13... | collective-permute-start | bytes 2359304 | tf_op jit(solution)/shard_map/ppermute | solution.py:1108
  235.9 32.7 %collective-permute-start.6 = (bf16[256,1536]{1,0:T(8,128)(2,1)}, bf16[256,1536]{1,0:T(8,128)(2,1)}, u32[]{:S(2)}, u32[]{:S(2)}) collective-permute-start(bf16[256,1536]{1,0:T(8,128)(2,1)} %get-tuple-element.122), channel_id=1, source_target_pairs={{8,0},{12,4},{16,8},{20,12},{24,16},{28,20},{9,1},{13,5},{17,9},{2... | collective-permute-start | bytes 2359304 | tf_op jit(solution)/shard_map/ppermute | solution.py:1108
  265.2 3.4 copy-start.8
  393.1 3.3 copy-start.14
  397.1 12.7 %copy-start.1 = (f32[24,96,96]{2,1,0:T(8,128)}, f32[24,96,96]{2,1,0:T(8,128)S(1)}, u32[]{:S(2)}) copy-start(f32[24,96,96]{2,1,0:T(8,128)S(1)} %pad_maximum_fusion.2) | copy-start | bytes 2654212
  405.4 4.4 %copy-start.7 = (f32[24,96,96]{2,1,0:T(8,128)S(1)}, f32[24,96,96]{2,1,0:T(8,128)}, u32[]{:S(2)}) copy-start(f32[24,96,96]{2,1,0:T(8,128)} %param.23) | copy-start | bytes 2654212
  409.8 3.6 copy-start.2
  409.8 3.6 copy-start.9
  413.4 2.9 copy-start.11
  416.3 3.3 copy-start.5
  416.3 3.3 copy-start.12
  417.8 4.1 copy-start.16
  (9 other events, 20.0 us)
Sparse Core Ops, SparseCore 0:
  11.5 92.7 all-gather.1

commit v4 on v3

--- a/solution.py
+++ b/solution.py
@@ -20,6 +20,7 @@
 rate_norm = 0.2
 highest = lax.Precision.HIGHEST
 VMEM_LIMIT = 60 * 1024 * 1024
+MESH_ID = pl.DeviceIdType.MESH
 
 
 def dot(a, b):
@@ -176,6 +177,215 @@
         cost_estimate=cost(2 * rows * width * (width + 4 * kp), 10e6, rows * kp * 12),
         name="attend",
     )(n_valid, q, summary, w_att, x)
+
+
+def forward_body(
+    depth, head, c_ref, n_ref, x_ref, px_ref, w_ref, e_ref, pe_ref, *refs
+):
+    q_ref, kv_ref, s_ref, mix_ref, sum_ref, stat_ref, part, unit, got, send, recv = refs
+    blocks, short, kp = e_ref.shape
+    width = x_ref.shape[1]
+    seq, mine = lax.axis_index("seq"), lax.axis_index("own")
+    z, y = seq // 2, seq % 2
+    along_y = (2 * z + (1 - y), mine)
+    after = (2 * lax.rem(z + 1, depth) + y, mine)
+    before = (2 * lax.rem(z + depth - 1, depth) + y, mine)
+    has_left, has_right = z > 0, z < depth - 1
+    shared = kp * 5 // 16
+    direct = kp - 2 * shared
+    barrier = pltpu.get_barrier_semaphore()
+    pl.semaphore_signal(barrier, inc=1, device_id=along_y, device_id_type=MESH_ID)
+
+    @pl.when(has_left)
+    def _():
+        pl.semaphore_signal(barrier, inc=1, device_id=before, device_id_type=MESH_ID)
+
+    @pl.when(has_right)
+    def _():
+        pl.semaphore_signal(barrier, inc=1, device_id=after, device_id_type=MESH_ID)
+
+    pl.semaphore_wait(barrier, 1 + jnp.minimum(z, 1) + jnp.minimum(depth - 1 - z, 1))
+
+    @pl.when(jnp.logical_not(has_left))
+    def _():
+        got[0] = jnp.zeros_like(got[0])
+
+    @pl.when(jnp.logical_not(has_right))
+    def _():
+        got[1] = jnp.zeros_like(got[1])
+
+    def copy(at, src, dst, there):
+        return pltpu.make_async_remote_copy(
+            src_ref=src,
+            dst_ref=dst,
+            send_sem=send.at[at],
+            recv_sem=recv.at[at],
+            device_id=there,
+            device_id_type=MESH_ID,
+        )
+
+    every = pl.ds(0, direct)
+    single = pl.ds(pl.multiple_of(direct + shared * y, 8), shared)
+    moves, hands = {}, {}
+    for kind in range(2):
+        cols = pl.ds(kind * width, width)
+        for side in range(2):
+            there = (after, before)[side]
+            at = (kind * 2 + side) * 3
+            moves[kind, side] = [
+                copy(at, unit.at[side, every, cols], got.at[side, every, cols], there),
+                copy(at + 1, unit.at[side, single, cols], got.at[side, single, cols], there),
+            ]
+            hands[kind, side] = copy(
+                at + 2, got.at[side, single, cols], got.at[side, single, cols], along_y
+            )
+    can_send = (has_right, has_left)
+    can_get = (has_left, has_right)
+
+    for kind in range(2):
+        cols = pl.ds(kind * width, width)
+        weight = pl.ds((1 + kind) * width, width)
+
+        def own_block(b, carry):
+            rows = pl.ds(pl.multiple_of(b * short, short), short)
+            kv = dot(x_ref[rows, :], w_ref[weight, :]).astype(BF)
+            kv_ref[rows, cols] = kv
+            total = dot_l(e_ref[b], kv)
+            part[b, :, cols] = total
+
+            @pl.when(b == 0)
+            def _():
+                for side in range(2):
+                    unit[side, :, cols] = c_ref[1 - side, b] * total
+
+            @pl.when(b > 0)
+            def _():
+                for side in range(2):
+                    unit[side, :, cols] += c_ref[1 - side, b] * total
+
+            return carry
+
+        def peer_block(b, carry):
+            rows = pl.ds(pl.multiple_of(b * short, short), short)
+            kv = dot(px_ref[rows, :], w_ref[weight, :]).astype(BF)
+            total = dot_l(pe_ref[b], kv)
+            for side in range(2):
+                unit[side, :, cols] += c_ref[1 - side, blocks + b] * total
+            return carry
+
+        lax.fori_loop(0, blocks, own_block, 0)
+        lax.fori_loop(0, blocks, peer_block, 0)
+        for side in range(2):
+
+            @pl.when(can_send[side])
+            def _():
+                for move in moves[kind, side]:
+                    move.start()
+
+    def query_block(b, carry):
+        rows = pl.ds(pl.multiple_of(b * short, short), short)
+        q_ref[rows, :] = dot(x_ref[rows, :], w_ref[pl.ds(0, width), :]).astype(BF)
+        return carry
+
+    lax.fori_loop(0, blocks, query_block, 0)
+    for kind in range(2):
+        for side in range(2):
+
+            @pl.when(can_get[side])
+            def _():
+                moves[kind, side][1].wait_recv()
+                hands[kind, side].start()
+
+    for kind in range(2):
+        for side in range(2):
+
+            @pl.when(can_get[side])
+            def _():
+                moves[kind, side][0].wait_recv()
+                hands[kind, side].wait_recv()
+
+    slab = 64
+
+    def combine(i, carry):
+        b, at = i // (kp // slab), i % (kp // slab)
+        rows = pl.ds(pl.multiple_of(at * slab, slab), slab)
+        total = c_ref[2, b] * unit[1, rows, :] + c_ref[3, b] * got[0, rows, :]
+        total = total + c_ref[4, b] * unit[0, rows, :] + c_ref[5, b] * got[1, rows, :]
+        s_ref[b, rows, :] = (total + c_ref[6, b] * part[b, rows, :]).astype(BF)
+        return carry
+
+    lax.fori_loop(0, blocks * (kp // slab), combine, 0)
+    pairs = width // (2 * head)
+    scale = head ** (-0.5)
+    low_lane = lax.broadcasted_iota(jnp.int32, (kp, 2 * head), 1) < head
+
+    def attend_block(b, carry):
+        rows = pl.ds(pl.multiple_of(b * short, short), short)
+        for j in range(pairs):
+            cols = pl.ds(j * 2 * head, 2 * head)
+            keys = head_pair(s_ref[b, :, cols], low_lane)
+            values = head_pair(s_ref[b, :, pl.ds(width + j * 2 * head, 2 * head)], low_lane)
+            scores = dot_t(q_ref[rows, cols], keys) * scale
+            prob = jnp.concatenate(softmax_pair(scores, kp), axis=1).astype(BF)
+            mix_ref[rows, cols] = dot(prob, values).astype(BF)
+        branch = dot(mix_ref[rows, :], w_ref[pl.ds(3 * width, width), :])
+        first = x_ref[rows, :].astype(F32) + branch
+        sum_ref[rows, :] = first
+        keep = (lax.broadcasted_iota(jnp.int32, (short, 1), 0) < n_ref[b]).astype(F32)
+        stat_ref[...] += jnp.concatenate(
+            [
+                jnp.sum(keep * first * first, axis=0, keepdims=True),
+                jnp.sum(keep * branch * branch, axis=0, keepdims=True),
+            ],
+            axis=0,
+        )
+        return carry
+
+    stat_ref[...] = jnp.zeros_like(stat_ref)
+    lax.fori_loop(0, blocks, attend_block, 0)
+    for kind in range(2):
+        for side in range(2):
+
+            @pl.when(can_send[side])
+            def _():
+                for move in moves[kind, side]:
+                    move.wait_send()
+
+            @pl.when(can_get[side])
+            def _():
+                hands[kind, side].wait_send()
+
+
+def forward(coef, n_valid, x, peer_x, w_att, e_own, e_peer, head, peers):
+    rows, width = x.shape
+    blocks, short, kp = e_own.shape
+    vmem = pl.BlockSpec(memory_space=pltpu.VMEM)
+    smem = pl.BlockSpec(memory_space=pltpu.SMEM)
+    return pl.pallas_call(
+        functools.partial(forward_body, peers // 2, head),
+        in_specs=[smem] * 2 + [vmem] * 5,
+        out_specs=[vmem] * 6,
+        out_shape=[
+            jax.ShapeDtypeStruct((rows, width), BF),
+            jax.ShapeDtypeStruct((rows, 2 * width), BF),
+            jax.ShapeDtypeStruct((blocks, kp, 2 * width), BF),
+            jax.ShapeDtypeStruct((rows, width), BF),
+            jax.ShapeDtypeStruct((rows, width), F32),
+            jax.ShapeDtypeStruct((2, width), F32),
+        ],
+        scratch_shapes=[
+            pltpu.VMEM((blocks, kp, 2 * width), F32),
+            pltpu.VMEM((2, kp, 2 * width), F32),
+            pltpu.VMEM((2, kp, 2 * width), F32),
+            pltpu.SemaphoreType.DMA((12,)),
+            pltpu.SemaphoreType.DMA((12,)),
+        ],
+        compiler_params=pltpu.CompilerParams(
+            collective_id=3, has_side_effects=True, vmem_limit_bytes=VMEM_LIMIT
+        ),
+        cost_estimate=cost(2 * rows * width * width * 8, 200e6, rows * kp * 12),
+        name="forward",
+    )(coef, n_valid, x, peer_x, w_att, e_own, e_peer)
 
 
 def normalize(values):
@@ -481,9 +691,6 @@
     )(coef, places, e_rows, kv, grad_parts, *far_parts, dq, w_att, grad_first)
 
 
-MESH_ID = pl.DeviceIdType.MESH
-
-
 def reduce_body(depth, half, n_src, extra_keep, *refs):
     sources = refs[:n_src]
     outs = refs[n_src : n_src + 5]
@@ -645,38 +852,38 @@
             return carry
 
         lax.fori_loop(0, depth * 4, body, 0)
-        state["e1"] = [push(e_sum.at[:, :, 1 - x], e_got1, along_x)]
-
-    def extra_1():
-        wait_recv(state["e1"])
-
-        def body(i, carry):
-            zz, yy = i // 2, i % 2
-            e_sum1[zz, yy] = e_sum[zz, yy, x] + e_got1[zz, yy]
-            return carry
-
-        lax.fori_loop(0, depth * 2, body, 0)
-        state["e2"] = [push(e_sum1.at[:, 1 - y], e_got2, along_y)]
-
-    def extra_2():
-        wait_recv(state["e2"])
-
-        def body(zz, carry):
-            e_sum2[zz] = e_sum1[zz, y] + e_got2[zz]
-            return carry
-
-        lax.fori_loop(0, depth, body, 0)
         state["ez"] = [
-            push(e_sum2.at[lax.rem(z + d, depth)], e_gotz.at[d - 1], along_z[d - 1])
+            push(e_sum.at[lax.rem(z + d, depth)], e_gotz.at[d - 1], along_z[d - 1])
             for d in range(1, depth)
         ]
 
+    def extra_1():
+        wait_recv(state["ez"])
+
+        def body(i, carry):
+            yy, xx = i // 2, i % 2
+            total = e_sum[z, yy, xx]
+            for d in range(depth - 1):
+                total = total + e_gotz[d, yy, xx]
+            e_sum1[yy, xx] = total
+            return carry
+
+        lax.fori_loop(0, 4, body, 0)
+        state["e1"] = [push(e_sum1.at[:, 1 - x], e_got1, along_x)]
+
+    def extra_2():
+        wait_recv(state["e1"])
+
+        def body(yy, carry):
+            e_sum2[yy] = e_sum1[yy, x] + e_got1[yy]
+            return carry
+
+        lax.fori_loop(0, 2, body, 0)
+        state["e2"] = [push(e_sum2.at[1 - y], e_got2, along_y)]
+
     def extra_z():
-        wait_recv(state["ez"])
-        total = e_sum2[z]
-        for d in range(depth - 1):
-            total = total + e_gotz[d]
-        e_all[z, y] = total
+        wait_recv(state["e2"])
+        e_all[z, y] = e_sum2[y] + e_got2[...]
         state["gz"] = [push(e_all.at[z, y], e_all.at[z, y], there) for there in along_z]
 
     def extra_gather_y():
@@ -749,11 +956,11 @@
         pltpu.VMEM((depth, 4, e_rows_all, kp), F32),
         pltpu.VMEM((depth, 4, e_rows_all, kp), F32),
         pltpu.VMEM((depth, 2, 2, e_rows_all, kp), F32),
-        pltpu.VMEM((depth, 2, e_rows_all, kp), F32),
-        pltpu.VMEM((depth, 2, e_rows_all, kp), F32),
-        pltpu.VMEM((depth, e_rows_all, kp), F32),
-        pltpu.VMEM((depth, e_rows_all, kp), F32),
-        pltpu.VMEM((depth - 1, e_rows_all, kp), F32),
+        pltpu.VMEM((2, e_rows_all, kp), F32),
+        pltpu.VMEM((2, 2, e_rows_all, kp), F32),
+        pltpu.VMEM((e_rows_all, kp), F32),
+        pltpu.VMEM((2, e_rows_all, kp), F32),
+        pltpu.VMEM((depth - 1, 2, 2, e_rows_all, kp), F32),
         pltpu.VMEM((depth, 2, e_rows_all, kp), F32),
         pltpu.VMEM((2, 2, depth, 2, 8, kp), F32),
         pltpu.SemaphoreType.DMA((messages,)),
@@ -1040,41 +1247,59 @@
         return jnp.where(keep, rows, jnp.zeros((), BF))
 
     e_own = proj_rows(own_at)
-    e_own_t = e_own.transpose(0, 2, 1)
-    e_peer_t = proj_rows(peer_at).transpose(0, 2, 1)
+    e_peer = proj_rows(peer_at)
     n_own = take(n_valid, own_at)
 
-    query, keyval, part_own = project(x, w_att, e_own_t, True)
-    (part_peer,) = project(peer_x, w_att, e_peer_t, False)
     coef = lambda flag, at: take(flag, at).astype(F32)
-
-    def unit_sum(flag):
-        mine = coef(flag, own_at)
-        theirs = coef(flag, peer_at)
-        total = mine[0] * part_own[0]
-        for b in range(1, blocks):
-            total = total + mine[b] * part_own[b]
-        for b in range(blocks):
-            total = total + theirs[b] * part_peer[b]
-        return total
-
-    head_sum, tail_sum = unit_sum(is_head), unit_sum(is_tail)
-    from_left = lax.ppermute(tail_sum, "seq", [(i, i + 2) for i in range(peers - 2)])
-    from_right = lax.ppermute(head_sum, "seq", [(i + 2, i) for i in range(peers - 2)])
     head_cross = (b_start[0] < unit_start).astype(F32)
     tail_cross = (b_end[-1] > unit_end).astype(F32)
     own_head, own_tail = coef(is_head, own_at), coef(is_tail, own_at)
-    summary = jnp.stack(
-        [
-            jnp.where(
-                own_head[b] > 0,
-                head_sum + head_cross * from_left,
-                jnp.where(own_tail[b] > 0, tail_sum + tail_cross * from_right, part_own[b]),
-            ).astype(BF)
-            for b in range(blocks)
-        ]
-    )
-    mixed, first_sum, row_sums = attend(n_own, query, summary, w_att, x, head)
+    if fused:
+        pick_tail = (1.0 - own_head) * own_tail
+        unit_coef = lambda flag: jnp.concatenate([coef(flag, own_at), coef(flag, peer_at)])
+        pad = lambda v: jnp.concatenate([v, jnp.zeros((blocks,), F32)])
+        table = jnp.stack(
+            [
+                unit_coef(is_head),
+                unit_coef(is_tail),
+                pad(own_head),
+                pad(own_head * head_cross),
+                pad(pick_tail),
+                pad(pick_tail * tail_cross),
+                pad((1.0 - own_head) * (1.0 - own_tail)),
+            ]
+        )
+        query, keyval, summary, mixed, first_sum, row_sums = forward(
+            table, n_own, x, peer_x, w_att, e_own, e_peer, head, peers
+        )
+    else:
+        query, keyval, part_own = project(x, w_att, e_own.transpose(0, 2, 1), True)
+        (part_peer,) = project(peer_x, w_att, e_peer.transpose(0, 2, 1), False)
+
+        def unit_sum(flag):
+            mine = coef(flag, own_at)
+            theirs = coef(flag, peer_at)
+            total = mine[0] * part_own[0]
+            for b in range(1, blocks):
+                total = total + mine[b] * part_own[b]
+            for b in range(blocks):
+                total = total + theirs[b] * part_peer[b]
+            return total
+
+        head_sum, tail_sum = unit_sum(is_head), unit_sum(is_tail)
+        from_left = lax.ppermute(tail_sum, "seq", [(i, i + 2) for i in range(peers - 2)])
+        from_right = lax.ppermute(head_sum, "seq", [(i + 2, i) for i in range(peers - 2)])
+        summary = jnp.stack(
+            [
+                jnp.where(
+                    own_head[b] > 0,
+                    head_sum + head_cross * from_left,
+                    jnp.where(own_tail[b] > 0, tail_sum + tail_cross * from_right, part_own[b]),
+                ).astype(BF)
+                for b in range(blocks)
+            ]
+        )
+        mixed, first_sum, row_sums = attend(n_own, query, summary, w_att, x, head)
     (
         result,
         hidden,

time: 437 us -> 423 us (0.968)
  Pallas kernels: 281 us -> 315 us
  waiting for transfers between devices: 19.2 us -> 2.7 us
  other arithmetic: 31 us -> 17 us
  starting transfers between devices: 20.4 us -> 11.7 us
  local copies, waits for them, and re-layouts: 24.8 us -> 20.4 us
    pallas_call x3 -> x1, Pallas kernels: 29.2 us -> 70.3 us  [forward(): pl.pallas_call(functools.partial(forward_body, peers // 2, head), in_spec...]
    ppermute x2 -> x0, waiting for transfers between devices: 15.8 us -> none  [the longest x1 12.6 us: per_device(): lax.ppermute(tail_sum, 'seq', [(i, i + 2) for i in range(peers - 2)])]
    pallas_call x1, Pallas kernels: 53.7 us -> 42.2 us  [gather_bands(): pl.pallas_call(functools.partial(gather_body, depth, size // 2), in_specs...]
    add x1 -> x0, other arithmetic: 9.89 us -> none  [unit_sum(): total = total + theirs[b] * part_peer[b]]
    ppermute x2 -> x0, starting transfers between devices: 6.87 us -> none  [the longest x1 3.66 us: per_device(): lax.ppermute(head_sum, 'seq', [(i + 2, i) for i in range(peers - 2)])]
    another operation x3, other arithmetic: 5.91 us -> 0.33 us  [the longest x2 5.73 us: per_device(): jnp.stack([jnp.where(own_head[b] > 0, head_sum + head_cross * from_left,...]
  transfers between devices with their start and end apart: 8 -> 6, of which waited for: 3 -> 1; matrix products, arithmetic and copies ran while one was open for 9% -> 5% of each run, Pallas kernels for 26% -> 34%
where the time goes in v4:
time: 423 us; the launch traced here: 415 us
  Pallas kernels  315 us (74%)
  between operations  30.3 us (7%)
  local copies, waits for them, and re-layouts  20.4 us (5%)
  matrix products  18 us (4%)
  other arithmetic  17 us (4%)
  starting transfers between devices  11.7 us (3%)
    pallas_call x1, Pallas kernels, reduce_all(): pl.pallas_call(functools.partial(reduce_body, depth, half, n_src, keep),...  101 us
    pallas_call x1, Pallas kernels, forward(): pl.pallas_call(functools.partial(forward_body, peers // 2, head), in_spec...  70.3 us
    pallas_call x1, Pallas kernels, gather_bands(): pl.pallas_call(functools.partial(gather_body, depth, size // 2), in_specs...  42.2 us
    pallas_call x1, Pallas kernels, feed(): pl.pallas_call(functools.partial(feed_body, chunks), grid=(rows // tile,)...  34.9 us
    pallas_call x4, Pallas kernels, outer_rows(): pl.pallas_call(functools.partial(outer_body, False), grid=(tall * wide,),...  24.1 us
    pallas_call x1, Pallas kernels, back(): pl.pallas_call(functools.partial(back_body, width, blocks), grid_spec=plt...  17.4 us
    pallas_call x1, Pallas kernels, attend_back(): pl.pallas_call(functools.partial(attend_back_body, width, head, kp), grid...  15.7 us
    pallas_call x1, Pallas kernels, outer_up(): pl.pallas_call(functools.partial(outer_body, True), grid=(chunks,), in_sp...  9.25 us
  transfers between devices with their start and end apart: 6, of which 1 were waited for; matrix products, arithmetic and copies ran while one was open for 5% of the time, Pallas kernels for 34%

profile of v4, /device:TPU:9, one launch (start us, length us, event | category | flops | bytes accessed | tf_op | source)
XLA Modules:
  0.0 415.4 jit_solution(6557266979147310597)
XLA Ops:
  39.0 42.2 %gather_bands.1 = (bf16[4,2,2,2,96,768]{5,4,3,2,1,0:T(8,128)(2,1)}, bf16[2,2,512,256]{3,2,1,0:T(8,128)(2,1)}) custom-call(bf16[96,768]{1,0:T(8,128)(2,1)} %reshape.177.band_ref, bf16[512,256]{1,0:T(8,128)(2,1)} %convert_element_type.70.proj_ref), custom_call_target="tpu_custom_call" | custom-call | flops 1000000000 | bytes 90000000 | tf_op jit(solution)/shard_map/gather_bands/pallas_call | solution.py:1072
  85.4 70.3 %forward.1 = (bf16[1024,768]{1,0:T(8,128)(2,1)}, bf16[1024,1536]{1,0:T(8,128)(2,1)}, bf16[2,256,1536]{2,1,0:T(8,128)(2,1)}, bf16[1024,768]{1,0:T(8,128)(2,1)}, f32[1024,768]{1,0:T(8,128)}, /*index=5*/f32[2,768]{1,0:T(2,128)}) custom-call(f32[7,4]{1,0:T(8,128)} %stack.70.c_ref, s32[2]{0:T(128)} %copy-done.22, bf16[1024,768]{1,0:T(8,128)(2,1)} %bitcast.177, ...), custom_call_target="tpu_custom_call" | custom-call | flops 9663676416 | bytes 200000000 | tf_op jit(solution)/shard_map/forward/pallas_call | solution.py:364
  157.0 34.9 %feed.1 = (bf16[1024,768]{1,0:T(8,128)(2,1)}, bf16[1024,3072]{1,0:T(8,128)(2,1)}, bf16[1024,3072]{1,0:T(8,128)(2,1)}, bf16[1024,768]{1,0:T(8,128)(2,1)}, bf16[10...) custom-call(f32[1024,768]{1,0:T(8,128)} %get-tuple-element.43.first_, ...), custom_call_target="tpu_custom_call" | custom-call | flops 19327352832 | bytes 30000000 | tf_op jit(solution)/shard_map/feed/pallas_call | solution.py:483
  191.9 15.7 %attend_back.1 = (bf16[1024,768]{1,0:T(8,128)(2,1)}, f32[2,256,1536]{2,1,0:T(8,128)}) custom-call(bf16[1024,768]{1,0:T(8,128)(2,1)} %get-tuple-element.46.q_ref, bf16[2,256,1536]{2,1,0:T(8,128)(2,1)} %get-tuple-element.47.s_ref, bf16[1024,768]{1,0:T(8,128)(2,1)} %get-tuple-element.48.g_ref), custom_call_target="tpu_custom_call" | custom-call | flops 3221225472 | bytes 10000000 | tf_op jit(solution)/shard_map/attend_back/pallas_call | solution.py:554
  207.6 3.4 fusion.2
  211.0 3.4 collective-permute-start.1
  214.4 1.9 collective-permute-start.3
  216.3 3.1 collective-permute-start.2
  219.5 1.9 collective-permute-start.4
  223.0 4.3 %outer_query.1 = bf16[768,768]{1,0:T(8,128)(2,1)} custom-call(bf16[1024,768]{1,0:T(8,128)(2,1)} %bitcast.178, bf16[1024,768]{1,0:T(8,128)(2,1)} %get-tuple-element.50.refs_4_.r_ref), custom_call_target="tpu_custom_call" | custom-call | flops 1207959552 | bytes 20000000 | tf_op jit(solution)/shard_map/outer_query/pallas_call | solution.py:604
  227.3 4.3 %outer_out.1 = bf16[768,768]{1,0:T(8,128)(2,1)} custom-call(bf16[1024,768]{1,0:T(8,128)(2,1)} %get-tuple-element.58.l_ref, bf16[1024,768]{1,0:T(8,128)(2,1)} %get-tuple-element.59.r_ref), custom_call_target="tpu_custom_call" | custom-call | flops 1207959552 | bytes 20000000 | tf_op jit(solution)/shard_map/outer_out/pallas_call | solution.py:604
  231.6 9.6 %outer_down.1 = bf16[3072,768]{1,0:T(8,128)(2,1)} custom-call(bf16[1024,3072]{1,0:T(8,128)(2,1)} %get-tuple-element.55.l_ref, bf16[1024,768]{1,0:T(8,128)(2,1)} %get-tuple-element.56.r_ref), custom_call_target="tpu_custom_call" | custom-call | flops 4831838208 | bytes 20000000 | tf_op jit(solution)/shard_map/outer_down/pallas_call | solution.py:604
  241.2 9.3 %outer_up.1 = bf16[8,4,96,768]{3,2,1,0:T(8,128)(2,1)} custom-call(bf16[1024,768]{1,0:T(8,128)(2,1)} %get-tuple-element.53.l_ref, bf16[1024,3072]{1,0:T(8,128)(2,1)} %get-tuple-element.54.r_ref), custom_call_target="tpu_custom_call" | custom-call | flops 4831838208 | bytes 20000000 | tf_op jit(solution)/shard_map/outer_up/pallas_call | solution.py:585
  250.5 2.7 collective-permute-done.4.refs_3_
  253.2 17.4 %back.1 = (bf16[1024,1536]{1,0:T(8,128)(2,1)}, f32[2048,256]{1,0:T(8,128)}, f32[1024,768]{1,0:T(8,128)}) custom-call(f32[2,6]{1,0:T(2,128)} %concatenate.45.c_ref, s32[2,2]{1,0:T(2,128)} %pad_add_fusion.n_ref, bf16[2,512,256]{2,1,0:T(8,128)(2,1)} %maximum_select_fusion.e_ref, bf16[1024,1536]{1,0:T(8,128)(2,1)} %get-tuple-element.45.kv_ref, ...), custom_call_target="tpu_custom_call" | custom-call | flops 5234491392 | bytes 20000000 | tf_op jit(solution)/shard_map/back/pallas_call | solution.py:661
  270.6 1.8 copy.66
  272.3 5.8 %outer_keyval.1 = bf16[1536,768]{1,0:T(8,128)(2,1)} custom-call(bf16[1024,768]{1,0:T(8,128)(2,1)} %bitcast.179, bf16[1024,1536]{1,0:T(8,128)(2,1)} %get-tuple-element.57.r_ref), custom_call_target="tpu_custom_call" | custom-call | flops 2415919104 | bytes 20000000 | tf_op jit(solution)/shard_map/outer_keyval/pallas_call | solution.py:604
  278.1 1.6 pad_maximum_fusion.refs_5_
  279.8 101.5 %reduce_all.1 = (f32[96,768]{1,0:T(8,128)}, f32[96,768]{1,0:T(8,128)}, f32[96,768]{1,0:T(8,128)}, f32[4,2,64,256]{3,2,1,0:T(8,128)}, f32[2,2,4,2,8,256]{5,4,3,2,1,0:T(8,128)}) custom-call(bf16[2,4,2,2,96,768]{5,4,3,2,1,0:T(8,128)(2,1)} %bitcast.153, bf16[2,4,2,2,96,768]{5,4,3,2,1,0:T(8,128)(2,1)} %bitcast.152, bf16[4,2,96,768]{3,2,1,0:T(8,128)(2,1)} %bitcast.161, ...), custom_call_target="tpu_custom_call" | custom-call | tf_op jit(solution)/shard_map/reduce_all/pallas_call | solution.py:970
  385.8 2.1 fusion.24
  387.9 2.5 fusion.4
  391.8 4.4 %fusion.5 = f32[24,96,96]{2,1,0:T(8,128)} fusion(f32[24,96,96]{2,1,0:T(8,128)} %param.24, f32[24,96,96]{2,1,0:T(8,128)S(1)} %pad_maximum_fusion.1), kind=kOutput, calls=%fused_computation.11 | convolution fusion | flops 255246336 | bytes 2654208 | tf_op jit(solution)/shard_map/tji,tjk->tik/dot_general | solution.py:1097
  396.3 3.6 fusion.6
  402.4 1.9 fusion.9
  (136 shorter events, 35.5 us)
Async XLA Ops:
  7.2 378.6 %copy-start = (f32[24,96,96]{2,1,0:T(8,128)S(1)}, f32[24,96,96]{2,1,0:T(8,128)}, u32[]{:S(2)}) copy-start(f32[24,96,96]{2,1,0:T(8,128)} %param.26) | copy-start | bytes 2654212
  7.2 149.8 %all-gather.2.cloned.1.call-start = ((), (), s32[]{:S(2)}) async-start(), calls=%async_computation | async-start | bytes 9732096 | tf_op jit(solution)/shard_map/all_gather | solution.py:1133
  8.7 2.8 copy-start.23
  8.7 2.8 copy-start.24
  8.7 13.4 %copy-start.3 = (f32[24,96,96]{2,1,0:T(8,128)S(1)}, f32[24,96,96]{2,1,0:T(8,128)}, u32[]{:S(2)}) copy-start(f32[24,96,96]{2,1,0:T(8,128)} %param.22) | copy-start | bytes 2654212
  10.0 75.4 %collective-permute-start = (bf16[1024,768]{1,0:T(8,128)(2,1)}, bf16[1024,768]{1,0:T(8,128)(2,1)}, u32[]{:S(2)}, u32[]{:S(2)}) collective-permute-start(bf16[1024,768]{1,0:T(8,128)(2,1)} %bitcast.176), channel_id=1, source_target_pairs={{0,4},{4,0},{8,12},{12,8},{16,20},{20,16},{24,28},{28,24},{1,5},{5... | collective-permute-start | bytes 4718600 | tf_op jit(solution)/shard_map/ppermute | solution.py:1213
  27.8 55.4 %copy-start.22 = (s32[2]{0:T(128)}, s32[2]{0:T(128)S(1)}, u32[]{:S(2)}) copy-start(s32[2]{0:T(128)S(1)} %get-tuple-element.117.n_ref) | copy-start | bytes 28
  211.0 39.5 %collective-permute-start.1 = (bf16[256,1536]{1,0:T(8,128)(2,1)}, bf16[256,1536]{1,0:T(8,128)(2,1)S(1)}, u32[]{:S(2)}, u32[]{:S(2)}) collective-permute-start(bf16[256,1536]{1,0:T(8,128)(2,1)} %get-tuple-element.124), channel_id=1, source_target_pairs={{0,4},{4,8},{8,12},{12,16},{16,20},{20,24},{24,28},{1,5},{5,9},{9,... | collective-permute-start | bytes 2359304 | tf_op jit(solution)/shard_map/ppermute | solution.py:1331
  214.4 36.1 %collective-permute-start.3 = (bf16[256,1536]{1,0:T(8,128)(2,1)}, bf16[256,1536]{1,0:T(8,128)(2,1)S(1)}, u32[]{:S(2)}, u32[]{:S(2)}) collective-permute-start(bf16[256,1536]{1,0:T(8,128)(2,1)} %get-tuple-element.124), channel_id=1, source_target_pairs={{0,8},{4,12},{8,16},{12,20},{16,24},{20,28},{1,9},{5,13},{9,17},{1... | collective-permute-start | bytes 2359304 | tf_op jit(solution)/shard_map/ppermute | solution.py:1331
  216.3 34.2 %collective-permute-start.2 = (bf16[256,1536]{1,0:T(8,128)(2,1)}, bf16[256,1536]{1,0:T(8,128)(2,1)S(1)}, u32[]{:S(2)}, u32[]{:S(2)}) collective-permute-start(bf16[256,1536]{1,0:T(8,128)(2,1)} %get-tuple-element.123), channel_id=1, source_target_pairs={{4,0},{8,4},{12,8},{16,12},{20,16},{24,20},{28,24},{5,1},{9,5},{13... | collective-permute-start | bytes 2359304 | tf_op jit(solution)/shard_map/ppermute | solution.py:1333
  219.5 33.7 %collective-permute-start.4 = (bf16[256,1536]{1,0:T(8,128)(2,1)}, bf16[256,1536]{1,0:T(8,128)(2,1)}, u32[]{:S(2)}, u32[]{:S(2)}) collective-permute-start(bf16[256,1536]{1,0:T(8,128)(2,1)} %get-tuple-element.123), channel_id=1, source_target_pairs={{8,0},{12,4},{16,8},{20,12},{24,16},{28,20},{9,1},{13,5},{17,9},{2... | collective-permute-start | bytes 2359304 | tf_op jit(solution)/shard_map/ppermute | solution.py:1333
  250.5 2.7 copy-start.9
  250.5 2.7 copy-start.11
  250.5 2.7 copy-start.10
  381.3 3.3 copy-start.17
  385.8 10.4 %copy-start.1 = (f32[24,96,96]{2,1,0:T(8,128)}, f32[24,96,96]{2,1,0:T(8,128)S(1)}, u32[]{:S(2)}) copy-start(f32[24,96,96]{2,1,0:T(8,128)S(1)} %pad_maximum_fusion.1) | copy-start | bytes 2654212
  391.8 4.4 %copy-start.8 = (f32[24,96,96]{2,1,0:T(8,128)S(1)}, f32[24,96,96]{2,1,0:T(8,128)}, u32[]{:S(2)}) copy-start(f32[24,96,96]{2,1,0:T(8,128)} %param.23) | copy-start | bytes 2654212
  396.2 3.6 copy-start.2
  396.2 3.6 copy-start.12
  402.4 3.1 copy-start.20
  402.4 3.1 copy-start.21
  402.4 3.7 copy-start.6
  402.4 3.7 copy-start.15
  404.3 4.1 copy-start.19
  (9 other events, 15.5 us)
Sparse Core Ops, SparseCore 0:
  11.5 102.1 all-gather.1

commit v5 on v4

--- a/solution.py
+++ b/solution.py
@@ -49,6 +49,81 @@
 
 def cost(flops, nbytes, trans=0):
     return pl.CostEstimate(flops=int(flops), bytes_accessed=int(nbytes), transcendentals=int(trans))
+
+
+def tables_body(blocks, rows_here, l_ref, o_ref, v_ref, i_ref, f_ref, b_ref):
+    seq = lax.axis_index("seq")
+    side = seq % 2
+    row_start = seq * rows_here
+    row_end = row_start + rows_here
+    unit_start = (seq - side) * rows_here
+    peer_start = (seq + 1 - 2 * side) * rows_here
+    flag = lambda cond: jnp.where(cond, 1.0, 0.0).astype(F32)
+
+    def locate(row):
+        def body(i, carry):
+            at, start, end, off, count = carry
+            stop = at + l_ref[0, i]
+            inside = jnp.logical_and(row >= at, row < stop)
+            pick = lambda new, old: jnp.where(inside, new, old)
+            return (
+                stop,
+                pick(at, start),
+                pick(stop, end),
+                pick(o_ref[0, i], off),
+                pick(v_ref[0, i], count),
+            )
+
+        zero = jnp.int32(0)
+        return lax.fori_loop(0, l_ref.shape[1], body, (zero,) * 5)[1:]
+
+    starts, ends = [], []
+    for k in range(2 * blocks):
+        row = row_start + SHORT * k if k < blocks else peer_start + SHORT * (k - blocks)
+        start, end, off, count = locate(row)
+        starts.append(start)
+        ends.append(end)
+        i_ref[0, k] = off + row - start
+        i_ref[1, k] = jnp.clip(count - (row - start), 0, SHORT)
+    first = jnp.where(side == 0, starts[0], starts[blocks])
+    last = jnp.where(side == 0, starts[-1], starts[blocks - 1])
+    last_end = jnp.where(side == 0, ends[-1], ends[blocks - 1])
+    head_cross = flag(first < unit_start)
+    tail_cross = flag(last_end > unit_start + 2 * rows_here)
+    for k in range(2 * blocks):
+        is_head, is_tail = flag(starts[k] == first), flag(starts[k] == last)
+        pick_tail = (1.0 - is_head) * is_tail
+        f_ref[0, k] = is_head
+        f_ref[1, k] = is_tail
+        f_ref[2, k] = is_head
+        f_ref[3, k] = is_head * head_cross
+        f_ref[4, k] = pick_tail
+        f_ref[5, k] = pick_tail * tail_cross
+        f_ref[6, k] = (1.0 - is_head) * (1.0 - is_tail)
+    own_last, own_end = starts[blocks - 1], ends[blocks - 1]
+    for k in range(blocks):
+        at_head, at_tail = flag(starts[k] == starts[0]), flag(starts[k] == own_last)
+        for other in range(blocks):
+            b_ref[k, other] = flag(starts[k] == starts[other])
+        for far in range(2):
+            reach = far * rows_here
+            b_ref[k, blocks + 2 * far] = at_head * flag(starts[0] < row_start - reach)
+            b_ref[k, blocks + 2 * far + 1] = at_tail * flag(own_end > row_end + reach)
+
+
+def tables(lengths, offsets, valid_count, blocks, rows_here):
+    smem = pl.BlockSpec(memory_space=pltpu.SMEM)
+    return pl.pallas_call(
+        functools.partial(tables_body, blocks, rows_here),
+        in_specs=[smem] * 3,
+        out_specs=[smem] * 3,
+        out_shape=[
+            jax.ShapeDtypeStruct((2, 2 * blocks), jnp.int32),
+            jax.ShapeDtypeStruct((7, 2 * blocks), F32),
+            jax.ShapeDtypeStruct((blocks, blocks + 4), F32),
+        ],
+        name="tables",
+    )(lengths, offsets, valid_count)
 
 
 def project_body(width, with_query, x_ref, w_ref, e_ref, *outs):
@@ -331,7 +406,7 @@
         branch = dot(mix_ref[rows, :], w_ref[pl.ds(3 * width, width), :])
         first = x_ref[rows, :].astype(F32) + branch
         sum_ref[rows, :] = first
-        keep = (lax.broadcasted_iota(jnp.int32, (short, 1), 0) < n_ref[b]).astype(F32)
+        keep = (lax.broadcasted_iota(jnp.int32, (short, 1), 0) < n_ref[1, b]).astype(F32)
         stat_ref[...] += jnp.concatenate(
             [
                 jnp.sum(keep * first * first, axis=0, keepdims=True),
@@ -693,15 +768,15 @@
 
 def reduce_body(depth, half, n_src, extra_keep, *refs):
     sources = refs[:n_src]
-    outs = refs[n_src : n_src + 5]
+    grads, shares_out, rows_out = refs[n_src : n_src + 3]
     (own, got_c, sum_c, got_a, got_b, sum_a, sum_b, got_a2, got_b2, sum_z, got_z) = refs[
-        n_src + 5 : n_src + 16
+        n_src + 3 : n_src + 14
     ]
-    keep_a, keep_b, keep_z = refs[n_src + 16 : n_src + 19]
+    keep_a, keep_b, keep_z = refs[n_src + 14 : n_src + 17]
     (e_own, e_got, e_sum, e_got1, e_sum1, e_got2, e_sum2, e_gotz, e_all, e_rows) = refs[
-        n_src + 19 : n_src + 29
+        n_src + 17 : n_src + 27
     ]
-    send, recv, local = refs[n_src + 29 :]
+    send, recv, local = refs[n_src + 27 :]
     seq, mine = lax.axis_index("seq"), lax.axis_index("own")
     z, y, x, c = seq // 2, seq % 2, mine // 2, mine % 2
     core = (seq, 2 * x + (1 - c))
@@ -745,7 +820,8 @@
     e_first = [push(extra.at[:, :, 1 - c], e_got, core)]
     e_load = [load(extra.at[:, :, c], e_own)]
     piece_first, piece_load = [], []
-    for p in range(6):
+
+    def piece_core(p):
         at, part = p // 2, pl.ds((p % 2) * cols, cols)
         if at < 2:
             first = [
@@ -840,7 +916,7 @@
         total = keep_z[p]
         for d in range(depth - 1):
             total = total + got_z[p, d].astype(F32)
-        outs[p // 2][:, pl.ds((p % 2) * cols, cols)] = total
+        grads[(p // 2 + 1) % 3, :, pl.ds((p % 2) * cols, cols)] = total
 
     def extra_c():
         e_load[0].wait()
@@ -900,16 +976,21 @@
         state["gc"] = [push(e_rows.at[:, c], e_rows.at[:, c], core)]
 
     stages = [piece_c, piece_1, piece_2, piece_z]
-    small = [extra_c, extra_1, extra_2, extra_z, extra_gather_y, extra_gather_x, extra_gather_c]
+    small = {0: extra_c, 3: extra_1, 4: extra_2, 5: extra_z, 6: extra_gather_y}
+    small |= {7: extra_gather_x, 8: extra_gather_c}
+    piece_core(0)
+    piece_core(1)
     for turn in range(9):
-        if turn < len(small):
-            small[turn]()
         for stage in range(4):
             if 0 <= turn - stage < 6:
                 stages[stage](turn - stage)
-    outs[3][...] = e_all[:, :, pl.ds(0, extra_keep), :]
+            if stage == 0 and turn + 2 < 6:
+                piece_core(turn + 2)
+        if turn in small:
+            small[turn]()
+    shares_out[...] = e_all[:, :, pl.ds(0, extra_keep), :]
     wait_recv(state["gc"])
-    outs[4][...] = e_rows[...]
+    rows_out[...] = e_rows[...]
     for copy in sent:
         copy.wait_send()
 
@@ -970,9 +1051,9 @@
     return pl.pallas_call(
         functools.partial(reduce_body, depth, half, n_src, keep),
         in_specs=[any_spec] * n_src,
-        out_specs=[vmem] * 5,
-        out_shape=[jax.ShapeDtypeStruct((size, width), F32)] * 3
-        + [
+        out_specs=[vmem] * 3,
+        out_shape=[
+            jax.ShapeDtypeStruct((3, size, width), F32),
             jax.ShapeDtypeStruct((depth, 2, keep, kp), F32),
             jax.ShapeDtypeStruct((2, 2, depth, 2, 8, kp), F32),
         ],
@@ -1102,6 +1183,88 @@
     return (new_left, new_right, weight - rate_matrix * step)
 
 
+def exact(a, b, left, right):
+    return lax.dot_general(
+        a, b, (((left,), (right,)), ((), ())), precision=highest, preferred_element_type=F32
+    )
+
+
+def step_body(bands, *refs):
+    band_ref, tiles, proj_ref, blocks = refs[0], refs[1:6], refs[6], refs[7:12]
+    rows_ref, norm_ref, second_ref = refs[12:15]
+    owned_ref, new_tiles, new_blocks = refs[15], refs[16:19], refs[19:22]
+    grad_ref, second_new_ref, norm_new_ref, rms_ref = refs[22:]
+    at = pl.program_id(0)
+    size, kp = tiles[0].shape[1], proj_ref.shape[-1]
+
+    def update(grad, state, new, t):
+        left, right, root_left, root_right, weight = (ref[t] for ref in state)
+        new[0][t] = decay * left + (1.0 - decay) * exact(grad, grad, 1, 1)
+        new[1][t] = decay * right + (1.0 - decay) * exact(grad, grad, 0, 0)
+        new[2][t] = weight - rate_matrix * exact(root_left, exact(grad, root_right, 1, 0), 1, 0)
+
+    @pl.when(at < bands)
+    def _():
+        for t in range(tiles[0].shape[0]):
+            grad = band_ref[0, :, pl.ds(t * size, size)]
+            owned_ref[t] = grad
+            update(grad, tiles, new_tiles, t)
+
+    @pl.when(at >= bands)
+    def _():
+        update(proj_ref[0], blocks, new_blocks, 0)
+
+    @pl.when(at == bands)
+    def _():
+        depth = rows_ref.shape[2]
+
+        def row(r):
+            return rows_ref[r // 2 % 2, r % 2, r // 8 % depth, r // 4 % 2, pl.ds(0, 1), :]
+
+        per = norm_ref.shape[1] // kp
+        for i in range(4):
+            grad = jnp.concatenate([row(per * i + j) for j in range(per)], axis=1)
+            grad_ref[pl.ds(i, 1), :] = grad
+            second = decay * second_ref[pl.ds(i, 1), :] + (1.0 - decay) * grad * grad
+            second_new_ref[pl.ds(i, 1), :] = second
+            norm_new_ref[pl.ds(i, 1), :] = norm_ref[pl.ds(i, 1), :] - rate_norm * grad * lax.rsqrt(second)
+        count = jnp.sum(row(6 * per), axis=1, keepdims=True)
+        for i in range(2):
+            square = row(4 * per + per * i)
+            for j in range(1, per):
+                square = square + row(4 * per + per * i + j)
+            total = jnp.sum(square, axis=1, keepdims=True)
+            ratio = jnp.sqrt(total / (count * norm_ref.shape[1]))
+            rms_ref[pl.ds(i, 1), :] = jnp.broadcast_to(ratio, (1, rms_ref.shape[1]))
+
+
+def step_all(bands, tiles, proj_grad, blocks, rows, norm_params, norm_stat):
+    count, size, width = bands.shape
+    each, kp = width // size, proj_grad.shape[-1]
+    n_blocks = proj_grad.shape[0]
+    tile = lambda: vspec((each, size, size), lambda i: (jnp.minimum(i, count - 1), 0, 0))
+    block = lambda: vspec((1, kp, kp), lambda i: (jnp.maximum(i - count, 0), 0, 0))
+    whole = lambda a: vspec(a.shape, lambda i: (0,) * len(a.shape))
+    like = lambda a: jax.ShapeDtypeStruct(a.shape, F32)
+    rms = jax.ShapeDtypeStruct((2, 128), F32)
+    return pl.pallas_call(
+        functools.partial(step_body, count),
+        grid=(count + n_blocks,),
+        in_specs=[vspec((1, size, width), lambda i: (jnp.minimum(i, count - 1), 0, 0))]
+        + [tile() for _ in range(5)]
+        + [block() for _ in range(6)]
+        + [whole(rows), whole(norm_params), whole(norm_stat)],
+        out_specs=[tile() for _ in range(4)]
+        + [block() for _ in range(3)]
+        + [whole(norm_params)] * 3
+        + [whole(rms)],
+        out_shape=[like(tiles[0])] * 4 + [like(proj_grad)] * 3 + [like(norm_params)] * 3 + [rms],
+        compiler_params=params(),
+        cost_estimate=cost(1e9, 20e6),
+        name="step_all",
+    )(bands, *tiles, proj_grad, *blocks, rows, norm_params, norm_stat)
+
+
 def to_matrix(tiles, rows, cols):
     size = tiles.shape[-1]
     return (
@@ -1206,9 +1369,6 @@
     per_dev = weights.shape[0]
     att_dev = 4 * (width // size) ** 2 // devices
     x = tokens[0]
-    seq = lax.axis_index("seq")
-    side = seq % 2
-
     swap = [(i, i ^ 1) for i in range(peers)]
     peer_x = lax.ppermute(x, "seq", swap)
     own_size = lax.axis_size("own")
@@ -1217,84 +1377,47 @@
         weights, projection, att_dev, width, both, fused, peers
     )
 
-    lens, offs, counts = lengths[0], offsets[0], valid_count[0]
-    ends = jnp.cumsum(lens)
-    starts = ends - lens
-    unit_rows = 2 * rows_here
-    unit_start = (seq - side) * rows_here
-    unit_end = unit_start + unit_rows
-    block_row = unit_start + SHORT * jnp.arange(2 * blocks, dtype=jnp.int32)
-    hot = ((starts[None, :] <= block_row[:, None]) & (block_row[:, None] < ends[None, :])).astype(
-        jnp.int32
-    )
-    b_start = jnp.sum(hot * starts[None, :], axis=1)
-    b_end = jnp.sum(hot * ends[None, :], axis=1)
-    place = block_row - b_start
-    column = jnp.sum(hot * offs[None, :], axis=1) + place
-    n_valid = jnp.clip(jnp.sum(hot * counts[None, :], axis=1) - place, 0, SHORT)
-    is_head = b_start == b_start[0]
-    is_tail = b_start == b_start[-1]
-    own_at = side * blocks
-    peer_at = (1 - side) * blocks
-    take = lambda v, at: lax.dynamic_slice_in_dim(v, at, blocks, 0)
+    places, table, coef_back = tables(lengths, offsets, valid_count, blocks, rows_here)
 
     def proj_rows(at):
-        col, n = take(column, at), take(n_valid, at)
+        col, n = places[0, at : at + blocks], places[1, at : at + blocks]
         rows = jnp.stack(
             [lax.dynamic_slice_in_dim(proj_all, col[b], SHORT, 0) for b in range(blocks)]
         )
         keep = lax.broadcasted_iota(jnp.int32, (blocks, SHORT, 1), 1) < n[:, None, None]
         return jnp.where(keep, rows, jnp.zeros((), BF))
 
-    e_own = proj_rows(own_at)
-    e_peer = proj_rows(peer_at)
-    n_own = take(n_valid, own_at)
-
-    coef = lambda flag, at: take(flag, at).astype(F32)
-    head_cross = (b_start[0] < unit_start).astype(F32)
-    tail_cross = (b_end[-1] > unit_end).astype(F32)
-    own_head, own_tail = coef(is_head, own_at), coef(is_tail, own_at)
+    e_own = proj_rows(0)
+    e_peer = proj_rows(blocks)
+    n_own = places[1, :blocks]
+
     if fused:
-        pick_tail = (1.0 - own_head) * own_tail
-        unit_coef = lambda flag: jnp.concatenate([coef(flag, own_at), coef(flag, peer_at)])
-        pad = lambda v: jnp.concatenate([v, jnp.zeros((blocks,), F32)])
-        table = jnp.stack(
-            [
-                unit_coef(is_head),
-                unit_coef(is_tail),
-                pad(own_head),
-                pad(own_head * head_cross),
-                pad(pick_tail),
-                pad(pick_tail * tail_cross),
-                pad((1.0 - own_head) * (1.0 - own_tail)),
-            ]
-        )
         query, keyval, summary, mixed, first_sum, row_sums = forward(
-            table, n_own, x, peer_x, w_att, e_own, e_peer, head, peers
+            table, places, x, peer_x, w_att, e_own, e_peer, head, peers
         )
     else:
         query, keyval, part_own = project(x, w_att, e_own.transpose(0, 2, 1), True)
         (part_peer,) = project(peer_x, w_att, e_peer.transpose(0, 2, 1), False)
 
         def unit_sum(flag):
-            mine = coef(flag, own_at)
-            theirs = coef(flag, peer_at)
-            total = mine[0] * part_own[0]
+            total = flag[0] * part_own[0]
             for b in range(1, blocks):
-                total = total + mine[b] * part_own[b]
+                total = total + flag[b] * part_own[b]
             for b in range(blocks):
-                total = total + theirs[b] * part_peer[b]
+                total = total + flag[blocks + b] * part_peer[b]
             return total
 
-        head_sum, tail_sum = unit_sum(is_head), unit_sum(is_tail)
+        head_sum, tail_sum = unit_sum(table[0]), unit_sum(table[1])
         from_left = lax.ppermute(tail_sum, "seq", [(i, i + 2) for i in range(peers - 2)])
         from_right = lax.ppermute(head_sum, "seq", [(i + 2, i) for i in range(peers - 2)])
         summary = jnp.stack(
             [
-                jnp.where(
-                    own_head[b] > 0,
-                    head_sum + head_cross * from_left,
-                    jnp.where(own_tail[b] > 0, tail_sum + tail_cross * from_right, part_own[b]),
+                (
+                    table[2, b] * head_sum
+                    + table[3, b] * from_left
+                    + table[4, b] * tail_sum
+                    + table[5, b] * from_right
+                    + table[6, b] * part_own[b]
                 ).astype(BF)
                 for b in range(blocks)
             ]
@@ -1313,28 +1436,16 @@
     ) = feed(first_sum, w_ffn, w_att, cotangent[0], norm_params, 256)
     grad_query, grad_parts = attend_back(query, summary, grad_mix, head)
 
-    row_start = seq * rows_here
-    row_end = row_start + rows_here
-    o_start, o_end = take(b_start, own_at), take(b_end, own_at)
-    g_head = grad_parts[0]
-    g_tail = grad_parts[-1]
+    g_head = coef_back[0, 0] * grad_parts[0]
+    g_tail = coef_back[-1, 0] * grad_parts[0]
     for b in range(1, blocks):
-        g_head = g_head + (o_start[b] == o_start[0]).astype(F32) * grad_parts[b]
-    for b in range(blocks - 1):
-        g_tail = g_tail + (o_start[b] == o_start[-1]).astype(F32) * grad_parts[b]
+        g_head = g_head + coef_back[0, b] * grad_parts[b]
+        g_tail = g_tail + coef_back[-1, b] * grad_parts[b]
     low_head, low_tail = g_head.astype(BF), g_tail.astype(BF)
-    far_parts, far_flags = [], []
-    at_head = (o_start == o_start[0]).astype(F32)
-    at_tail = (o_start == o_start[-1]).astype(F32)
+    far_parts = []
     for far in (1, 2):
-        reach = (far - 1) * rows_here
         far_parts.append(lax.ppermute(low_tail, "seq", [(i, i + far) for i in range(peers - far)]))
-        far_flags.append(at_head * (o_start[0] < row_start - reach).astype(F32))
         far_parts.append(lax.ppermute(low_head, "seq", [(i + far, i) for i in range(peers - far)]))
-        far_flags.append(at_tail * (o_end[-1] > row_end + reach).astype(F32))
-    together = (o_start[:, None] == o_start[None, :]).astype(F32)
-    coef_back = jnp.concatenate([together, jnp.stack(far_flags, axis=1)], axis=1)
-    own_col = take(column, own_at)
     gtype = BF if fused else F32
     g_up = outer_up(first_low, grad_up, size, gtype)
     g_down = outer_rows(hidden, grad_down, gtype, "outer_down")
@@ -1342,7 +1453,7 @@
     g_query = outer_rows(x, grad_query, gtype, "outer_query")
     grad_keyval, grad_proj, grad_input = back(
         coef_back,
-        jnp.stack([own_col, n_own]),
+        places,
         e_own,
         keyval,
         grad_parts,
@@ -1370,14 +1481,38 @@
         extra = jnp.pad(extra, ((0, 0), (0, 7), (0, 0)))
         shares = grad_proj.reshape(own_size, peers, part_rows // peers, kp).swapaxes(0, 1)
         shares = shares.reshape(devices, part_rows // peers, kp)
-        ffn_a, ffn_b, att, proj_parts, rows = reduce_all(
+        banded_grads, proj_parts, rows = reduce_all(
             g_query, g_keyval, g_out, g_up, g_down, jnp.concatenate([shares, extra], axis=1), peers
         )
-        owned = jnp.concatenate(
-            [from_bands(att, size), from_bands(ffn_a, size), from_bands(ffn_b, size)], axis=0
+        (
+            owned,
+            left_new,
+            right_new,
+            weights_new,
+            proj_left_new,
+            proj_right_new,
+            proj_blocks,
+            norm_grad,
+            stat_new,
+            norm_new,
+            rms,
+        ) = step_all(
+            banded_grads,
+            [stat_left, stat_right, root_left, root_right, weights],
+            proj_parts.reshape(-1, kp, kp),
+            [
+                projection_left,
+                projection_right,
+                projection_root_left,
+                projection_root_right,
+                projection.reshape(-1, kp, kp),
+            ],
+            rows,
+            norm_params,
+            norm_stat,
         )
         proj_grad = proj_parts.reshape(part_rows, kp)
-        totals = rows[..., 0, :].transpose(2, 3, 0, 1, 4).reshape(devices, kp)
+        residual_rms = rms[:, 0]
     else:
         owned = scatter_weight_grads(
             jnp.concatenate([g_query, g_keyval, g_out], axis=0), g_up, g_down, per_dev, att_dev, both
@@ -1388,23 +1523,23 @@
             packed, lax.axis_index("own") * part_rows, part_rows, 0
         )
         totals = packed[grad_proj.shape[0] :]
-    norm_grad = totals[:n_norm].reshape(4, width)
-    row_total = totals[n_norm : n_norm + n_row].reshape(2, width).sum(axis=1)
-    valid_total = totals[n_norm + n_row].sum()
-    residual_rms = jnp.sqrt(row_total / (valid_total * width))
-    left_new, right_new, weights_new = shampoo(
-        owned, stat_left, stat_right, root_left, root_right, weights
-    )
-    proj_left_new, proj_right_new, proj_blocks = shampoo(
-        proj_grad.reshape(-1, kp, kp),
-        projection_left,
-        projection_right,
-        projection_root_left,
-        projection_root_right,
-        projection.reshape(-1, kp, kp),
-    )
-    stat_new = decay * norm_stat + (1.0 - decay) * norm_grad * norm_grad
-    norm_new = norm_params - rate_norm * norm_grad * lax.rsqrt(stat_new)
+        norm_grad = totals[:n_norm].reshape(4, width)
+        row_total = totals[n_norm : n_norm + n_row].reshape(2, width).sum(axis=1)
+        valid_total = totals[n_norm + n_row].sum()
+        residual_rms = jnp.sqrt(row_total / (valid_total * width))
+        left_new, right_new, weights_new = shampoo(
+            owned, stat_left, stat_right, root_left, root_right, weights
+        )
+        proj_left_new, proj_right_new, proj_blocks = shampoo(
+            proj_grad.reshape(-1, kp, kp),
+            projection_left,
+            projection_right,
+            projection_root_left,
+            projection_root_right,
+            projection.reshape(-1, kp, kp),
+        )
+        stat_new = decay * norm_stat + (1.0 - decay) * norm_grad * norm_grad
+        norm_new = norm_params - rate_norm * norm_grad * lax.rsqrt(stat_new)
     return (
         result[None],
         grad_input[None],

time: 423 us -> 406 us (0.960)
  Pallas kernels: 315 us -> 336 us
  matrix products: 18 us -> 0 us
  local copies, waits for them, and re-layouts: 20.4 us -> 10.5 us
  between operations: 30.3 us -> 23.1 us
  other arithmetic: 17 us -> 11.8 us
    pallas_call x0 -> x2, Pallas kernels: none -> 18.9 us  [the longest x1 17.1 us: step_all(): pl.pallas_call(functools.partial(step_body, count), grid=(count + n_block...]
    dot_general x8 -> x0, matrix products: 18 us -> none  [the longest x2 6.28 us: shampoo(): jnp.einsum('tji,tjk->tik', grad, grad, precision=highest)]
    pallas_call x1, Pallas kernels: 101 us -> 87.7 us  [reduce_all(): pl.pallas_call(functools.partial(reduce_body, depth, half, n_src, keep),...]
    pallas_call x1, Pallas kernels: 34.9 us -> 45.5 us  [feed(): pl.pallas_call(functools.partial(feed_body, chunks), grid=(rows // tile,)...]
    pallas_call x1, Pallas kernels: 42.2 us -> 51.3 us  [gather_bands(): pl.pallas_call(functools.partial(gather_body, depth, size // 2), in_specs...]
  transfers between devices with their start and end apart: 6 -> 6, of which waited for: 1 -> 2; matrix products, arithmetic and copies ran while one was open for 5% -> 2% of each run, Pallas kernels for 34% -> 37%
where the time goes in v5:
time: 406 us; the launch traced here: 399 us
  Pallas kernels  336 us (83%)
  between operations  23.1 us (6%)
  starting transfers between devices  12.6 us (3%)
  other arithmetic  11.8 us (3%)
  local copies, waits for them, and re-layouts  10.5 us (3%)
  waiting for transfers between devices  4.43 us (1%)
    pallas_call x1, Pallas kernels, reduce_all(): pl.pallas_call(functools.partial(reduce_body, depth, half, n_src, keep),...  87.7 us
    pallas_call x1, Pallas kernels, forward(): pl.pallas_call(functools.partial(forward_body, peers // 2, head), in_spec...  67.2 us
    pallas_call x1, Pallas kernels, gather_bands(): pl.pallas_call(functools.partial(gather_body, depth, size // 2), in_specs...  51.3 us
    pallas_call x1, Pallas kernels, feed(): pl.pallas_call(functools.partial(feed_body, chunks), grid=(rows // tile,)...  45.5 us
    pallas_call x4, Pallas kernels, outer_rows(): pl.pallas_call(functools.partial(outer_body, False), grid=(tall * wide,),...  23.6 us
    pallas_call x1, Pallas kernels, back(): pl.pallas_call(functools.partial(back_body, width, blocks), grid_spec=plt...  17.4 us
    pallas_call x1, Pallas kernels, step_all(): pl.pallas_call(functools.partial(step_body, count), grid=(count + n_block...  17.1 us
    pallas_call x1, Pallas kernels, attend_back(): pl.pallas_call(functools.partial(attend_back_body, width, head, kp), grid...  15.5 us
  transfers between devices with their start and end apart: 6, of which 2 were waited for; matrix products, arithmetic and copies ran while one was open for 2% of the time, Pallas kernels for 37%

profile of v5, /device:TPU:9, one launch (start us, length us, event | category | flops | bytes accessed | tf_op | source)
XLA Modules:
  0.0 398.7 jit_solution(17480760943633818871)
XLA Ops:
  7.2 1.4 convert_element_type.25
  11.2 1.8 tables.1
  13.1 1.4 fusion.3
  25.3 51.3 %gather_bands.1 = (bf16[4,2,2,2,96,768]{5,4,3,2,1,0:T(8,128)(2,1)}, bf16[2,2,512,256]{3,2,1,0:T(8,128)(2,1)}) custom-call(bf16[96,768]{1,0:T(8,128)(2,1)} %reshape.161.band_ref, bf16[512,256]{1,0:T(8,128)(2,1)} %convert_element_type.26.proj_ref), custom_call_target="tpu_custom_call" | custom-call | flops 1000000000 | bytes 90000000 | tf_op jit(solution)/shard_map/gather_bands/pallas_call | solution.py:1153
  77.2 1.4 dynamic-slice_bitcast_fusion.1
  80.0 67.2 %forward.1 = (bf16[1024,768]{1,0:T(8,128)(2,1)}, bf16[1024,1536]{1,0:T(8,128)(2,1)}, bf16[2,256,1536]{2,1,0:T(8,128)(2,1)}, bf16[1024,768]{1,0:T(8,128)(2,1)}, f32[1024,768]{1,0:T(8,128)}, /*index=5*/f32[2,768]{1,0:T(2,128)}) custom-call(f32[7,4]{1,0:T(8,128)} %get-tuple-element.53.c_ref, s32[2,4]{1,0:T(2,128)} %get-tuple-element.54.n_ref, ...), custom_call_target="tpu_custom_call" | custom-call | flops 9663676416 | bytes 200000000 | tf_op jit(solution)/shard_map/forward/pallas_call | solution.py:439
  148.0 45.5 %feed.1 = (bf16[1024,768]{1,0:T(8,128)(2,1)}, bf16[1024,3072]{1,0:T(8,128)(2,1)}, bf16[1024,3072]{1,0:T(8,128)(2,1)}, bf16[1024,768]{1,0:T(8,128)(2,1)}, bf16[10...) custom-call(f32[1024,768]{1,0:T(8,128)} %get-tuple-element.57.first_, ...), custom_call_target="tpu_custom_call" | custom-call | flops 19327352832 | bytes 30000000 | tf_op jit(solution)/shard_map/feed/pallas_call | solution.py:558
  193.5 15.5 %attend_back.1 = (bf16[1024,768]{1,0:T(8,128)(2,1)}, f32[2,256,1536]{2,1,0:T(8,128)}) custom-call(bf16[1024,768]{1,0:T(8,128)(2,1)} %get-tuple-element.61.q_ref, bf16[2,256,1536]{2,1,0:T(8,128)(2,1)} %get-tuple-element.62.s_ref, bf16[1024,768]{1,0:T(8,128)(2,1)} %get-tuple-element.63.g_ref), custom_call_target="tpu_custom_call" | custom-call | flops 3221225472 | bytes 10000000 | tf_op jit(solution)/shard_map/attend_back/pallas_call | solution.py:629
  209.0 6.0 %fusion.1 = (bf16[256,1536]{1,0:T(8,128)(2,1)}, bf16[256,1536]{1,0:T(8,128)(2,1)}) fusion(f32[2,256,1536]{2,1,0:T(8,128)} %get-tuple-element.64.p_ref, f32[]{:T(128)} %bitcast.24, f32[]{:T(128)} %bitcast.23, f32[]{:T(128)} %bitcast.21, f32[]{:T(128)} %bitcast.20), kind=kLoop, calls=%fused_computation.4 | loop fusion | flops 3145728 | bytes 4718608 | tf_op jit(solution)/shard_map/convert_element_type | solution.py:1444
  215.0 1.9 collective-permute-start.1
  216.9 3.2 collective-permute-start.3
  220.1 4.3 %collective-permute-start.2 = (bf16[256,1536]{1,0:T(8,128)(2,1)}, bf16[256,1536]{1,0:T(8,128)(2,1)S(1)}, u32[]{:S(2)}, u32[]{:S(2)}) collective-permute-start(bf16[256,1536]{1,0:T(8,128)(2,1)} %get-tuple-element.92), channel_id=1, source_target_pairs={{4,0},{8,4},{12,8},{16,12},{20,16},{24,20},{28,24},{5,1},{9,5},{13... | collective-permute-start | bytes 2359304 | tf_op jit(solution)/shard_map/ppermute | solution.py:1448
  224.5 1.9 collective-permute-start.4
  226.5 4.3 %outer_query.1 = bf16[768,768]{1,0:T(8,128)(2,1)} custom-call(bf16[1024,768]{1,0:T(8,128)(2,1)} %bitcast.78, bf16[1024,768]{1,0:T(8,128)(2,1)} %get-tuple-element.65.refs_4_.r_ref), custom_call_target="tpu_custom_call" | custom-call | flops 1207959552 | bytes 20000000 | tf_op jit(solution)/shard_map/outer_query/pallas_call | solution.py:679
  230.9 4.3 %outer_out.1 = bf16[768,768]{1,0:T(8,128)(2,1)} custom-call(bf16[1024,768]{1,0:T(8,128)(2,1)} %get-tuple-element.73.l_ref, bf16[1024,768]{1,0:T(8,128)(2,1)} %get-tuple-element.74.r_ref), custom_call_target="tpu_custom_call" | custom-call | flops 1207959552 | bytes 20000000 | tf_op jit(solution)/shard_map/outer_out/pallas_call | solution.py:679
  235.2 9.2 %outer_down.1 = bf16[3072,768]{1,0:T(8,128)(2,1)} custom-call(bf16[1024,3072]{1,0:T(8,128)(2,1)} %get-tuple-element.70.l_ref, bf16[1024,768]{1,0:T(8,128)(2,1)} %get-tuple-element.71.r_ref), custom_call_target="tpu_custom_call" | custom-call | flops 4831838208 | bytes 20000000 | tf_op jit(solution)/shard_map/outer_down/pallas_call | solution.py:679
  244.4 9.2 %outer_up.1 = bf16[8,4,96,768]{3,2,1,0:T(8,128)(2,1)} custom-call(bf16[1024,768]{1,0:T(8,128)(2,1)} %get-tuple-element.68.l_ref, bf16[1024,3072]{1,0:T(8,128)(2,1)} %get-tuple-element.69.r_ref), custom_call_target="tpu_custom_call" | custom-call | flops 4831838208 | bytes 20000000 | tf_op jit(solution)/shard_map/outer_up/pallas_call | solution.py:660
  254.4 3.5 collective-permute-done.4.refs_3_
  258.0 17.4 %back.1 = (bf16[1024,1536]{1,0:T(8,128)(2,1)}, f32[2048,256]{1,0:T(8,128)}, f32[1024,768]{1,0:T(8,128)}) custom-call(f32[2,6]{1,0:T(2,128)} %get-tuple-element.59.c_ref, s32[2,4]{1,0:T(2,128)} %get-tuple-element.54.n_ref, bf16[2,512,256]{2,1,0:T(8,128)(2,1)} %get-tuple-element.109.e_ref, bf16[1024,1536]{1,0:T(8,128)(2,1)} %get-tuple-element.60.kv_ref, ...), custom_call_target="tpu_custom_call" | custom-call | flops 5234491392 | bytes 20000000 | tf_op jit(solution)/shard_map/back/pallas_call | solution.py:736
  275.3 1.8 copy.36
  277.1 5.8 %outer_keyval.1 = bf16[1536,768]{1,0:T(8,128)(2,1)} custom-call(bf16[1024,768]{1,0:T(8,128)(2,1)} %bitcast.79, bf16[1024,1536]{1,0:T(8,128)(2,1)} %get-tuple-element.72.r_ref), custom_call_target="tpu_custom_call" | custom-call | flops 2415919104 | bytes 20000000 | tf_op jit(solution)/shard_map/outer_keyval/pallas_call | solution.py:679
  282.9 1.6 pad_maximum_fusion.refs_5_
  284.6 87.7 %reduce_all.1 = (f32[3,96,768]{2,1,0:T(8,128)}, f32[4,2,64,256]{3,2,1,0:T(8,128)}, f32[2,2,4,2,8,256]{5,4,3,2,1,0:T(8,128)}) custom-call(bf16[2,4,2,2,96,768]{5,4,3,2,1,0:T(8,128)(2,1)} %bitcast.62, bf16[2,4,2,2,96,768]{5,4,3,2,1,0:T(8,128)(2,1)} %bitcast.61, bf16[4,2,96,768]{3,2,1,0:T(8,128)(2,1)} %bitcast.69, bf16[2,4,2,96,768]{4,3,2,1,0:T(8,128)(2,1)} %bitcast.63, ...), custom_call_target="tpu_custom_call" | custom-call | tf_op jit(solution)/shard_map/reduce_all/pallas_call | solution.py:1051
  372.3 17.1 %step_all.1 = (f32[24,96,96]{2,1,0:T(8,128)}, f32[24,96,96]{2,1,0:T(8,128)}, f32[24,96,96]{2,1,0:T(8,128)}, f32[24,96,96]{2,1,0:T(8,128)}, f32[2,256,256]{2,1,0:...) custom-call(f32[3,96,768]{2,1,0:T(8,128)} %get-tuple-element.78.refs, ...), custom_call_target="tpu_custom_call" | custom-call | flops 1000000000 | bytes 20000000 | tf_op jit(solution)/shard_map/step_all/pallas_call | solution.py:1250
  (47 shorter events, 10.8 us)
Async XLA Ops:
  7.2 140.8 %all-gather.2.cloned.1.call-start = ((), (), s32[]{:S(2)}) async-start(), calls=%async_computation | async-start | bytes 9732096 | tf_op jit(solution)/shard_map/all_gather | solution.py:1296
  8.6 1.4 copy-start.8
  8.6 12.0 %copy-start = (f32[512,256]{1,0:T(8,128)S(1)}, f32[512,256]{1,0:T(8,128)}, u32[]{:S(2)}) copy-start(f32[512,256]{1,0:T(8,128)} %param.27) | copy-start | bytes 1572868
  10.0 70.0 %collective-permute-start = (bf16[1024,768]{1,0:T(8,128)(2,1)S(1)}, bf16[1024,768]{1,0:T(8,128)(2,1)}, u32[]{:S(2)}, u32[]{:S(2)}) collective-permute-start(bf16[1024,768]{1,0:T(8,128)(2,1)S(1)} %bitcast.80), channel_id=1, source_target_pairs={{0,4},{4,0},{8,12},{12,8},{16,20},{20,16},{24,28},{28,24},{1,5},{5... | collective-permute-start | bytes 4718600 | tf_op jit(solution)/shard_map/ppermute | solution.py:1373
  13.1 8.3 %copy-start.5 = (s32[2,4]{1,0:T(2,128)S(1)}, s32[2,4]{1,0:T(2,128)}, u32[]{:S(2)}) copy-start(s32[2,4]{1,0:T(2,128)} %get-tuple-element.54.n_ref) | copy-start | bytes 100
  25.3 51.3 %copy-start.7 = (f32[2,6]{1,0:T(2,128)S(1)}, f32[2,6]{1,0:T(2,128)}, u32[]{:S(2)}) copy-start(f32[2,6]{1,0:T(2,128)} %get-tuple-element.59.c_ref) | copy-start | bytes 148
  209.0 17.4 %copy-start.6 = (f32[4,768]{1,0:T(4,128)S(1)}, f32[4,768]{1,0:T(4,128)}, u32[]{:S(2)}) copy-start(f32[4,768]{1,0:T(4,128)} %get-tuple-element.76) | copy-start | bytes 36868
  215.0 38.5 %collective-permute-start.1 = (bf16[256,1536]{1,0:T(8,128)(2,1)}, bf16[256,1536]{1,0:T(8,128)(2,1)S(1)}, u32[]{:S(2)}, u32[]{:S(2)}) collective-permute-start(bf16[256,1536]{1,0:T(8,128)(2,1)} %get-tuple-element.93), channel_id=1, source_target_pairs={{0,4},{4,8},{8,12},{12,16},{16,20},{20,24},{24,28},{1,5},{5,9},{9,... | collective-permute-start | bytes 2359304 | tf_op jit(solution)/shard_map/ppermute | solution.py:1447
  216.9 37.5 %collective-permute-start.3 = (bf16[256,1536]{1,0:T(8,128)(2,1)}, bf16[256,1536]{1,0:T(8,128)(2,1)S(1)}, u32[]{:S(2)}, u32[]{:S(2)}) collective-permute-start(bf16[256,1536]{1,0:T(8,128)(2,1)} %get-tuple-element.93), channel_id=1, source_target_pairs={{0,8},{4,12},{8,16},{12,20},{16,24},{20,28},{1,9},{5,13},{9,17},{1... | collective-permute-start | bytes 2359304 | tf_op jit(solution)/shard_map/ppermute | solution.py:1447
  220.1 34.3 %collective-permute-start.2 = (bf16[256,1536]{1,0:T(8,128)(2,1)}, bf16[256,1536]{1,0:T(8,128)(2,1)S(1)}, u32[]{:S(2)}, u32[]{:S(2)}) collective-permute-start(bf16[256,1536]{1,0:T(8,128)(2,1)} %get-tuple-element.92), channel_id=1, source_target_pairs={{4,0},{8,4},{12,8},{16,12},{20,16},{24,20},{28,24},{5,1},{9,5},{13... | collective-permute-start | bytes 2359304 | tf_op jit(solution)/shard_map/ppermute | solution.py:1448
  224.5 33.5 %collective-permute-start.4 = (bf16[256,1536]{1,0:T(8,128)(2,1)}, bf16[256,1536]{1,0:T(8,128)(2,1)}, u32[]{:S(2)}, u32[]{:S(2)}) collective-permute-start(bf16[256,1536]{1,0:T(8,128)(2,1)} %get-tuple-element.92), channel_id=1, source_target_pairs={{8,0},{12,4},{16,8},{20,12},{24,16},{28,20},{9,1},{13,5},{17,9},{2... | collective-permute-start | bytes 2359304 | tf_op jit(solution)/shard_map/ppermute | solution.py:1448
  253.5 4.4 %copy-start.2 = (bf16[256,1536]{1,0:T(8,128)(2,1)}, bf16[256,1536]{1,0:T(8,128)(2,1)S(1)}, u32[]{:S(2)}) copy-start(bf16[256,1536]{1,0:T(8,128)(2,1)S(1)} %collective-permute-done.1.refs_0_) | copy-start | bytes 2359300
  254.4 3.6 copy-start.4
  254.4 3.5 copy-start.3
  372.3 18.4 %copy-start.1 = (f32[4,2,64,256]{3,2,1,0:T(8,128)S(1)}, f32[4,2,64,256]{3,2,1,0:T(8,128)}, u32[]{:S(2)}) copy-start(f32[4,2,64,256]{3,2,1,0:T(8,128)} %get-tuple-element.79) | copy-start | bytes 1572868
Sparse Core Ops, SparseCore 0:
  11.5 95.7 all-gather.1

commit v6 on v5

--- a/solution.py
+++ b/solution.py
@@ -396,13 +396,21 @@
 
     def attend_block(b, carry):
         rows = pl.ds(pl.multiple_of(b * short, short), short)
-        for j in range(pairs):
-            cols = pl.ds(j * 2 * head, 2 * head)
+        def pair(j):
+            cols = pl.ds(pl.multiple_of(j * 2 * head, 2 * head), 2 * head)
+            vcols = pl.ds(pl.multiple_of(width + j * 2 * head, 2 * head), 2 * head)
             keys = head_pair(s_ref[b, :, cols], low_lane)
-            values = head_pair(s_ref[b, :, pl.ds(width + j * 2 * head, 2 * head)], low_lane)
+            values = head_pair(s_ref[b, :, vcols], low_lane)
             scores = dot_t(q_ref[rows, cols], keys) * scale
             prob = jnp.concatenate(softmax_pair(scores, kp), axis=1).astype(BF)
             mix_ref[rows, cols] = dot(prob, values).astype(BF)
+
+        def two(i, inner):
+            pair(2 * i)
+            pair(2 * i + 1)
+            return inner
+
+        lax.fori_loop(0, pairs // 2, two, 0)
         branch = dot(mix_ref[rows, :], w_ref[pl.ds(3 * width, width), :])
         first = x_ref[rows, :].astype(F32) + branch
         sum_ref[rows, :] = first
@@ -595,13 +603,15 @@
     )(first_sum, w_ffn, w_ffn, w_att, cotangent, norm_params)
 
 
-def attend_back_body(width, head, kp, q_ref, s_ref, g_ref, dq_ref, ds_ref):
-    pairs = width // (2 * head)
+def attend_back_body(width, head, kp, c_ref, q_ref, s_ref, g_ref, dq_ref, ds_ref, head_ref, tail_ref, acc_ref):
+    step = pl.program_id(0)
+    last = pl.num_programs(0) - 1
     scale = head ** (-0.5)
     low_lane = lax.broadcasted_iota(jnp.int32, (kp, 2 * head), 1) < head
-    for j in range(pairs):
-        cols = pl.ds(j * 2 * head, 2 * head)
-        vcols = pl.ds(width + j * 2 * head, 2 * head)
+
+    def pair(j):
+        cols = pl.ds(pl.multiple_of(j * 2 * head, 2 * head), 2 * head)
+        vcols = pl.ds(pl.multiple_of(width + j * 2 * head, 2 * head), 2 * head)
         keys = head_pair(s_ref[0, :, cols], low_lane)
         values = head_pair(s_ref[0, :, vcols], low_lane)
         q = q_ref[:, cols]
@@ -618,34 +628,57 @@
         dq_ref[:, cols] = (dot(grad_scores, keys) * scale).astype(BF)
         dk = dot_l(grad_scores, q) * scale
         dv = dot_l(prob_low, g)
-        ds_ref[0, :, cols] = jnp.where(low_lane, dk[:kp], dk[kp:])
-        ds_ref[0, :, vcols] = jnp.where(low_lane, dv[:kp], dv[kp:])
-
-
-def attend_back(q, summary, grad_mix, head):
+        for at, both in ((cols, dk), (vcols, dv)):
+            value = jnp.where(low_lane, both[:kp], both[kp:])
+            ds_ref[0, :, at] = value
+            for side, row, low_ref in ((0, 0, head_ref), (1, last, tail_ref)):
+                before = jnp.where(step > 0, acc_ref[side, :, at], 0.0)
+                total = before + c_ref[row, step] * value
+                acc_ref[side, :, at] = total
+                low_ref[:, at] = total.astype(BF)
+
+    def two(i, carry):
+        pair(2 * i)
+        pair(2 * i + 1)
+        return carry
+
+    lax.fori_loop(0, width // (4 * head), two, 0)
+
+
+def attend_back(coef, q, summary, grad_mix, head):
     rows, width = q.shape
     blocks, kp, _ = summary.shape
     short = rows // blocks
+    row = lambda i, *_: (i, 0)
+    lead = lambda i, *_: (i, 0, 0)
     return pl.pallas_call(
         functools.partial(attend_back_body, width, head, kp),
-        grid=(blocks,),
-        in_specs=[
-            vspec((short, width), lambda i: (i, 0)),
-            vspec((1, kp, 2 * width), lambda i: (i, 0, 0)),
-            vspec((short, width), lambda i: (i, 0)),
-        ],
-        out_specs=[
-            vspec((short, width), lambda i: (i, 0)),
-            vspec((1, kp, 2 * width), lambda i: (i, 0, 0)),
-        ],
+        grid_spec=pltpu.PrefetchScalarGridSpec(
+            num_scalar_prefetch=1,
+            grid=(blocks,),
+            in_specs=[
+                vspec((short, width), row),
+                vspec((1, kp, 2 * width), lead),
+                vspec((short, width), row),
+            ],
+            out_specs=[
+                vspec((short, width), row),
+                vspec((1, kp, 2 * width), lead),
+                vspec((kp, 2 * width), lambda i, *_: (0, 0)),
+                vspec((kp, 2 * width), lambda i, *_: (0, 0)),
+            ],
+            scratch_shapes=[pltpu.VMEM((2, kp, 2 * width), F32)],
+        ),
         out_shape=[
             jax.ShapeDtypeStruct((rows, width), BF),
             jax.ShapeDtypeStruct((blocks, kp, 2 * width), F32),
+            jax.ShapeDtypeStruct((kp, 2 * width), BF),
+            jax.ShapeDtypeStruct((kp, 2 * width), BF),
         ],
         compiler_params=params(),
         cost_estimate=cost(2 * rows * width * 8 * kp, 10e6, rows * kp * 12),
         name="attend_back",
-    )(q, summary, grad_mix)
+    )(coef, q, summary, grad_mix)
 
 
 def outer_body(split, l_ref, r_ref, o_ref):
@@ -1205,10 +1238,15 @@
 
     @pl.when(at < bands)
     def _():
-        for t in range(tiles[0].shape[0]):
-            grad = band_ref[0, :, pl.ds(t * size, size)]
-            owned_ref[t] = grad
-            update(grad, tiles, new_tiles, t)
+        def four(i, carry):
+            part = band_ref[0, :, pl.ds(pl.multiple_of(i * 4 * size, 128), 4 * size)]
+            for t in range(4):
+                grad = part[:, t * size : (t + 1) * size]
+                owned_ref[4 * i + t] = grad
+                update(grad, tiles, new_tiles, 4 * i + t)
+            return carry
+
+        lax.fori_loop(0, tiles[0].shape[0] // 4, four, 0)
 
     @pl.when(at >= bands)
     def _():
@@ -1288,19 +1326,48 @@
     )
 
 
+def bands_body(w_ref, p_ref, att_ref, ffn_ref, proj_ref):
+    count, size, _ = w_ref.shape
+    wide = att_ref.shape[1] // size
+    near = att_ref.shape[0] // size
+    for k in range(count):
+        at, cols = k // wide, pl.ds(k % wide * size, size)
+        tile = w_ref[k].astype(BF)
+        if at < near:
+            att_ref[pl.ds(at * size, size), cols] = tile
+        else:
+            ffn_ref[pl.ds((at - near) * size, size), cols] = tile
+    proj_ref[...] = p_ref[...].astype(BF)
+
+
+def make_bands(weights, projection, att_dev, width):
+    per_dev, size, _ = weights.shape
+    near = att_dev * size // width * size
+    return pl.pallas_call(
+        bands_body,
+        out_shape=[
+            jax.ShapeDtypeStruct((near, width), BF),
+            jax.ShapeDtypeStruct((per_dev * size // width * size - near, width), BF),
+            jax.ShapeDtypeStruct(projection.shape, BF),
+        ],
+        compiler_params=pltpu.CompilerParams(vmem_limit_bytes=VMEM_LIMIT),
+        name="make_bands",
+    )(weights, projection)
+
+
 def gather_weights(weights, projection, att_dev, width, both, fused, peers):
     size = weights.shape[-1]
     low = weights.astype(BF)
     groups, chunks = width // size, FF // width
     if banded(weights.shape[0], att_dev, width, size):
-        ffn = lax.all_gather(to_bands(low[att_dev:], width), both, axis=0, tiled=True)
-        band = to_bands(low[:att_dev], width)
+        band, far, proj_low = make_bands(weights, projection, att_dev, width)
+        ffn = lax.all_gather(far, both, axis=0, tiled=True)
         if fused:
-            att, proj = gather_bands(band, projection.astype(BF), peers)
+            att, proj = gather_bands(band, proj_low, peers)
             att, proj = att.reshape(-1, width), proj.reshape(-1, projection.shape[1])
         else:
             att = lax.all_gather(band, both, axis=0, tiled=True)
-            proj = lax.all_gather(projection.astype(BF), "own", axis=0, tiled=True)
+            proj = lax.all_gather(proj_low, "own", axis=0, tiled=True)
         return att, ffn.reshape(2 * groups, chunks, size, width), proj
     per_dev = weights.shape[0]
     proj = lax.all_gather(projection.astype(BF), "own", axis=0, tiled=True)
@@ -1434,14 +1501,10 @@
         grad_mix,
         norm_terms,
     ) = feed(first_sum, w_ffn, w_att, cotangent[0], norm_params, 256)
-    grad_query, grad_parts = attend_back(query, summary, grad_mix, head)
-
-    g_head = coef_back[0, 0] * grad_parts[0]
-    g_tail = coef_back[-1, 0] * grad_parts[0]
-    for b in range(1, blocks):
-        g_head = g_head + coef_back[0, b] * grad_parts[b]
-        g_tail = g_tail + coef_back[-1, b] * grad_parts[b]
-    low_head, low_tail = g_head.astype(BF), g_tail.astype(BF)
+    grad_query, grad_parts, low_head, low_tail = attend_back(
+        coef_back, query, summary, grad_mix, head
+    )
+
     far_parts = []
     for far in (1, 2):
         far_parts.append(lax.ppermute(low_tail, "seq", [(i, i + far) for i in range(peers - far)]))

time: 406 us -> 392 us (0.966)
  other arithmetic: 11.8 us -> 4.51 us
    pallas_call x1, Pallas kernels: 45.5 us -> 34.9 us  [feed(): pl.pallas_call(functools.partial(feed_body, chunks), grid=(rows // tile,)...]
    convert_element_type x3 -> x0, other arithmetic: 8.09 us -> none  [the longest x1 6.01 us: per_device(): low_head, low_tail = (g_head.astype(BF), g_tail.astype(BF))]
  transfers between devices with their start and end apart: 6 -> 6, of which waited for: 2 -> 2; matrix products, arithmetic and copies ran while one was open for 2% -> 2% of each run, Pallas kernels for 37% -> 39%
where the time goes in v6:
time: 392 us; the launch traced here: 387 us
  Pallas kernels  335 us (85%)
  between operations  22.6 us (6%)
  starting transfers between devices  12.7 us (3%)
  local copies, waits for them, and re-layouts  7.69 us (2%)
  other arithmetic  4.51 us (1%)
  waiting for transfers between devices  4.41 us (1%)
    pallas_call x1, Pallas kernels, reduce_all(): pl.pallas_call(functools.partial(reduce_body, depth, half, n_src, keep),...  87.4 us
    pallas_call x1, Pallas kernels, forward(): pl.pallas_call(functools.partial(forward_body, peers // 2, head), in_spec...  70.5 us
    pallas_call x1, Pallas kernels, gather_bands(): pl.pallas_call(functools.partial(gather_body, depth, size // 2), in_specs...  52 us
    pallas_call x1, Pallas kernels, feed(): pl.pallas_call(functools.partial(feed_body, chunks), grid=(rows // tile,)...  34.9 us
    pallas_call x4, Pallas kernels, outer_rows(): pl.pallas_call(functools.partial(outer_body, False), grid=(tall * wide,),...  23.6 us
    pallas_call x1, Pallas kernels, attend_back(): pl.pallas_call(functools.partial(attend_back_body, width, head, kp), grid...  18 us
    pallas_call x1, Pallas kernels, step_all(): pl.pallas_call(functools.partial(step_body, count), grid=(count + n_block...  17.4 us
    pallas_call x1, Pallas kernels, back(): pl.pallas_call(functools.partial(back_body, width, blocks), grid_spec=plt...  17.3 us
  transfers between devices with their start and end apart: 6, of which 2 were waited for; matrix products, arithmetic and copies ran while one was open for 2% of the time, Pallas kernels for 39%

profile of v6, /device:TPU:9, one launch (start us, length us, event | category | flops | bytes accessed | tf_op | source)
XLA Modules:
  0.0 386.7 jit_solution(3486959321800998098)
XLA Ops:
  7.2 2.6 make_bands.1
  11.2 1.8 tables.1
  13.0 1.4 fusion
  19.6 1.5 slice_reduce_fusion.1
  24.4 52.0 %gather_bands.1 = (bf16[4,2,2,2,96,768]{5,4,3,2,1,0:T(8,128)(2,1)}, bf16[2,2,512,256]{3,2,1,0:T(8,128)(2,1)}) custom-call(bf16[96,768]{1,0:T(8,128)(2,1)} %get-tuple-element.60.band_ref, bf16[512,256]{1,0:T(8,128)(2,1)} %get-tuple-element.61.proj_ref), custom_call_target="tpu_custom_call" | custom-call | flops 1000000000 | bytes 90000000 | tf_op jit(solution)/shard_map/gather_bands/pallas_call | solution.py:1186
  76.4 1.5 dynamic-slice_bitcast_fusion.1
  79.3 70.5 %forward.1 = (bf16[1024,768]{1,0:T(8,128)(2,1)}, bf16[1024,1536]{1,0:T(8,128)(2,1)}, bf16[2,256,1536]{2,1,0:T(8,128)(2,1)}, bf16[1024,768]{1,0:T(8,128)(2,1)}, f32[1024,768]{1,0:T(8,128)}, /*index=5*/f32[2,768]{1,0:T(2,128)}) custom-call(f32[7,4]{1,0:T(8,128)} %get-tuple-element.58.c_ref, s32[2,4]{1,0:T(2,128)} %get-tuple-element.59.n_ref, ...), custom_call_target="tpu_custom_call" | custom-call | flops 9663676416 | bytes 200000000 | tf_op jit(solution)/shard_map/forward/pallas_call | solution.py:447
  150.5 34.9 %feed.1 = (bf16[1024,768]{1,0:T(8,128)(2,1)}, bf16[1024,3072]{1,0:T(8,128)(2,1)}, bf16[1024,3072]{1,0:T(8,128)(2,1)}, bf16[1024,768]{1,0:T(8,128)(2,1)}, bf16[10...) custom-call(f32[1024,768]{1,0:T(8,128)} %get-tuple-element.64.first_, ...), custom_call_target="tpu_custom_call" | custom-call | flops 19327352832 | bytes 30000000 | tf_op jit(solution)/shard_map/feed/pallas_call | solution.py:566
  185.4 18.0 %attend_back.1 = (bf16[1024,768]{1,0:T(8,128)(2,1)}, f32[2,256,1536]{2,1,0:T(8,128)}, bf16[256,1536]{1,0:T(8,128)(2,1)}, bf16[256,1536]{1,0:T(8,128)(2,1)}) custom-call(f32[2,6]{1,0:T(2,128)} %get-tuple-element.67.c_ref, bf16[1024,768]{1,0:T(8,128)(2,1)} %get-tuple-element.69.q_ref, bf16[2,256,1536]{2,1,0:T(8,128)(2,1)} %get-tuple-element.70.s_ref, ...), custom_call_target="tpu_custom_call" | custom-call | flops 3221225472 | bytes 10000000 | tf_op jit(solution)/shard_map/attend_back/pallas_call | solution.py:654
  203.4 2.2 collective-permute-start.1
  205.5 3.0 collective-permute-start.3
  208.6 4.3 %collective-permute-start.2 = (bf16[256,1536]{1,0:T(8,128)(2,1)}, bf16[256,1536]{1,0:T(8,128)(2,1)S(1)}, u32[]{:S(2)}, u32[]{:S(2)}) collective-permute-start(bf16[256,1536]{1,0:T(8,128)(2,1)} %get-tuple-element.74), channel_id=1, source_target_pairs={{4,0},{8,4},{12,8},{16,12},{20,16},{24,20},{28,24},{5,1},{9,5},{13... | collective-permute-start | bytes 2359304 | tf_op jit(solution)/shard_map/ppermute | solution.py:1511
  212.8 1.9 collective-permute-start.4
  214.9 4.3 %outer_query.1 = bf16[768,768]{1,0:T(8,128)(2,1)} custom-call(bf16[1024,768]{1,0:T(8,128)(2,1)} %bitcast.58, bf16[1024,768]{1,0:T(8,128)(2,1)} %get-tuple-element.75.refs_4_.r_ref), custom_call_target="tpu_custom_call" | custom-call | flops 1207959552 | bytes 20000000 | tf_op jit(solution)/shard_map/outer_query/pallas_call | solution.py:712
  219.2 4.3 %outer_out.1 = bf16[768,768]{1,0:T(8,128)(2,1)} custom-call(bf16[1024,768]{1,0:T(8,128)(2,1)} %get-tuple-element.83.l_ref, bf16[1024,768]{1,0:T(8,128)(2,1)} %get-tuple-element.84.r_ref), custom_call_target="tpu_custom_call" | custom-call | flops 1207959552 | bytes 20000000 | tf_op jit(solution)/shard_map/outer_out/pallas_call | solution.py:712
  223.6 9.2 %outer_down.1 = bf16[3072,768]{1,0:T(8,128)(2,1)} custom-call(bf16[1024,3072]{1,0:T(8,128)(2,1)} %get-tuple-element.80.l_ref, bf16[1024,768]{1,0:T(8,128)(2,1)} %get-tuple-element.81.r_ref), custom_call_target="tpu_custom_call" | custom-call | flops 4831838208 | bytes 20000000 | tf_op jit(solution)/shard_map/outer_down/pallas_call | solution.py:712
  232.8 9.2 %outer_up.1 = bf16[8,4,96,768]{3,2,1,0:T(8,128)(2,1)} custom-call(bf16[1024,768]{1,0:T(8,128)(2,1)} %get-tuple-element.78.l_ref, bf16[1024,3072]{1,0:T(8,128)(2,1)} %get-tuple-element.79.r_ref), custom_call_target="tpu_custom_call" | custom-call | flops 4831838208 | bytes 20000000 | tf_op jit(solution)/shard_map/outer_up/pallas_call | solution.py:693
  242.8 3.5 collective-permute-done.4.refs_3_
  246.3 17.3 %back.1 = (bf16[1024,1536]{1,0:T(8,128)(2,1)}, f32[2048,256]{1,0:T(8,128)}, f32[1024,768]{1,0:T(8,128)}) custom-call(f32[2,6]{1,0:T(2,128)} %get-tuple-element.67.c_ref, s32[2,4]{1,0:T(2,128)} %get-tuple-element.59.n_ref, bf16[2,512,256]{2,1,0:T(8,128)(2,1)} %get-tuple-element.113.e_ref, bf16[1024,1536]{1,0:T(8,128)(2,1)} %get-tuple-element.68.kv_ref, ...), custom_call_target="tpu_custom_call" | custom-call | flops 5234491392 | bytes 20000000 | tf_op jit(solution)/shard_map/back/pallas_call | solution.py:769
  263.7 1.8 copy.32
  265.5 5.8 %outer_keyval.1 = bf16[1536,768]{1,0:T(8,128)(2,1)} custom-call(bf16[1024,768]{1,0:T(8,128)(2,1)} %bitcast.59, bf16[1024,1536]{1,0:T(8,128)(2,1)} %get-tuple-element.82.r_ref), custom_call_target="tpu_custom_call" | custom-call | flops 2415919104 | bytes 20000000 | tf_op jit(solution)/shard_map/outer_keyval/pallas_call | solution.py:712
  271.3 1.6 pad_maximum_fusion.refs_5_
  272.9 87.4 %reduce_all.1 = (f32[3,96,768]{2,1,0:T(8,128)}, f32[4,2,64,256]{3,2,1,0:T(8,128)}, f32[2,2,4,2,8,256]{5,4,3,2,1,0:T(8,128)}) custom-call(bf16[2,4,2,2,96,768]{5,4,3,2,1,0:T(8,128)(2,1)} %bitcast.43, bf16[2,4,2,2,96,768]{5,4,3,2,1,0:T(8,128)(2,1)} %bitcast.42, bf16[4,2,96,768]{3,2,1,0:T(8,128)(2,1)} %bitcast.49, bf16[2,4,2,96,768]{4,3,2,1,0:T(8,128)(2,1)} %bitcast.44, ...), custom_call_target="tpu_custom_call" | custom-call | tf_op jit(solution)/shard_map/reduce_all/pallas_call | solution.py:1084
  360.3 17.4 %step_all.1 = (f32[24,96,96]{2,1,0:T(8,128)}, f32[24,96,96]{2,1,0:T(8,128)}, f32[24,96,96]{2,1,0:T(8,128)}, f32[24,96,96]{2,1,0:T(8,128)}, f32[2,256,256]{2,1,0:...) custom-call(f32[3,96,768]{2,1,0:T(8,128)} %get-tuple-element.88.refs, ...), custom_call_target="tpu_custom_call" | custom-call | flops 1000000000 | bytes 20000000 | tf_op jit(solution)/shard_map/step_all/pallas_call | solution.py:1288
  (32 shorter events, 6.6 us)
Async XLA Ops:
  7.2 2.7 copy-start.5
  7.2 143.3 %all-gather.2.cloned.1.call-start = ((), (), s32[]{:S(2)}) async-start(), calls=%async_computation | async-start | bytes 9732096 | tf_op jit(solution)/shard_map/all_gather | solution.py:1364
  9.9 69.4 %collective-permute-start = (bf16[1024,768]{1,0:T(8,128)(2,1)S(1)}, bf16[1024,768]{1,0:T(8,128)(2,1)}, u32[]{:S(2)}, u32[]{:S(2)}) collective-permute-start(bf16[1024,768]{1,0:T(8,128)(2,1)S(1)} %bitcast.60), channel_id=1, source_target_pairs={{0,4},{4,0},{8,12},{12,8},{16,20},{20,16},{24,28},{28,24},{1,5},{5... | collective-permute-start | bytes 4718600 | tf_op jit(solution)/shard_map/ppermute | solution.py:1440
  185.4 29.4 %copy-start.4 = (f32[4,768]{1,0:T(4,128)S(1)}, f32[4,768]{1,0:T(4,128)}, u32[]{:S(2)}) copy-start(f32[4,768]{1,0:T(4,128)} %get-tuple-element.86) | copy-start | bytes 36868
  203.4 38.6 %collective-permute-start.1 = (bf16[256,1536]{1,0:T(8,128)(2,1)}, bf16[256,1536]{1,0:T(8,128)(2,1)S(1)}, u32[]{:S(2)}, u32[]{:S(2)}) collective-permute-start(bf16[256,1536]{1,0:T(8,128)(2,1)} %get-tuple-element.73), channel_id=1, source_target_pairs={{0,4},{4,8},{8,12},{12,16},{16,20},{20,24},{24,28},{1,5},{5,9},{9,... | collective-permute-start | bytes 2359304 | tf_op jit(solution)/shard_map/ppermute | solution.py:1510
  205.5 37.3 %collective-permute-start.3 = (bf16[256,1536]{1,0:T(8,128)(2,1)}, bf16[256,1536]{1,0:T(8,128)(2,1)S(1)}, u32[]{:S(2)}, u32[]{:S(2)}) collective-permute-start(bf16[256,1536]{1,0:T(8,128)(2,1)} %get-tuple-element.73), channel_id=1, source_target_pairs={{0,8},{4,12},{8,16},{12,20},{16,24},{20,28},{1,9},{5,13},{9,17},{1... | collective-permute-start | bytes 2359304 | tf_op jit(solution)/shard_map/ppermute | solution.py:1510
  208.6 34.2 %collective-permute-start.2 = (bf16[256,1536]{1,0:T(8,128)(2,1)}, bf16[256,1536]{1,0:T(8,128)(2,1)S(1)}, u32[]{:S(2)}, u32[]{:S(2)}) collective-permute-start(bf16[256,1536]{1,0:T(8,128)(2,1)} %get-tuple-element.74), channel_id=1, source_target_pairs={{4,0},{8,4},{12,8},{16,12},{20,16},{24,20},{28,24},{5,1},{9,5},{13... | collective-permute-start | bytes 2359304 | tf_op jit(solution)/shard_map/ppermute | solution.py:1511
  212.8 33.5 %collective-permute-start.4 = (bf16[256,1536]{1,0:T(8,128)(2,1)}, bf16[256,1536]{1,0:T(8,128)(2,1)}, u32[]{:S(2)}, u32[]{:S(2)}) collective-permute-start(bf16[256,1536]{1,0:T(8,128)(2,1)} %get-tuple-element.74), channel_id=1, source_target_pairs={{8,0},{12,4},{16,8},{20,12},{24,16},{28,20},{9,1},{13,5},{17,9},{2... | collective-permute-start | bytes 2359304 | tf_op jit(solution)/shard_map/ppermute | solution.py:1511
  241.9 4.4 %copy-start.1 = (bf16[256,1536]{1,0:T(8,128)(2,1)}, bf16[256,1536]{1,0:T(8,128)(2,1)S(1)}, u32[]{:S(2)}) copy-start(bf16[256,1536]{1,0:T(8,128)(2,1)S(1)} %collective-permute-done.1.refs_0_) | copy-start | bytes 2359300
  242.8 3.5 copy-start.3
  242.8 3.5 copy-start.2
  360.3 18.7 %copy-start = (f32[4,2,64,256]{3,2,1,0:T(8,128)S(1)}, f32[4,2,64,256]{3,2,1,0:T(8,128)}, u32[]{:S(2)}) copy-start(f32[4,2,64,256]{3,2,1,0:T(8,128)} %get-tuple-element.89) | copy-start | bytes 1572868
Sparse Core Ops, SparseCore 0:
  11.5 98.3 all-gather.1

commit v7 on v6

--- a/solution.py
+++ b/solution.py
@@ -415,10 +415,12 @@
         first = x_ref[rows, :].astype(F32) + branch
         sum_ref[rows, :] = first
         keep = (lax.broadcasted_iota(jnp.int32, (short, 1), 0) < n_ref[1, b]).astype(F32)
+        here = lax.broadcasted_iota(jnp.int32, (1, width), 1) == 0
         stat_ref[...] += jnp.concatenate(
             [
                 jnp.sum(keep * first * first, axis=0, keepdims=True),
                 jnp.sum(keep * branch * branch, axis=0, keepdims=True),
+                jnp.where(here, n_ref[1, b].astype(F32), 0.0),
             ],
             axis=0,
         )
@@ -454,7 +456,7 @@
             jax.ShapeDtypeStruct((blocks, kp, 2 * width), BF),
             jax.ShapeDtypeStruct((rows, width), BF),
             jax.ShapeDtypeStruct((rows, width), F32),
-            jax.ShapeDtypeStruct((2, width), F32),
+            jax.ShapeDtypeStruct((3, width), F32),
         ],
         scratch_shapes=[
             pltpu.VMEM((blocks, kp, 2 * width), F32),
@@ -603,31 +605,35 @@
     )(first_sum, w_ffn, w_ffn, w_att, cotangent, norm_params)
 
 
+def pair_back(key_cols, value_cols, q, g, head, low_lane):
+    kp = key_cols.shape[0]
+    scale = head ** (-0.5)
+    keys, values = head_pair(key_cols, low_lane), head_pair(value_cols, low_lane)
+    prob = softmax_pair(dot_t(q, keys) * scale, kp)
+    grad_prob = dot_t(g, values)
+    low_parts = []
+    for half in range(2):
+        p = prob[half]
+        d = grad_prob[:, half * kp : (half + 1) * kp]
+        low_parts.append((p * (d - jnp.sum(p * d, axis=-1, keepdims=True))).astype(BF))
+    grad_scores = jnp.concatenate(low_parts, axis=1)
+    prob_low = jnp.concatenate(prob, axis=1).astype(BF)
+    grad_q = (dot(grad_scores, keys) * scale).astype(BF)
+    return grad_q, dot_l(grad_scores, q) * scale, dot_l(prob_low, g)
+
+
 def attend_back_body(width, head, kp, c_ref, q_ref, s_ref, g_ref, dq_ref, ds_ref, head_ref, tail_ref, acc_ref):
     step = pl.program_id(0)
     last = pl.num_programs(0) - 1
-    scale = head ** (-0.5)
     low_lane = lax.broadcasted_iota(jnp.int32, (kp, 2 * head), 1) < head
 
     def pair(j):
         cols = pl.ds(pl.multiple_of(j * 2 * head, 2 * head), 2 * head)
         vcols = pl.ds(pl.multiple_of(width + j * 2 * head, 2 * head), 2 * head)
-        keys = head_pair(s_ref[0, :, cols], low_lane)
-        values = head_pair(s_ref[0, :, vcols], low_lane)
-        q = q_ref[:, cols]
-        g = g_ref[:, cols]
-        prob = softmax_pair(dot_t(q, keys) * scale, kp)
-        grad_prob = dot_t(g, values)
-        low_parts = []
-        for half in range(2):
-            p = prob[half]
-            d = grad_prob[:, half * kp : (half + 1) * kp]
-            low_parts.append((p * (d - jnp.sum(p * d, axis=-1, keepdims=True))).astype(BF))
-        grad_scores = jnp.concatenate(low_parts, axis=1)
-        prob_low = jnp.concatenate(prob, axis=1).astype(BF)
-        dq_ref[:, cols] = (dot(grad_scores, keys) * scale).astype(BF)
-        dk = dot_l(grad_scores, q) * scale
-        dv = dot_l(prob_low, g)
+        grads, dk, dv = pair_back(
+            s_ref[0, :, cols], s_ref[0, :, vcols], q_ref[:, cols], g_ref[:, cols], head, low_lane
+        )
+        dq_ref[:, cols] = grads
         for at, both in ((cols, dk), (vcols, dv)):
             value = jnp.where(low_lane, both[:kp], both[kp:])
             ds_ref[0, :, at] = value
@@ -722,6 +728,171 @@
         cost_estimate=cost(2 * rows * width * width * tall * wide, 20e6),
         name=name,
     )(left, right)
+
+
+def backward_body(peers, head, chunks, c_ref, q_ref, s_ref, g_ref, *refs):
+    sources, outs = refs[:7], refs[7:13]
+    grad_outs, scratch = refs[13:17], refs[17:]
+    dq_ref, ds_ref, far_refs = outs[0], outs[1], outs[2:]
+    held, (low_head, low_tail, g_down, g_up, g_out, g_query) = scratch[:7], scratch[7:13]
+    send, recv, local = scratch[13:]
+    blocks, kp, wide = s_ref.shape
+    width = wide // 2
+    short = q_ref.shape[0] // blocks
+    pairs = width // (2 * head)
+    seq, mine = lax.axis_index("seq"), lax.axis_index("own")
+    loads = [pltpu.make_async_copy(sources[k], held[k], local.at[k]) for k in range(7)]
+    for load in loads:
+        load.start()
+
+    def place(d):
+        return (lax.rem(seq + peers + d, peers), mine)
+
+    steps = (1, -1, 2, -2)
+    inside = lambda d: seq < peers - d if d > 0 else seq >= -d
+    can_send = [inside(d) for d in steps]
+    can_get = [inside(-d) for d in steps]
+    barrier = pltpu.get_barrier_semaphore()
+    for k in range(4):
+
+        @pl.when(can_send[k])
+        def _():
+            pl.semaphore_signal(barrier, inc=1, device_id=place(steps[k]), device_id_type=MESH_ID)
+
+        @pl.when(jnp.logical_not(can_get[k]))
+        def _():
+            far_refs[k][...] = jnp.zeros_like(far_refs[k])
+
+    pl.semaphore_wait(barrier, jnp.minimum(seq, 2) + jnp.minimum(peers - 1 - seq, 2))
+    low_lane = lax.broadcasted_iota(jnp.int32, (kp, 2 * head), 1) < head
+
+    def columns(j):
+        at = pl.multiple_of(j * 2 * head, 2 * head)
+        return pl.ds(at, 2 * head), pl.ds(pl.multiple_of(width + at, 2 * head), 2 * head)
+
+    def message(j, k, kind):
+        low = (low_tail, low_head)[k % 2]
+        cols = columns(j)[kind]
+        return pltpu.make_async_remote_copy(
+            src_ref=low.at[:, cols],
+            dst_ref=far_refs[k].at[:, cols],
+            send_sem=send.at[j, k, kind],
+            recv_sem=recv.at[j, k, kind],
+            device_id=place(steps[k]),
+            device_id_type=MESH_ID,
+        )
+
+    def pair(j, carry):
+        cols, vcols = columns(j)
+        head_sums, tail_sums = [0.0, 0.0], [0.0, 0.0]
+        for b in range(blocks):
+            rows = pl.ds(b * short, short)
+            grads, dk, dv = pair_back(
+                s_ref[b, :, cols], s_ref[b, :, vcols], q_ref[rows, cols], g_ref[rows, cols], head, low_lane
+            )
+            dq_ref[rows, cols] = grads
+            for kind, at, both in ((0, cols, dk), (1, vcols, dv)):
+                value = jnp.where(low_lane, both[:kp], both[kp:])
+                ds_ref[b, :, at] = value
+                head_sums[kind] = head_sums[kind] + c_ref[0, b] * value
+                tail_sums[kind] = tail_sums[kind] + c_ref[blocks - 1, b] * value
+        for kind, at in ((0, cols), (1, vcols)):
+            low_head[:, at] = head_sums[kind].astype(BF)
+            low_tail[:, at] = tail_sums[kind].astype(BF)
+        for k in range(4):
+
+            @pl.when(can_send[k])
+            def _():
+                for kind in range(2):
+                    message(j, k, kind).start()
+
+        return carry
+
+    lax.fori_loop(0, pairs, pair, 0)
+    first_low, grad_up, hidden, grad_down, mixed, grad_branch, x = held
+    stores = []
+
+    def store(src, dst):
+        copy = pltpu.make_async_copy(src, dst, local.at[7 + len(stores)])
+        copy.start()
+        stores.append(copy)
+
+    for load in loads:
+        load.wait()
+
+    def down_chunk(i, carry):
+        at = pl.ds(pl.multiple_of(i * width, width), width)
+        g_down[at, :] = dot_l(hidden[:, at], grad_down[...]).astype(BF)
+        return carry
+
+    def up_chunk(i, carry):
+        at = pl.ds(pl.multiple_of(i * width, width), width)
+        value = dot_l(first_low[...], grad_up[:, at]).astype(BF)
+        g_up[:, i] = value.reshape(g_up.shape[0], g_up.shape[2], width)
+        return carry
+
+    lax.fori_loop(0, chunks, down_chunk, 0)
+    store(g_down, grad_outs[0])
+    lax.fori_loop(0, chunks, up_chunk, 0)
+    store(g_up, grad_outs[1])
+    g_out[...] = dot_l(mixed[...], grad_branch[...]).astype(BF)
+    store(g_out, grad_outs[2])
+    g_query[...] = dot_l(x[...], dq_ref[...]).astype(BF)
+    store(g_query, grad_outs[3])
+
+    def finish(j, carry):
+        for k in range(4):
+
+            @pl.when(can_get[k])
+            def _():
+                for kind in range(2):
+                    message(j, k, kind).wait_recv()
+
+            @pl.when(can_send[k])
+            def _():
+                for kind in range(2):
+                    message(j, k, kind).wait_send()
+
+        return carry
+
+    lax.fori_loop(0, pairs, finish, 0)
+    for copy in stores:
+        copy.wait()
+
+
+def backward(coef, q, summary, grad_mix, operands, head, peers, size):
+    rows, width = q.shape
+    blocks, kp, _ = summary.shape
+    chunks = operands[1].shape[1] // width
+    groups = width // size
+    vmem, smem = pl.BlockSpec(memory_space=pltpu.VMEM), pl.BlockSpec(memory_space=pltpu.SMEM)
+    far = jax.ShapeDtypeStruct((kp, 2 * width), BF)
+    products = [(chunks * width, width), (groups, chunks, size, width), (width, width), (width, width)]
+    pairs = width // (2 * head)
+    return pl.pallas_call(
+        functools.partial(backward_body, peers, head, chunks),
+        in_specs=[smem] + [vmem] * 3 + [pl.BlockSpec(memory_space=pl.ANY)] * 7,
+        out_specs=[vmem] * 6 + [pl.BlockSpec(memory_space=pl.ANY)] * 4,
+        out_shape=[
+            jax.ShapeDtypeStruct((rows, width), BF),
+            jax.ShapeDtypeStruct((blocks, kp, 2 * width), F32),
+        ]
+        + [far] * 4
+        + [jax.ShapeDtypeStruct(shape, BF) for shape in products],
+        scratch_shapes=[pltpu.VMEM(a.shape, BF) for a in operands]
+        + [pltpu.VMEM(far.shape, BF)] * 2
+        + [pltpu.VMEM(shape, BF) for shape in products]
+        + [
+            pltpu.SemaphoreType.DMA((pairs, 4, 2)),
+            pltpu.SemaphoreType.DMA((pairs, 4, 2)),
+            pltpu.SemaphoreType.DMA((11,)),
+        ],
+        compiler_params=pltpu.CompilerParams(
+            collective_id=4, has_side_effects=True, vmem_limit_bytes=VMEM_LIMIT
+        ),
+        cost_estimate=cost(2 * rows * width * (8 * kp + 10 * width), 60e6, rows * kp * 12),
+        name="backward",
+    )(coef, q, summary, grad_mix, *operands)
 
 
 def back_body(
@@ -1266,7 +1437,7 @@
             second = decay * second_ref[pl.ds(i, 1), :] + (1.0 - decay) * grad * grad
             second_new_ref[pl.ds(i, 1), :] = second
             norm_new_ref[pl.ds(i, 1), :] = norm_ref[pl.ds(i, 1), :] - rate_norm * grad * lax.rsqrt(second)
-        count = jnp.sum(row(6 * per), axis=1, keepdims=True)
+        count = jnp.sum(sum(row(6 * per + j) for j in range(per)), axis=1, keepdims=True)
         for i in range(2):
             square = row(4 * per + per * i)
             for j in range(1, per):
@@ -1501,19 +1672,25 @@
         grad_mix,
         norm_terms,
     ) = feed(first_sum, w_ffn, w_att, cotangent[0], norm_params, 256)
-    grad_query, grad_parts, low_head, low_tail = attend_back(
-        coef_back, query, summary, grad_mix, head
-    )
-
-    far_parts = []
-    for far in (1, 2):
-        far_parts.append(lax.ppermute(low_tail, "seq", [(i, i + far) for i in range(peers - far)]))
-        far_parts.append(lax.ppermute(low_head, "seq", [(i + far, i) for i in range(peers - far)]))
     gtype = BF if fused else F32
-    g_up = outer_up(first_low, grad_up, size, gtype)
-    g_down = outer_rows(hidden, grad_down, gtype, "outer_down")
-    g_out = outer_rows(mixed, grad_branch, gtype, "outer_out")
-    g_query = outer_rows(x, grad_query, gtype, "outer_query")
+    if fused:
+        operands = [first_low, grad_up, hidden, grad_down, mixed, grad_branch, x]
+        grad_query, grad_parts, *far_parts, g_down, g_up, g_out, g_query = backward(
+            coef_back, query, summary, grad_mix, operands, head, peers, size
+        )
+    else:
+        grad_query, grad_parts, low_head, low_tail = attend_back(
+            coef_back, query, summary, grad_mix, head
+        )
+        far_parts = []
+        for far in (1, 2):
+            onward = [(i, i + far) for i in range(peers - far)]
+            far_parts.append(lax.ppermute(low_tail, "seq", onward))
+            far_parts.append(lax.ppermute(low_head, "seq", [(j, i) for i, j in onward]))
+        g_up = outer_up(first_low, grad_up, size, gtype)
+        g_down = outer_rows(hidden, grad_down, gtype, "outer_down")
+        g_out = outer_rows(mixed, grad_branch, gtype, "outer_out")
+        g_query = outer_rows(x, grad_query, gtype, "outer_query")
     grad_keyval, grad_proj, grad_input = back(
         coef_back,
         places,
@@ -1528,15 +1705,11 @@
     )
     g_keyval = outer_rows(x, grad_keyval, gtype, "outer_keyval")
     part_rows = projection.shape[0]
-    valid_here = jnp.sum(n_own).astype(F32)
-    extra = jnp.concatenate(
-        [
-            norm_terms.reshape(-1, kp),
-            row_sums.reshape(-1, kp),
-            jnp.full((1, kp), 1.0 / kp, F32) * valid_here,
-        ],
-        axis=0,
-    )
+    if not fused:
+        valid_here = jnp.sum(n_own).astype(F32)
+        here = lax.broadcasted_iota(jnp.int32, (1, width), 1) == 0
+        row_sums = jnp.concatenate([row_sums, jnp.where(here, valid_here, 0.0)], axis=0)
+    extra = jnp.concatenate([norm_terms.reshape(-1, kp), row_sums.reshape(-1, kp)], axis=0)
     n_norm = 4 * width // kp
     n_row = 2 * width // kp
     if fused:
@@ -1588,7 +1761,7 @@
         totals = packed[grad_proj.shape[0] :]
         norm_grad = totals[:n_norm].reshape(4, width)
         row_total = totals[n_norm : n_norm + n_row].reshape(2, width).sum(axis=1)
-        valid_total = totals[n_norm + n_row].sum()
+        valid_total = totals[n_norm + n_row : n_norm + n_row + width // kp].sum()
         residual_rms = jnp.sqrt(row_total / (valid_total * width))
         left_new, right_new, weights_new = shampoo(
             owned, stat_left, stat_right, root_left, root_right, weights

time: 392 us -> 379 us (0.967)
  starting transfers between devices: 12.7 us -> 1.34 us
  Pallas kernels: 335 us -> 340 us
  waiting for transfers between devices: 4.41 us -> 0.02 us
    pallas_call x2 -> x1, Pallas kernels: 27.1 us -> 45.6 us  [backward(): pl.pallas_call(functools.partial(backward_body, peers, head, chunks), in_...]
    pallas_call x4 -> x1, Pallas kernels: 23.6 us -> 5.8 us  [outer_rows(): pl.pallas_call(functools.partial(outer_body, False), grid=(tall * wide,),...]
    ppermute x4 -> x0, starting transfers between devices: 11.3 us -> none  [the longest x2 6.18 us: per_device(): lax.ppermute(low_head, 'seq', [(i + far, i) for i in range(peers - far)])]
    ppermute x4 -> x0, waiting for transfers between devices: 4.39 us -> none  [the longest x2 4.39 us: per_device(): lax.ppermute(low_head, 'seq', [(i + far, i) for i in range(peers - far)])]
  transfers between devices with their start and end apart: 6 -> 2, of which waited for: 2 -> 0; matrix products, arithmetic and copies ran while one was open for 2% -> 1% of each run, Pallas kernels for 39% -> 34%
where the time goes in v7:
time: 379 us; the launch traced here: 375 us
  Pallas kernels  340 us (90%)
  between operations  22 us (6%)
  local copies, waits for them, and re-layouts  8.77 us (2%)
    pallas_call x1, Pallas kernels, reduce_all(): pl.pallas_call(functools.partial(reduce_body, depth, half, n_src, keep),...  90 us
    pallas_call x1, Pallas kernels, forward(): pl.pallas_call(functools.partial(forward_body, peers // 2, head), in_spec...  70.4 us
    pallas_call x1, Pallas kernels, gather_bands(): pl.pallas_call(functools.partial(gather_body, depth, size // 2), in_specs...  54.2 us
    pallas_call x1, Pallas kernels, backward(): pl.pallas_call(functools.partial(backward_body, peers, head, chunks), in_...  45.6 us
    pallas_call x1, Pallas kernels, feed(): pl.pallas_call(functools.partial(feed_body, chunks), grid=(rows // tile,)...  34.9 us
    pallas_call x1, Pallas kernels, back(): pl.pallas_call(functools.partial(back_body, width, blocks), grid_spec=plt...  17.4 us
    pallas_call x1, Pallas kernels, step_all(): pl.pallas_call(functools.partial(step_body, count), grid=(count + n_block...  17.4 us
  transfers between devices with their start and end apart: 2, of which 0 were waited for; matrix products, arithmetic and copies ran while one was open for 1% of the time, Pallas kernels for 34%

profile of v7, /device:TPU:9, one launch (start us, length us, event | category | flops | bytes accessed | tf_op | source)
XLA Modules:
  0.0 375.2 jit_solution(6008899283096623291)
XLA Ops:
  7.2 0.0 all-gather.2.cloned.1.call-start
  7.2 2.6 make_bands.1
  9.9 1.3 collective-permute-start
  11.2 1.8 tables.1
  13.0 1.4 fusion
  22.2 54.2 %gather_bands.1 = (bf16[4,2,2,2,96,768]{5,4,3,2,1,0:T(8,128)(2,1)}, bf16[2,2,512,256]{3,2,1,0:T(8,128)(2,1)}) custom-call(bf16[96,768]{1,0:T(8,128)(2,1)} %get-tuple-element.66.band_ref, bf16[512,256]{1,0:T(8,128)(2,1)} %get-tuple-element.67.proj_ref), custom_call_target="tpu_custom_call" | custom-call | flops 1000000000 | bytes 90000000 | tf_op jit(solution)/shard_map/gather_bands/pallas_call | solution.py:1357
  76.4 1.5 dynamic-slice_bitcast_fusion.1
  77.9 0.1 slice_bitcast_fusion
  78.0 0.1 iota_compare_fusion.1
  78.1 0.1 iota_compare_fusion.2
  78.1 1.2 maximum_select_fusion
  79.4 1.1 copy-done.4
  80.5 70.4 %forward.1 = (bf16[1024,768]{1,0:T(8,128)(2,1)}, bf16[1024,1536]{1,0:T(8,128)(2,1)}, bf16[2,256,1536]{2,1,0:T(8,128)(2,1)}, bf16[1024,768]{1,0:T(8,128)(2,1)}, f32[1024,768]{1,0:T(8,128)}, /*index=5*/f32[3,768]{1,0:T(4,128)}) custom-call(f32[7,4]{1,0:T(8,128)} %get-tuple-element.64.c_ref, s32[2,4]{1,0:T(2,128)} %get-tuple-element.65.n_ref, ...), custom_call_target="tpu_custom_call" | custom-call | flops 9663676416 | bytes 200000000 | tf_op jit(solution)/shard_map/forward/pallas_call | solution.py:449
  150.9 0.7 reshape.146
  151.6 34.9 %feed.1 = (bf16[1024,768]{1,0:T(8,128)(2,1)}, bf16[1024,3072]{1,0:T(8,128)(2,1)}, bf16[1024,3072]{1,0:T(8,128)(2,1)}, bf16[1024,768]{1,0:T(8,128)(2,1)}, bf16[10...) custom-call(f32[1024,768]{1,0:T(8,128)} %get-tuple-element.70.first_, ...), custom_call_target="tpu_custom_call" | custom-call | flops 19327352832 | bytes 30000000 | tf_op jit(solution)/shard_map/feed/pallas_call | solution.py:568
  186.5 45.6 %backward.1 = (bf16[1024,768]{1,0:T(8,128)(2,1)}, f32[2,256,1536]{2,1,0:T(8,128)}, bf16[256,1536]{1,0:T(8,128)(2,1)}, bf16[256,1536]{1,0:T(8,128)(2,1)}, bf16[25...) custom-call(f32[2,6]{1,0:T(2,128)} %get-tuple-element.73.c_ref, ...), custom_call_target="tpu_custom_call" | custom-call | flops 15300820992 | bytes 60000000 | tf_op jit(solution)/shard_map/backward/pallas_call | solution.py:872
  232.2 17.4 %back.1 = (bf16[1024,1536]{1,0:T(8,128)(2,1)}, f32[2048,256]{1,0:T(8,128)}, f32[1024,768]{1,0:T(8,128)}) custom-call(f32[2,6]{1,0:T(2,128)} %get-tuple-element.73.c_ref, s32[2,4]{1,0:T(2,128)} %get-tuple-element.65.n_ref, bf16[2,512,256]{2,1,0:T(8,128)(2,1)} %get-tuple-element.124.e_ref, bf16[1024,1536]{1,0:T(8,128)(2,1)} %get-tuple-element.74.kv_ref, ...), custom_call_target="tpu_custom_call" | custom-call | flops 5234491392 | bytes 20000000 | tf_op jit(solution)/shard_map/back/pallas_call | solution.py:940
  249.6 1.8 copy.32
  251.4 5.8 %outer_keyval.1 = bf16[1536,768]{1,0:T(8,128)(2,1)} custom-call(bf16[1024,768]{1,0:T(8,128)(2,1)} %bitcast.58, bf16[1024,1536]{1,0:T(8,128)(2,1)} %get-tuple-element.95.r_ref), custom_call_target="tpu_custom_call" | custom-call | flops 2415919104 | bytes 20000000 | tf_op jit(solution)/shard_map/outer_keyval/pallas_call | solution.py:718
  257.2 1.6 pad_maximum_fusion.refs_5_
  258.9 90.0 %reduce_all.1 = (f32[3,96,768]{2,1,0:T(8,128)}, f32[4,2,64,256]{3,2,1,0:T(8,128)}, f32[2,2,4,2,8,256]{5,4,3,2,1,0:T(8,128)}) custom-call(bf16[2,4,2,2,96,768]{5,4,3,2,1,0:T(8,128)(2,1)} %bitcast.42, bf16[2,4,2,2,96,768]{5,4,3,2,1,0:T(8,128)(2,1)} %bitcast.41, bf16[4,2,96,768]{3,2,1,0:T(8,128)(2,1)} %bitcast.49, bf16[2,4,2,96,768]{4,3,2,1,0:T(8,128)(2,1)} %bitcast.43, ...), custom_call_target="tpu_custom_call" | custom-call | tf_op jit(solution)/shard_map/reduce_all/pallas_call | solution.py:1255
  348.9 17.4 %step_all.1 = (f32[24,96,96]{2,1,0:T(8,128)}, f32[24,96,96]{2,1,0:T(8,128)}, f32[24,96,96]{2,1,0:T(8,128)}, f32[24,96,96]{2,1,0:T(8,128)}, f32[2,256,256]{2,1,0:...) custom-call(f32[3,96,768]{2,1,0:T(8,128)} %get-tuple-element.100.ref, ...), custom_call_target="tpu_custom_call" | custom-call | flops 1000000000 | bytes 20000000 | tf_op jit(solution)/shard_map/step_all/pallas_call | solution.py:1459
  366.3 1.3 slice_reduce_fusion
  367.6 0.8 copy.34
  (16 shorter events, 0.1 us)
Async XLA Ops:
  7.2 2.7 copy-start.3
  7.2 144.4 %all-gather.2.cloned.1.call-start = ((), (), s32[]{:S(2)}) async-start(), calls=%async_computation | async-start | bytes 9732096 | tf_op jit(solution)/shard_map/all_gather | solution.py:1535
  9.9 69.5 %collective-permute-start = (bf16[1024,768]{1,0:T(8,128)(2,1)S(1)}, bf16[1024,768]{1,0:T(8,128)(2,1)S(1)}, u32[]{:S(2)}, u32[]{:S(2)}) collective-permute-start(bf16[1024,768]{1,0:T(8,128)(2,1)S(1)} %bitcast.59), channel_id=1, source_target_pairs={{0,4},{4,0},{8,12},{12,8},{16,20},{20,16},{24,28},{28,24},{1,5},{5... | collective-permute-start | bytes 4718600 | tf_op jit(solution)/shard_map/ppermute | solution.py:1611
  76.4 1.5 copy-start.1
  79.4 1.1 copy-start.4
  249.6 1.8 copy-start.2
  348.9 18.7 %copy-start = (f32[4,2,64,256]{3,2,1,0:T(8,128)S(1)}, f32[4,2,64,256]{3,2,1,0:T(8,128)}, u32[]{:S(2)}) copy-start(f32[4,2,64,256]{3,2,1,0:T(8,128)} %get-tuple-element.101) | copy-start | bytes 1572868
Sparse Core Ops, SparseCore 0:
  11.5 100.3 all-gather.1

commit v8 on v7

--- a/solution.py
+++ b/solution.py
@@ -124,6 +124,36 @@
         ],
         name="tables",
     )(lengths, offsets, valid_count)
+
+
+def pick_body(places_ref, proj_ref, own_ref, peer_ref):
+    blocks, short, kp = own_ref.shape
+    span = short + 16
+    keep = lax.broadcasted_iota(jnp.int32, (short, 1), 0)
+    for first, out in ((0, own_ref), (blocks, peer_ref)):
+
+        def block(b, carry):
+            column = places_ref[0, first + b]
+            at = jnp.clip((column // 16) * 16, 0, proj_ref.shape[0] - span)
+            rows = proj_ref[pl.ds(pl.multiple_of(at, 16), span), :].astype(F32)
+            rows = pltpu.roll(rows, lax.rem(span + at - column, span), 0)[:short]
+            out[b] = jnp.where(keep < places_ref[1, first + b], rows, 0.0).astype(BF)
+            return carry
+
+        lax.fori_loop(0, blocks, block, 0)
+
+
+def pick_rows(places, proj_all, blocks):
+    vmem, smem = pl.BlockSpec(memory_space=pltpu.VMEM), pl.BlockSpec(memory_space=pltpu.SMEM)
+    shape = jax.ShapeDtypeStruct((blocks, SHORT, proj_all.shape[1]), BF)
+    return pl.pallas_call(
+        pick_body,
+        in_specs=[smem, vmem],
+        out_specs=[vmem] * 2,
+        out_shape=[shape] * 2,
+        compiler_params=pltpu.CompilerParams(vmem_limit_bytes=VMEM_LIMIT),
+        name="pick_rows",
+    )(places, proj_all)
 
 
 def project_body(width, with_query, x_ref, w_ref, e_ref, *outs):
@@ -1444,7 +1474,7 @@
                 square = square + row(4 * per + per * i + j)
             total = jnp.sum(square, axis=1, keepdims=True)
             ratio = jnp.sqrt(total / (count * norm_ref.shape[1]))
-            rms_ref[pl.ds(i, 1), :] = jnp.broadcast_to(ratio, (1, rms_ref.shape[1]))
+            rms_ref[i] = jnp.sum(ratio)
 
 
 def step_all(bands, tiles, proj_grad, blocks, rows, norm_params, norm_stat):
@@ -1455,7 +1485,7 @@
     block = lambda: vspec((1, kp, kp), lambda i: (jnp.maximum(i - count, 0), 0, 0))
     whole = lambda a: vspec(a.shape, lambda i: (0,) * len(a.shape))
     like = lambda a: jax.ShapeDtypeStruct(a.shape, F32)
-    rms = jax.ShapeDtypeStruct((2, 128), F32)
+    rms = jax.ShapeDtypeStruct((2,), F32)
     return pl.pallas_call(
         functools.partial(step_body, count),
         grid=(count + n_blocks,),
@@ -1466,7 +1496,7 @@
         out_specs=[tile() for _ in range(4)]
         + [block() for _ in range(3)]
         + [whole(norm_params)] * 3
-        + [whole(rms)],
+        + [pl.BlockSpec(memory_space=pltpu.SMEM)],
         out_shape=[like(tiles[0])] * 4 + [like(proj_grad)] * 3 + [like(norm_params)] * 3 + [rms],
         compiler_params=params(),
         cost_estimate=cost(1e9, 20e6),
@@ -1617,16 +1647,7 @@
 
     places, table, coef_back = tables(lengths, offsets, valid_count, blocks, rows_here)
 
-    def proj_rows(at):
-        col, n = places[0, at : at + blocks], places[1, at : at + blocks]
-        rows = jnp.stack(
-            [lax.dynamic_slice_in_dim(proj_all, col[b], SHORT, 0) for b in range(blocks)]
-        )
-        keep = lax.broadcasted_iota(jnp.int32, (blocks, SHORT, 1), 1) < n[:, None, None]
-        return jnp.where(keep, rows, jnp.zeros((), BF))
-
-    e_own = proj_rows(0)
-    e_peer = proj_rows(blocks)
+    e_own, e_peer = pick_rows(places, proj_all, blocks)
     n_own = places[1, :blocks]
 
     if fused:
@@ -1731,7 +1752,7 @@
             norm_grad,
             stat_new,
             norm_new,
-            rms,
+            residual_rms,
         ) = step_all(
             banded_grads,
             [stat_left, stat_right, root_left, root_right, weights],
@@ -1748,7 +1769,6 @@
             norm_stat,
         )
         proj_grad = proj_parts.reshape(part_rows, kp)
-        residual_rms = rms[:, 0]
     else:
         owned = scatter_weight_grads(
             jnp.concatenate([g_query, g_keyval, g_out], axis=0), g_up, g_down, per_dev, att_dev, both

time: 379 us -> 374 us (0.987)
  Pallas kernels: 340 us -> 350 us
  between operations: 22 us -> 14.2 us
  local copies, waits for them, and re-layouts: 8.77 us -> 4.49 us
    pallas_call x1, Pallas kernels: 54.2 us -> 64.2 us  [gather_bands(): pl.pallas_call(functools.partial(gather_body, depth, size // 2), in_specs...]
  transfers between devices with their start and end apart: 2 -> 2, of which waited for: 0 -> 0; matrix products, arithmetic and copies ran while one was open for 1% -> 0% of each run, Pallas kernels for 34% -> 37%
where the time goes in v8:
time: 374 us; the launch traced here: 371 us
  Pallas kernels  350 us (94%)
  between operations  14.2 us (4%)
  local copies, waits for them, and re-layouts  4.49 us (1%)
    pallas_call x1, Pallas kernels, reduce_all(): pl.pallas_call(functools.partial(reduce_body, depth, half, n_src, keep),...  88.7 us
    pallas_call x1, Pallas kernels, forward(): pl.pallas_call(functools.partial(forward_body, peers // 2, head), in_spec...  67.7 us
    pallas_call x1, Pallas kernels, gather_bands(): pl.pallas_call(functools.partial(gather_body, depth, size // 2), in_specs...  64.2 us
    pallas_call x1, Pallas kernels, backward(): pl.pallas_call(functools.partial(backward_body, peers, head, chunks), in_...  45.8 us
    pallas_call x1, Pallas kernels, feed(): pl.pallas_call(functools.partial(feed_body, chunks), grid=(rows // tile,)...  34.9 us
    pallas_call x1, Pallas kernels, step_all(): pl.pallas_call(functools.partial(step_body, count), grid=(count + n_block...  17.6 us
    pallas_call x1, Pallas kernels, back(): pl.pallas_call(functools.partial(back_body, width, blocks), grid_spec=plt...  17.3 us
  transfers between devices with their start and end apart: 2, of which 0 were waited for; matrix products, arithmetic and copies ran while one was open for 0% of the time, Pallas kernels for 37%

profile of v8, /device:TPU:9, one launch (start us, length us, event | category | flops | bytes accessed | tf_op | source)
XLA Modules:
  0.0 371.4 jit_solution(697409920980829894)
XLA Ops:
  7.2 0.0 copy-start.2
  7.2 0.0 all-gather.2.cloned.1.call-start
  7.2 2.6 make_bands.1
  9.8 0.0 all-gather.2.cloned.1.call-update
  9.9 0.0 copy-done.2
  9.9 1.3 collective-permute-start
  11.2 1.8 tables.1
  13.0 64.2 %gather_bands.1 = (bf16[4,2,2,2,96,768]{5,4,3,2,1,0:T(8,128)(2,1)}, bf16[2,2,512,256]{3,2,1,0:T(8,128)(2,1)}) custom-call(bf16[96,768]{1,0:T(8,128)(2,1)} %get-tuple-element.68.band_ref, bf16[512,256]{1,0:T(8,128)(2,1)} %get-tuple-element.69.proj_ref), custom_call_target="tpu_custom_call" | custom-call | flops 1000000000 | bytes 90000000 | tf_op jit(solution)/shard_map/gather_bands/pallas_call | solution.py:1387
  77.2 3.3 pick_rows.1
  80.6 0.0 collective-permute-done.px_ref
  80.6 1.1 copy-done.3
  81.7 67.7 %forward.1 = (bf16[1024,768]{1,0:T(8,128)(2,1)}, bf16[1024,1536]{1,0:T(8,128)(2,1)}, bf16[2,256,1536]{2,1,0:T(8,128)(2,1)}, bf16[1024,768]{1,0:T(8,128)(2,1)}, f32[1024,768]{1,0:T(8,128)}, /*index=5*/f32[3,768]{1,0:T(4,128)}) custom-call(f32[7,4]{1,0:T(8,128)} %get-tuple-element.66.c_ref, s32[2,4]{1,0:T(2,128)} %get-tuple-element.67.places_ref.n_ref, ...), custom_call_target="tpu_custom_call" | custom-call | flops 9663676416 | bytes 200000000 | tf_op jit(solution)/shard_map/forward/pallas_call | solution.py:479
  149.4 0.7 reshape.88
  150.1 34.9 %feed.1 = (bf16[1024,768]{1,0:T(8,128)(2,1)}, bf16[1024,3072]{1,0:T(8,128)(2,1)}, bf16[1024,3072]{1,0:T(8,128)(2,1)}, bf16[1024,768]{1,0:T(8,128)(2,1)}, bf16[10...) custom-call(f32[1024,768]{1,0:T(8,128)} %get-tuple-element.74.first_, ...), custom_call_target="tpu_custom_call" | custom-call | flops 19327352832 | bytes 30000000 | tf_op jit(solution)/shard_map/feed/pallas_call | solution.py:598
  185.0 45.8 %backward.1 = (bf16[1024,768]{1,0:T(8,128)(2,1)}, f32[2,256,1536]{2,1,0:T(8,128)}, bf16[256,1536]{1,0:T(8,128)(2,1)}, bf16[256,1536]{1,0:T(8,128)(2,1)}, bf16[25...) custom-call(f32[2,6]{1,0:T(2,128)} %get-tuple-element.77.c_ref, ...), custom_call_target="tpu_custom_call" | custom-call | flops 15300820992 | bytes 60000000 | tf_op jit(solution)/shard_map/backward/pallas_call | solution.py:902
  230.8 17.3 %back.1 = (bf16[1024,1536]{1,0:T(8,128)(2,1)}, f32[2048,256]{1,0:T(8,128)}, f32[1024,768]{1,0:T(8,128)}) custom-call(f32[2,6]{1,0:T(2,128)} %get-tuple-element.77.c_ref, s32[2,4]{1,0:T(2,128)} %get-tuple-element.67.places_ref.n_ref, bf16[2,512,256]{2,1,0:T(8,128)(2,1)} %get-tuple-element.72.e_ref, bf16[1024,1536]{1,0:T(8,128)(2,1)} %get-tuple-element.78.kv_ref, ...), custom_call_target="tpu_custom_call" | custom-call | flops 5234491392 | bytes 20000000 | tf_op jit(solution)/shard_map/back/pallas_call | solution.py:970
  248.2 1.8 copy.31
  249.9 0.0 copy-done.1
  250.0 5.8 %outer_keyval.1 = bf16[1536,768]{1,0:T(8,128)(2,1)} custom-call(bf16[1024,768]{1,0:T(8,128)(2,1)} %bitcast.42, bf16[1024,1536]{1,0:T(8,128)(2,1)} %get-tuple-element.99.r_ref), custom_call_target="tpu_custom_call" | custom-call | flops 2415919104 | bytes 20000000 | tf_op jit(solution)/shard_map/outer_keyval/pallas_call | solution.py:748
  255.8 1.6 pad_maximum_fusion.refs_5_
  257.5 88.7 %reduce_all.1 = (f32[3,96,768]{2,1,0:T(8,128)}, f32[4,2,64,256]{3,2,1,0:T(8,128)}, f32[2,2,4,2,8,256]{5,4,3,2,1,0:T(8,128)}) custom-call(bf16[2,4,2,2,96,768]{5,4,3,2,1,0:T(8,128)(2,1)} %bitcast.26, bf16[2,4,2,2,96,768]{5,4,3,2,1,0:T(8,128)(2,1)} %bitcast.25, bf16[4,2,96,768]{3,2,1,0:T(8,128)(2,1)} %bitcast.33, bf16[2,4,2,96,768]{4,3,2,1,0:T(8,128)(2,1)} %bitcast.27, ...), custom_call_target="tpu_custom_call" | custom-call | tf_op jit(solution)/shard_map/reduce_all/pallas_call | solution.py:1285
  346.2 0.0 copy-start
  346.2 17.6 %step_all.1 = (f32[24,96,96]{2,1,0:T(8,128)}, f32[24,96,96]{2,1,0:T(8,128)}, f32[24,96,96]{2,1,0:T(8,128)}, f32[24,96,96]{2,1,0:T(8,128)}, f32[2,256,256]{2,1,0:...) custom-call(f32[3,96,768]{2,1,0:T(8,128)} %get-tuple-element.104.ref, ...), custom_call_target="tpu_custom_call" | custom-call | flops 1000000000 | bytes 20000000 | tf_op jit(solution)/shard_map/step_all/pallas_call | solution.py:1489
  363.7 0.8 copy.33
  (8 shorter events, 0.1 us)
Async XLA Ops:
  7.2 2.7 copy-start.2
  7.2 142.9 %all-gather.2.cloned.1.call-start = ((), (), s32[]{:S(2)}) async-start(), calls=%async_computation | async-start | bytes 9732096 | tf_op jit(solution)/shard_map/all_gather | solution.py:1565
  9.9 70.7 %collective-permute-start = (bf16[1024,768]{1,0:T(8,128)(2,1)S(1)}, bf16[1024,768]{1,0:T(8,128)(2,1)S(1)}, u32[]{:S(2)}, u32[]{:S(2)}) collective-permute-start(bf16[1024,768]{1,0:T(8,128)(2,1)S(1)} %bitcast.43), channel_id=1, source_target_pairs={{0,4},{4,0},{8,12},{12,8},{16,20},{20,16},{24,28},{28,24},{1,5},{5... | collective-permute-start | bytes 4718600 | tf_op jit(solution)/shard_map/ppermute | solution.py:1641
  80.6 1.1 copy-start.3
  248.2 1.8 copy-start.1
  346.2 17.6 %copy-start = (f32[4,2,64,256]{3,2,1,0:T(8,128)S(1)}, f32[4,2,64,256]{3,2,1,0:T(8,128)}, u32[]{:S(2)}) copy-start(f32[4,2,64,256]{3,2,1,0:T(8,128)} %get-tuple-element.105) | copy-start | bytes 1572868
Sparse Core Ops, SparseCore 0:
  11.5 94.0 all-gather.1

commit v9 on v8

--- a/solution.py
+++ b/solution.py
@@ -925,11 +925,32 @@
     )(coef, q, summary, grad_mix, *operands)
 
 
-def back_body(
-    width, blocks, c_ref, n_ref, e_ref, kv_ref, p_ref, *refs
-):
+def pack_sums(out_ref, gp_ref, norm_ref, sums_ref):
+    depth, _, _, tall, kp = out_ref.shape
+    each = tall - 8
+    per = norm_ref.shape[1] // kp
+    rows = [(norm_ref, i, j) for i in range(4) for j in range(per)]
+    rows += [(sums_ref, i, j) for i in range(3) for j in range(per)]
+    top = lax.broadcasted_iota(jnp.int32, (8, kp), 0) == 0
+    for device in range(8 * depth):
+        z, y, x, c = device // 8, device // 4 % 2, device // 2 % 2, device % 2
+        at = ((2 * x + c) * 2 * depth + 2 * z + y) * each
+        out_ref[z, 2 * y + x, c, pl.ds(0, each), :] = gp_ref[pl.ds(at, each), :]
+        if device < len(rows):
+            ref, i, j = rows[device]
+            line = jnp.where(top, ref[pl.ds(i, 1), pl.ds(j * kp, kp)], 0.0)
+        else:
+            line = jnp.zeros((8, kp), F32)
+        out_ref[z, 2 * y + x, c, pl.ds(each, 8), :] = line
+
+
+def back_body(width, blocks, packed, c_ref, n_ref, e_ref, kv_ref, p_ref, *refs):
     far_refs = refs[:4]
-    dq_ref, w_ref, df_ref, dkv_ref, gp_ref, gi_ref = refs[4:]
+    dq_ref, w_ref, df_ref = refs[4:7]
+    if packed:
+        x_ref, norm_ref, sums_ref, gkv_ref, out_ref, gi_ref, gp_ref, acc_ref = refs[7:]
+    else:
+        dkv_ref, gp_ref, gi_ref = refs[7:]
     step = pl.program_id(0)
     short, kp = e_ref.shape[1], e_ref.shape[2]
     total = c_ref[step, 0] * p_ref[0]
@@ -939,7 +960,6 @@
         total = total + c_ref[step, blocks + k] * far_refs[k][...].astype(F32)
     summary = total.astype(BF)
     dkv = dot(e_ref[0], summary).astype(BF)
-    dkv_ref[...] = dkv
     keep = lax.broadcasted_iota(jnp.int32, (short, 1), 0) < n_ref[1, step]
     grad_e = jnp.where(keep, dot_t(kv_ref[...], summary), 0.0)
     column = n_ref[0, step]
@@ -959,16 +979,49 @@
         + dot_t(dkv[:, :width], w_ref[pl.ds(width, width), :])
         + dot_t(dkv[:, width:], w_ref[pl.ds(2 * width, width), :])
     )
-
-
-def back(coef, places, e_rows, kv, grad_parts, far_parts, dq, w_att, grad_first, positions):
+    if not packed:
+        dkv_ref[...] = dkv
+        return
+    for kind in range(2):
+        rows = pl.ds(kind * width, width)
+        value = dot_l(x_ref[...], dkv[:, kind * width : (kind + 1) * width])
+        value = value + jnp.where(step > 0, acc_ref[rows, :], 0.0)
+        acc_ref[rows, :] = value
+        gkv_ref[rows, :] = value.astype(BF)
+
+    @pl.when(step == blocks - 1)
+    def _():
+        pack_sums(out_ref, gp_ref, norm_ref, sums_ref)
+
+
+def back(coef, places, e_rows, kv, grad_parts, far_parts, dq, w_att, grad_first, positions, small=None, depth=0):
     rows, width = dq.shape
     blocks, short, kp = e_rows.shape
     row = lambda i, *_: (i, 0)
     lead = lambda i, *_: (i, 0, 0)
     fixed = lambda i, *_: (0, 0)
+    packed = small is not None
+    more_specs, scratch = [], []
+    if packed:
+        tall = positions // (8 * depth) + 8
+        more_specs = [
+            vspec((short, width), row),
+            vspec(small[1].shape, fixed),
+            vspec(small[2].shape, fixed),
+        ]
+        first_spec, second_spec = (
+            vspec((2 * width, width), fixed),
+            vspec((depth, 4, 2, tall, kp), lambda i, *_: (0,) * 5),
+        )
+        first_out = jax.ShapeDtypeStruct((2 * width, width), BF)
+        second_out = jax.ShapeDtypeStruct((depth, 4, 2, tall, kp), F32)
+        scratch = [pltpu.VMEM((positions, kp), F32), pltpu.VMEM((2 * width, width), F32)]
+    else:
+        first_spec, second_spec = vspec((short, 2 * width), row), vspec((positions, kp), fixed)
+        first_out = jax.ShapeDtypeStruct((rows, 2 * width), BF)
+        second_out = jax.ShapeDtypeStruct((positions, kp), F32)
     return pl.pallas_call(
-        functools.partial(back_body, width, blocks),
+        functools.partial(back_body, width, blocks, packed),
         grid_spec=pltpu.PrefetchScalarGridSpec(
             num_scalar_prefetch=2,
             grid=(blocks,),
@@ -982,22 +1035,16 @@
                 vspec((short, width), row),
                 vspec((3 * width, width), fixed, True),
                 vspec((short, width), row),
-            ],
-            out_specs=[
-                vspec((short, 2 * width), row),
-                vspec((positions, kp), fixed),
-                vspec((short, width), row),
-            ],
+            ]
+            + more_specs,
+            out_specs=[first_spec, second_spec, vspec((short, width), row)],
+            scratch_shapes=scratch,
         ),
-        out_shape=[
-            jax.ShapeDtypeStruct((rows, 2 * width), BF),
-            jax.ShapeDtypeStruct((positions, kp), F32),
-            jax.ShapeDtypeStruct((rows, width), F32),
-        ],
+        out_shape=[first_out, second_out, jax.ShapeDtypeStruct((rows, width), F32)],
         compiler_params=params(),
         cost_estimate=cost(2 * rows * width * (3 * width + 4 * kp), 20e6),
         name="back",
-    )(coef, places, e_rows, kv, grad_parts, *far_parts, dq, w_att, grad_first)
+    )(coef, places, e_rows, kv, grad_parts, *far_parts, dq, w_att, grad_first, *(small or ()))
 
 
 def reduce_body(depth, half, n_src, extra_keep, *refs):
@@ -1233,7 +1280,7 @@
     depth = peers // 2
     size, width = g_up.shape[2], g_up.shape[3]
     half = size // 2
-    e_rows_all, kp = extra.shape[1], extra.shape[2]
+    e_rows_all, kp = extra.shape[-2:]
     keep = e_rows_all - 8
     sources = (
         [
@@ -1245,7 +1292,7 @@
             g_keyval.reshape(2, 4, 2, size, width),
             g_out.reshape(4, 2, size, width),
         ]
-        + [extra.reshape(depth, 4, 2, e_rows_all, kp)]
+        + [extra]
     )
     n_src = len(sources)
     cols = width // 2
@@ -1299,7 +1346,7 @@
     )(*sources)
 
 
-def gather_body(depth, half, band_ref, proj_ref, out_ref, pout_ref, send, recv, local):
+def gather_body(depth, band_ref, proj_ref, out_ref, pout_ref, send, recv, local):
     seq, mine = lax.axis_index("seq"), lax.axis_index("own")
     z, y, x, c = seq // 2, seq % 2, mine // 2, mine % 2
     core = (seq, 2 * x + (1 - c))
@@ -1348,27 +1395,22 @@
         from_x.append(push(slab, slab, along_x))
         from_y.append(push(slab, slab, along_y))
         last.append(push(slab, slab, core))
-    low, high = pl.ds(0, half), pl.ds(half, half)
     cross = []
     for k in range(depth):
         plane = planes[k]
+        from_y[k].wait_recv()
+        slab = out_ref.at[plane, 1 - y, x, c]
+        cross.append(push(slab, slab, along_x))
+        last.append(push(slab, slab, core))
         from_x[k].wait_recv()
         slab = out_ref.at[plane, y, 1 - x, c]
-        part = out_ref.at[plane, y, 1 - x, c, low, :]
-        cross_y = push(part, part, along_y)
-        last.append(push(slab, slab, core))
-        from_y[k].wait_recv()
-        slab = out_ref.at[plane, 1 - y, x, c]
-        part = out_ref.at[plane, 1 - y, x, c, high, :]
-        cross.append((cross_y, push(part, part, along_x)))
         last.append(push(slab, slab, core))
         if k == 0:
             proj_x.wait_recv()
             slab = pout_ref.at[1 - x, c]
             last.append(push(slab, slab, core))
     for k in range(depth):
-        for copy in cross[k]:
-            copy.wait_recv()
+        cross[k].wait_recv()
         slab = out_ref.at[planes[k], 1 - y, 1 - x, c]
         last.append(push(slab, slab, core))
     for copy in last:
@@ -1382,10 +1424,10 @@
 def gather_bands(band, proj, peers):
     depth = peers // 2
     size, width = band.shape
-    messages = (depth - 1) + 3 + 2 + 3 * (depth - 1) + 4 * depth + 1 + depth
+    messages = (depth - 1) + 3 + 2 + 3 * (depth - 1) + 3 * depth + 1 + depth
     vmem = pl.BlockSpec(memory_space=pltpu.VMEM)
     return pl.pallas_call(
-        functools.partial(gather_body, depth, size // 2),
+        functools.partial(gather_body, depth),
         in_specs=[vmem] * 2,
         out_specs=[vmem] * 2,
         out_shape=[
@@ -1712,7 +1754,8 @@
         g_down = outer_rows(hidden, grad_down, gtype, "outer_down")
         g_out = outer_rows(mixed, grad_branch, gtype, "outer_out")
         g_query = outer_rows(x, grad_query, gtype, "outer_query")
-    grad_keyval, grad_proj, grad_input = back(
+    part_rows = projection.shape[0]
+    back_args = (
         coef_back,
         places,
         e_own,
@@ -1724,22 +1767,22 @@
         grad_first,
         proj_all.shape[0],
     )
-    g_keyval = outer_rows(x, grad_keyval, gtype, "outer_keyval")
-    part_rows = projection.shape[0]
-    if not fused:
+    if fused:
+        g_keyval, small_sums, grad_input = back(
+            *back_args, (x, norm_terms, row_sums), peers // 2
+        )
+    else:
+        grad_keyval, grad_proj, grad_input = back(*back_args)
+        g_keyval = outer_rows(x, grad_keyval, gtype, "outer_keyval")
         valid_here = jnp.sum(n_own).astype(F32)
         here = lax.broadcasted_iota(jnp.int32, (1, width), 1) == 0
         row_sums = jnp.concatenate([row_sums, jnp.where(here, valid_here, 0.0)], axis=0)
-    extra = jnp.concatenate([norm_terms.reshape(-1, kp), row_sums.reshape(-1, kp)], axis=0)
+        extra = jnp.concatenate([norm_terms.reshape(-1, kp), row_sums.reshape(-1, kp)], axis=0)
     n_norm = 4 * width // kp
     n_row = 2 * width // kp
     if fused:
-        extra = jnp.pad(extra, ((0, devices - extra.shape[0]), (0, 0)))[:, None, :]
-        extra = jnp.pad(extra, ((0, 0), (0, 7), (0, 0)))
-        shares = grad_proj.reshape(own_size, peers, part_rows // peers, kp).swapaxes(0, 1)
-        shares = shares.reshape(devices, part_rows // peers, kp)
         banded_grads, proj_parts, rows = reduce_all(
-            g_query, g_keyval, g_out, g_up, g_down, jnp.concatenate([shares, extra], axis=1), peers
+            g_query, g_keyval, g_out, g_up, g_down, small_sums, peers
         )
         (
             owned,

time: 374 us -> 368 us (0.984)
  Pallas kernels: 350 us -> 346 us
    pallas_call x3 -> x2, Pallas kernels: 87.4 us -> 83.3 us  [the longest x1 62.8 us: gather_bands(): pl.pallas_call(functools.partial(gather_body, depth), in_specs=[vmem] * 2...]
  transfers between devices with their start and end apart: 2 -> 2, of which waited for: 0 -> 0; matrix products, arithmetic and copies ran while one was open for 0% -> 0% of each run, Pallas kernels for 37% -> 38%
where the time goes in v9:
time: 368 us; the launch traced here: 363 us
  Pallas kernels  346 us (94%)
  between operations  14.1 us (4%)
    pallas_call x1, Pallas kernels, reduce_all(): pl.pallas_call(functools.partial(reduce_body, depth, half, n_src, keep),...  87.9 us
    pallas_call x1, Pallas kernels, forward(): pl.pallas_call(functools.partial(forward_body, peers // 2, head), in_spec...  68.3 us
    pallas_call x1, Pallas kernels, gather_bands(): pl.pallas_call(functools.partial(gather_body, depth), in_specs=[vmem] * 2...  62.8 us
    pallas_call x1, Pallas kernels, backward(): pl.pallas_call(functools.partial(backward_body, peers, head, chunks), in_...  45.8 us
    pallas_call x1, Pallas kernels, feed(): pl.pallas_call(functools.partial(feed_body, chunks), grid=(rows // tile,)...  34.9 us
    pallas_call x1, Pallas kernels, back(): pl.pallas_call(functools.partial(back_body, width, blocks, packed), grid_...  20.5 us
    pallas_call x1, Pallas kernels, step_all(): pl.pallas_call(functools.partial(step_body, count), grid=(count + n_block...  17.5 us
  transfers between devices with their start and end apart: 2, of which 0 were waited for; matrix products, arithmetic and copies ran while one was open for 0% of the time, Pallas kernels for 38%

profile of v9, /device:TPU:9, one launch (start us, length us, event | category | flops | bytes accessed | tf_op | source)
XLA Modules:
  0.0 363.0 jit_solution(13331530963615214689)
XLA Ops:
  7.2 0.0 copy-start.1
  7.2 0.0 all-gather.2.cloned.1.call-start
  7.2 2.6 make_bands.1
  9.8 0.0 all-gather.2.cloned.1.call-update
  9.9 0.0 copy-done.1
  9.9 1.3 collective-permute-start
  11.2 1.8 tables.1
  13.0 62.8 %gather_bands.1 = (bf16[4,2,2,2,96,768]{5,4,3,2,1,0:T(8,128)(2,1)}, bf16[2,2,512,256]{3,2,1,0:T(8,128)(2,1)}) custom-call(bf16[96,768]{1,0:T(8,128)(2,1)} %get-tuple-element.68.band_ref, bf16[512,256]{1,0:T(8,128)(2,1)} %get-tuple-element.69.proj_ref), custom_call_target="tpu_custom_call" | custom-call | flops 1000000000 | bytes 90000000 | tf_op jit(solution)/shard_map/gather_bands/pallas_call | solution.py:1429
  75.8 3.3 pick_rows.1
  79.1 0.0 collective-permute-done.px_ref
  79.1 0.0 copy-start.2
  79.1 1.1 copy-done.2
  80.3 68.3 %forward.1 = (bf16[1024,768]{1,0:T(8,128)(2,1)}, bf16[1024,1536]{1,0:T(8,128)(2,1)}, bf16[2,256,1536]{2,1,0:T(8,128)(2,1)}, bf16[1024,768]{1,0:T(8,128)(2,1)}, f32[1024,768]{1,0:T(8,128)}, /*index=5*/f32[3,768]{1,0:T(4,128)}) custom-call(f32[7,4]{1,0:T(8,128)} %get-tuple-element.66.c_ref, s32[2,4]{1,0:T(2,128)} %get-tuple-element.67.places_ref.n_ref, ...), custom_call_target="tpu_custom_call" | custom-call | flops 9663676416 | bytes 200000000 | tf_op jit(solution)/shard_map/forward/pallas_call | solution.py:479
  148.6 0.0 all-gather.2.cloned.1.call-done
  148.6 34.9 %feed.1 = (bf16[1024,768]{1,0:T(8,128)(2,1)}, bf16[1024,3072]{1,0:T(8,128)(2,1)}, bf16[1024,3072]{1,0:T(8,128)(2,1)}, bf16[1024,768]{1,0:T(8,128)(2,1)}, bf16[10...) custom-call(f32[1024,768]{1,0:T(8,128)} %get-tuple-element.74.first_, ...), custom_call_target="tpu_custom_call" | custom-call | flops 19327352832 | bytes 30000000 | tf_op jit(solution)/shard_map/feed/pallas_call | solution.py:598
  183.5 45.8 %backward.1 = (bf16[1024,768]{1,0:T(8,128)(2,1)}, f32[2,256,1536]{2,1,0:T(8,128)}, bf16[256,1536]{1,0:T(8,128)(2,1)}, bf16[256,1536]{1,0:T(8,128)(2,1)}, bf16[25...) custom-call(f32[2,6]{1,0:T(2,128)} %get-tuple-element.77.c_ref, ...), custom_call_target="tpu_custom_call" | custom-call | flops 15300820992 | bytes 60000000 | tf_op jit(solution)/shard_map/backward/pallas_call | solution.py:902
  229.4 20.5 %back.1 = (bf16[1536,768]{1,0:T(8,128)(2,1)}, f32[4,4,2,72,256]{4,3,2,1,0:T(8,128)}, f32[1024,768]{1,0:T(8,128)}) custom-call(f32[2,6]{1,0:T(2,128)} %get-tuple-element.77.c_ref, s32[2,4]{1,0:T(2,128)} %get-tuple-element.67.places_ref.n_ref, bf16[2,512,256]{2,1,0:T(8,128)(2,1)} %get-tuple-element.72.e_ref, bf16[1024,1536]{1,0:T(8,128)(2,1)} %get-tuple-element.78.kv_ref, ...), custom_call_target="tpu_custom_call" | custom-call | flops 5234491392 | bytes 20000000 | tf_op jit(solution)/shard_map/back/pallas_call | solution.py:1023
  249.9 87.9 %reduce_all.1 = (f32[3,96,768]{2,1,0:T(8,128)}, f32[4,2,64,256]{3,2,1,0:T(8,128)}, f32[2,2,4,2,8,256]{5,4,3,2,1,0:T(8,128)}) custom-call(bf16[2,4,2,2,96,768]{5,4,3,2,1,0:T(8,128)(2,1)} %bitcast.20, bf16[2,4,2,2,96,768]{5,4,3,2,1,0:T(8,128)(2,1)} %bitcast.19, bf16[4,2,96,768]{3,2,1,0:T(8,128)(2,1)} %bitcast.30, bf16[2,4,2,96,768]{4,3,2,1,0:T(8,128)(2,1)} %bitcast.21, ...), custom_call_target="tpu_custom_call" | custom-call | tf_op jit(solution)/shard_map/reduce_all/pallas_call | solution.py:1332
  337.8 0.0 copy-start
  337.8 17.5 %step_all.1 = (f32[24,96,96]{2,1,0:T(8,128)}, f32[24,96,96]{2,1,0:T(8,128)}, f32[24,96,96]{2,1,0:T(8,128)}, f32[24,96,96]{2,1,0:T(8,128)}, f32[2,256,256]{2,1,0:...) custom-call(f32[3,96,768]{2,1,0:T(8,128)} %get-tuple-element.104.ref, ...), custom_call_target="tpu_custom_call" | custom-call | flops 1000000000 | bytes 20000000 | tf_op jit(solution)/shard_map/step_all/pallas_call | solution.py:1531
  355.4 0.0 copy-done
  355.4 0.8 copy.32
Async XLA Ops:
  7.2 2.7 copy-start.1
  7.2 141.4 %all-gather.2.cloned.1.call-start = ((), (), s32[]{:S(2)}) async-start(), calls=%async_computation | async-start | bytes 9732096 | tf_op jit(solution)/shard_map/all_gather | solution.py:1607
  9.9 69.3 %collective-permute-start = (bf16[1024,768]{1,0:T(8,128)(2,1)S(1)}, bf16[1024,768]{1,0:T(8,128)(2,1)S(1)}, u32[]{:S(2)}, u32[]{:S(2)}) collective-permute-start(bf16[1024,768]{1,0:T(8,128)(2,1)S(1)} %bitcast.28), channel_id=1, source_target_pairs={{0,4},{4,0},{8,12},{12,8},{16,20},{20,16},{24,28},{28,24},{1,5},{5... | collective-permute-start | bytes 4718600 | tf_op jit(solution)/shard_map/ppermute | solution.py:1683
  79.1 1.1 copy-start.2
  337.8 17.6 %copy-start = (f32[4,2,64,256]{3,2,1,0:T(8,128)S(1)}, f32[4,2,64,256]{3,2,1,0:T(8,128)}, u32[]{:S(2)}) copy-start(f32[4,2,64,256]{3,2,1,0:T(8,128)} %get-tuple-element.105) | copy-start | bytes 1572868
Sparse Core Ops, SparseCore 0:
  11.5 96.1 all-gather.1
